TPU v7x, 128 devices: a whole 4x4x4 slice. The times are simulated.
128 devices in a mesh: row: 8 (over y, z_lo), col: 16 (over x, z_hi, core).
Axes of the slice: x: 4, y: 4, z: 4 (z_hi: 2, z_lo: 2; z = z_hi * 2 + z_lo), core: 2. Of those that a mesh axis runs over, the one named last changes fastest.
Arguments:
- tokens: bfloat16 [4096, 6144], P('row', 'col'), may hold values from -40 to 40
- ln_gain: float32 [6144], replicated, may hold values from 0.25 to 1.75
- w_qkv: bfloat16 [6144, 3, 4096], P('row', None, 'col'), may hold values from -0.078125 to 0.078125
- q_gain: float32 [128], replicated, may hold values from 0.1 to 1.9
- k_gain: float32 [128], replicated, may hold values from 0.1 to 1.9
- w_up: bfloat16 [6144, 12288], P('row', 'col'), may hold values from -0.078125 to 0.078125
- w_out: bfloat16 [4096, 6144], P('col', 'row'), may hold values from -0.5 to 0.5
- w_down: bfloat16 [12288, 6144], P('col', 'row'), may hold values from -0.078125 to 0.078125
Outputs:
- mixed: bfloat16 [4096, 6144], P('row', 'col')
All inputs are finite; a program needn't handle non-finite values.
Results may differ from a plain program's by a relative error of at most 0.017.
Values may be sent and summed in bfloat16 or wider, within the bound.
No kernel may reach another device: no remote copies, remote signals or barrier semaphores. Data moves between devices by JAX's collectives and lax.ppermute only.
A program may use at most 128 MiB of HBM per device.

v0:
```python
import math

import jax
import jax.numpy as jnp
from jax import lax
from jax.sharding import PartitionSpec as P

HD = 128
PATCHES = 256


epsilon = 1e-06


def layer_norm(values_in, gain_vec):
    x_float = values_in.astype(jnp.float32)
    centre = jnp.mean(x_float, axis=-1, keepdims=True)
    deviation = x_float - centre
    variance = jnp.mean(deviation * deviation, axis=-1, keepdims=True)
    return deviation * lax.rsqrt(variance + epsilon) * gain_vec


def attend(projected, q_gain, k_gain):
    tok_count = projected.shape[0]
    frame_count = tok_count // PATCHES
    arranged = projected.reshape(frame_count, PATCHES, 3, -1, HD)
    queries = layer_norm(arranged[:, :, 0], q_gain).astype(jnp.bfloat16)
    key_vecs = layer_norm(arranged[:, :, 1], k_gain).astype(jnp.bfloat16)
    value_vecs = arranged[:, :, 2].astype(jnp.bfloat16)
    scores = jnp.einsum(
        "fqhd,fkhd->fhqk", queries, key_vecs, preferred_element_type=jnp.float32
    ) / math.sqrt(HD)
    exponent = jnp.exp(scores)
    attn_probs = (exponent / jnp.sum(exponent, axis=-1, keepdims=True)).astype(jnp.bfloat16)
    attended = jnp.einsum(
        "fhqk,fkhd->fqhd", attn_probs, value_vecs, preferred_element_type=jnp.float32
    )
    return attended.astype(jnp.bfloat16).reshape(tok_count, -1)


def shards(tokens, ln_gain, w_qkv, q_gain, k_gain, w_up, w_out, w_down):
    gathered = lax.all_gather(tokens, "col", axis=1, tiled=True)
    normed = layer_norm(gathered, ln_gain).astype(jnp.bfloat16)

    def add_rows(weight_rows):
        flattened = weight_rows.reshape(weight_rows.shape[0], -1)
        return jnp.dot(normed, flattened, preferred_element_type=jnp.float32)

    weight_rows = (
        lax.all_gather(w_qkv, "row", axis=0, tiled=True),
        lax.all_gather(w_up, "row", axis=0, tiled=True),
    )
    projected = add_rows(weight_rows[0])
    pre_act = add_rows(weight_rows[1])
    attended = attend(projected, q_gain, k_gain)
    activated = jax.nn.gelu(pre_act, approximate=False).astype(jnp.bfloat16)
    column_block = jnp.dot(
        attended,
        lax.all_gather(w_out, "row", axis=1, tiled=True),
        preferred_element_type=jnp.float32,
    )
    column_block = column_block + jnp.dot(
        activated,
        lax.all_gather(w_down, "row", axis=1, tiled=True),
        preferred_element_type=jnp.float32,
    )
    summed = lax.psum_scatter(
        column_block.astype(jnp.bfloat16), "col", scatter_dimension=1, tiled=True
    ).astype(jnp.float32)
    return (tokens.astype(jnp.float32) + summed).astype(jnp.bfloat16)


def solution(mesh):
    in_specs = (
        P("row", "col"),
        P(),
        P("row", None, "col"),
        P(),
        P(),
        P("row", "col"),
        P("col", "row"),
        P("col", "row"),
    )
    out_specs = P("row", "col")
    return jax.shard_map(shards, mesh=mesh, in_specs=in_specs, out_specs=out_specs, check_vma=False)
```

profile of v0, /device:TPU:32, one launch (start us, length us, event | category | flops | bytes accessed | tf_op | source)
XLA Modules:
  0.0 847.0 jit_solution(13845213418589235404)
XLA Ops:
  6.5 0.7 all-gather.6.cloned.1.call-update
  7.3 2.4 copy.17
  9.8 0.7 all-gather.14.cloned.1.call-update
  10.5 0.5 all-gather.12.cloned.1.call-update
  11.1 0.5 all-gather.10.cloned.1.call-update
  11.7 68.6 %all-gather.6.cloned.1.call-done = bf16[512,6144]{1,0:T(8,128)(2,1)} async-done(((bf16[512,384]{1,0:T(8,128)(2,1)}), bf16[512,6144]{1,0:T(8,128)(2,1)}) %all-gather.6.cloned.1.call-update) | async-done | bytes 6291472 | tf_op jit(solution)/shard_map/all_gather | solution.py:42
  80.3 3.8 convert_reduce_fusion
  84.2 0.7 copy-done
  84.9 1.8 fusion.2
  86.7 6.3 fusion.4
  93.0 175.0 %all-gather.8.cloned.1.call-done = bf16[6144,3,256]{0,2,1:T(8,128)(2,1)} async-done(((bf16[768,3,256]{0,2,1:T(8,128)(2,1)}), bf16[6144,3,256]{0,2,1:T(8,128)(2,1)}) %all-gather.8.cloned.1.call-update) | async-done | bytes 9437200 | tf_op jit(solution)/shard_map/all_gather | solution.py:50
  268.0 9.5 %fusion.93 = f32[2,256,3,2,128]{1,4,3,2,0:T(8,128)S(1)} fusion(bf16[2,256,6144,1,1]{2,1,4,3,0:T(8,128)(2,1)} %bitcast.46, bf16[3,2,128,6144,1]{3,2,1,0,4:T(8,128)(2,1)} %bitcast.49), kind=kOutput, calls=%fused_computation.121 | convolution fusion | flops 4831838208 | bytes 17301504 | tf_op jit(solution)/shard_map/dot_general | solution.py:47
  277.9 0.4 copy-done.3
  278.2 0.4 fusion.15
  278.7 0.3 fusion.16
  279.2 181.6 %all-gather.14.cloned.1.call-done = bf16[768,6144]{1,0:T(8,128)(2,1)} async-done(((bf16[768,768]{1,0:T(8,128)(2,1)}), bf16[768,6144]{1,0:T(8,128)(2,1)}) %all-gather.14.cloned.1.call-update) | async-done | bytes 9437200 | tf_op jit(solution)/shard_map/all_gather | solution.py:64
  460.8 192.6 %all-gather.12.cloned.1.call-done = bf16[6144,768]{1,0:T(8,128)(2,1)} async-done(((bf16[768,768]{1,0:T(8,128)(2,1)}), bf16[6144,768]{1,0:T(8,128)(2,1)}) %all-gather.12.cloned.1.call-update) | async-done | bytes 9437200 | tf_op jit(solution)/shard_map/all_gather | solution.py:51
  653.5 26.3 %fusion.17 = f32[512,6144]{1,0:T(8,128)} fusion(bf16[768,6144]{1,0:T(8,128)(2,1)} %all-gather.14.cloned.1.call-done, bf16[512,6144]{1,0:T(8,128)(2,1)} %fusion.4, bf16[6144,768]{1,0:T(8,128)(2,1)} %all-gather.12.cloned.1.call-done), kind=kOutput, calls=%fused_computation.32 | convolution fusion | flops 9689235456 | bytes 37748736 | tf_op jit(solution)/shard_map/dot_general | solution.py:62
  679.8 49.2 %all-gather.10.cloned.1.call-done = bf16[256,6144]{1,0:T(8,128)(2,1)} async-done(((bf16[256,768]{1,0:T(8,128)(2,1)}), bf16[256,6144]{1,0:T(8,128)(2,1)}) %all-gather.10.cloned.1.call-update) | async-done | bytes 3145744 | tf_op jit(solution)/shard_map/all_gather | solution.py:59
  729.0 9.9 %add_convert_fusion = bf16[512,6144]{1,0:T(8,128)(2,1)} fusion(f32[512,6144]{1,0:T(8,128)} %fusion.17, bf16[256,6144]{1,0:T(8,128)(2,1)} %all-gather.10.cloned.1.call-done, bf16[64,8,2,128]{3,2,1,0:T(2,128)(2,1)S(1)} %bitcast.47), kind=kOutput, calls=%fused_computation.7 | convolution fusion | flops 1616904192 | bytes 22282240 | tf_op jit(solution)/shard_map/dot_general | solution.py:57
  739.0 8.7 %copy.26 = bf16[512,6144]{0,1:T(8,128)(2,1)} copy(bf16[512,6144]{1,0:T(8,128)(2,1)} %add_convert_fusion) | data formatting | bytes 12582912
  747.6 90.5 %reduce-scatter.4.cloned.1.call-done = bf16[384,512]{1,0:T(8,128)(2,1)} async-done(((bf16[6144,512]{1,0:T(8,128)(2,1)}), bf16[384,512]{1,0:T(8,128)(2,1)}) %reduce-scatter.4.cloned.1.call-update) | async-done | bytes 393232
  838.1 1.2 copy.27
  839.3 0.8 add_convert_fusion.1
  (24 shorter events, 0.7 us)
Async XLA Ops:
  6.5 73.8 %all-gather.6.cloned.1.call-start = ((), (), s32[]{:S(2)}) async-start(), calls=%async_computation.1 | async-start | bytes 6684672 | tf_op jit(solution)/shard_map/all_gather | solution.py:42
  7.3 260.8 %all-gather.8.cloned.1.call-start = ((), (), s32[]{:S(2)}) async-start(), calls=%async_computation.2 | async-start | bytes 10616832 | tf_op jit(solution)/shard_map/all_gather | solution.py:50
  9.7 451.1 %all-gather.14.cloned.1.call-start = ((), (), s32[]{:S(2)}) async-start(), calls=%async_computation.5 | async-start | bytes 10616832 | tf_op jit(solution)/shard_map/all_gather | solution.py:64
  10.5 643.0 %all-gather.12.cloned.1.call-start = ((), (), s32[]{:S(2)}) async-start(), calls=%async_computation.4 | async-start | bytes 10616832 | tf_op jit(solution)/shard_map/all_gather | solution.py:51
  11.0 718.0 %all-gather.10.cloned.1.call-start = ((), (), s32[]{:S(2)}) async-start(), calls=%async_computation.3 | async-start | bytes 3538944 | tf_op jit(solution)/shard_map/all_gather | solution.py:59
  11.6 826.5 %reduce-scatter.4.cloned.1.call-start = ((), (), s32[]{:S(2)}) async-start(), calls=%async_computation.6 | async-start | bytes 6684672
  80.3 4.6 copy-start
  84.9 1.8 copy-start.2
  277.6 0.7 copy-start.3
  277.6 0.7 copy-start.4
  747.6 91.7 %copy-start.1 = (bf16[512,384]{1,0:T(8,128)(2,1)S(1)}, bf16[512,384]{1,0:T(8,128)(2,1)}, u32[]{:S(2)}) copy-start(bf16[512,384]{1,0:T(8,128)(2,1)} %param.8) | copy-start | bytes 1179652
Sparse Core Ops, SparseCore 0:
  9.6 70.6 all-gather.5
  81.9 186.0 all-gather.7
  269.7 191.0 all-gather.13
  462.3 191.0 all-gather.11
  655.0 74.0 all-gather.9
  747.8 90.2 reduce-scatter.3
where the time goes:
time: 849 us; the launch traced here: 847 us
  waiting for transfers between devices  760 us (90%)
  matrix products  46.5 us (5%)
  local copies, waits for them, and re-layouts  13.6 us (2%)
  between operations  13.6 us (2%)
  other arithmetic  13 us (2%)
    all_gather x1, waiting for transfers between devices, shards(): lax.all_gather(w_up, 'row', axis=0, tiled=True)  193 us
    all_gather x1, waiting for transfers between devices, shards(): lax.all_gather(w_down, 'row', axis=1, tiled=True)  182 us
    all_gather x1, waiting for transfers between devices, shards(): lax.all_gather(w_qkv, 'row', axis=0, tiled=True)  175 us
    unnamed x7, waiting for transfers between devices  92.9 us
    all_gather x1, waiting for transfers between devices, shards(): gathered = lax.all_gather(tokens, 'col', axis=1, tiled=True)  68.6 us
    all_gather x1, waiting for transfers between devices, shards(): lax.all_gather(w_out, 'row', axis=1, tiled=True)  49.2 us
    dot_general x1, matrix products, shards(): jnp.dot(activated, lax.all_gather(w_down, 'row', axis=1, tiled=True), pre...  26.3 us
  transfers between devices with their start and end apart: 6, of which 6 were waited for; matrix products, arithmetic and copies ran while one was open for 6% of the time, Pallas kernels for 0%

commit v1 on v0

v1 whole, which is shorter than its diff:
```python
import functools
import math

import jax
import jax.numpy as jnp
from jax import lax
from jax.experimental import pallas as pl
from jax.experimental.pallas import tpu as pltpu
from jax.sharding import Mesh, PartitionSpec as P

HD = 128
PATCHES = 256
EPS = 1e-06
AXES = ("y", "l", "x", "h", "c")
SIZES = {"y": 4, "l": 2, "x": 4, "h": 2, "c": 2}
VMEM_LIMIT = 40 << 20
OFFSETS = (1, 3, 2, 0)


def shift(value, axis, by):
    size = SIZES[axis]
    return lax.ppermute(value, axis, [(i, (i + by) % size) for i in range(size)])


def move_z(value, pairs):
    place = lambda z: (z & 1) * 2 + (z >> 1)
    return lax.ppermute(value, ("l", "h"), [(place(s), place(d)) for s, d in pairs])


def norm_rows(value, gain):
    centre = jnp.mean(value, axis=-1, keepdims=True)
    deviation = value - centre
    variance = jnp.mean(deviation * deviation, axis=-1, keepdims=True)
    return deviation * lax.rsqrt(variance + EPS) * gain


def project_kernel(index, *refs):
    own, other = refs[0:4], refs[4:8]
    w_ref, mine_ref, theirs_ref, acc_ref = refs[8:]
    step = pl.program_id(0)
    core, slot = index[4], index[5]
    groups, width = w_ref.shape[1], w_ref.shape[-1]
    for j in range(4):

        @pl.when(step == j)
        def _():
            for g in range(groups):
                part = jnp.dot(
                    own[j][...].reshape(1024, 384), w_ref[0, g, core], preferred_element_type=jnp.float32
                )
                part += jnp.dot(
                    other[j][...].reshape(1024, 384), w_ref[0, g, 1 - core], preferred_element_type=jnp.float32
                )
                part = part.reshape(2, 512, width)
                cols = slice(g * width, (g + 1) * width)
                if j:
                    part += acc_ref[:, :, cols]
                acc_ref[:, :, cols] = part

    @pl.when(step == 3)
    def _():
        mine_ref[...] = acc_ref[slot]
        theirs_ref[...] = acc_ref[1 - slot].astype(jnp.bfloat16)


def project(index, own, other, weights):
    groups, width = weights.shape[1], weights.shape[-1]
    total = groups * width
    piece = pl.BlockSpec((2, 512, 384), lambda j, i: (0, 0, 0))
    whole = pl.BlockSpec((512, total), lambda j, i: (0, 0))
    return pl.pallas_call(
        project_kernel,
        out_shape=(
            jax.ShapeDtypeStruct((512, total), jnp.float32),
            jax.ShapeDtypeStruct((512, total), jnp.bfloat16),
        ),
        grid_spec=pltpu.PrefetchScalarGridSpec(
            num_scalar_prefetch=1,
            grid=(4,),
            in_specs=[piece] * 8
            + [pl.BlockSpec((1, groups, 2, 384, width), lambda j, i: (i[j], 0, 0, 0, 0))],
            out_specs=(whole, whole),
            scratch_shapes=[pltpu.VMEM((2, 512, total), jnp.float32)],
        ),
        compiler_params=pltpu.CompilerParams(vmem_limit_bytes=VMEM_LIMIT),
        cost_estimate=pl.CostEstimate(
            flops=2 * 1024 * 3072 * total, bytes_accessed=2 * 3072 * (1024 + total), transcendentals=0
        ),
    )(index, *own, *other, weights)


def attend_kernel(mine_ref, got_ref, q_gain_ref, k_gain_ref, out_ref):
    for frame in range(2):
        rows = slice(frame * PATCHES, (frame + 1) * PATCHES)
        for head in range(2):

            def part(which):
                cols = slice(which * 256 + head * HD, which * 256 + (head + 1) * HD)
                return mine_ref[rows, cols] + got_ref[rows, cols].astype(jnp.float32)

            queries = norm_rows(part(0), q_gain_ref[...]).astype(jnp.bfloat16)
            key_vecs = norm_rows(part(1), k_gain_ref[...]).astype(jnp.bfloat16)
            scores = lax.dot_general(
                queries, key_vecs, (((1,), (1,)), ((), ())), preferred_element_type=jnp.float32
            ) / math.sqrt(HD)
            exponent = jnp.exp(scores)
            probs = (exponent / jnp.sum(exponent, axis=-1, keepdims=True)).astype(jnp.bfloat16)
            out_ref[rows, head * HD : (head + 1) * HD] = jnp.dot(
                probs, part(2).astype(jnp.bfloat16), preferred_element_type=jnp.float32
            ).astype(jnp.bfloat16)


def attend(mine, got, q_gain, k_gain):
    return pl.pallas_call(
        attend_kernel,
        out_shape=jax.ShapeDtypeStruct((512, 256), jnp.bfloat16),
        compiler_params=pltpu.CompilerParams(vmem_limit_bytes=VMEM_LIMIT),
        cost_estimate=pl.CostEstimate(
            flops=4 * 4 * 256 * 256 * 128, bytes_accessed=512 * 768 * 6, transcendentals=4 * 256 * 256
        ),
    )(mine, got, q_gain.reshape(1, HD), k_gain.reshape(1, HD))


def output_kernel(index, att_own, att_other, act_own, act_other, w_out_ref, w_down_ref, *outs):
    keep, send = outs[0:4], outs[4:8]
    step = pl.program_id(0)
    core, slot = index[4], index[5]
    for j in range(4):

        @pl.when(step == j)
        def _():
            for att, act, place in ((att_own, act_own, slot), (att_other, act_other, 1 - slot)):
                for half, target in ((core, keep[j]), (1 - core, send[j])):
                    cols = pl.ds(pl.multiple_of(half * 384, 128), 384)
                    term = jnp.dot(att[...], w_out_ref[0, :, cols], preferred_element_type=jnp.float32)
                    term += jnp.dot(act[...], w_down_ref[0, :, cols], preferred_element_type=jnp.float32)
                    target[place] = term.astype(jnp.bfloat16)


def output_terms(index, att_own, att_other, act_own, act_other, w_out, w_down):
    whole = lambda *shape: pl.BlockSpec(shape, lambda j, i: (0,) * len(shape))
    return pl.pallas_call(
        output_kernel,
        out_shape=[jax.ShapeDtypeStruct((2, 512, 384), jnp.bfloat16)] * 8,
        grid_spec=pltpu.PrefetchScalarGridSpec(
            num_scalar_prefetch=1,
            grid=(4,),
            in_specs=[whole(512, 256), whole(512, 256), whole(512, 768), whole(512, 768)]
            + [pl.BlockSpec((1, k, 768), lambda j, i: (i[j], 0, 0)) for k in (256, 768)],
            out_specs=[whole(2, 512, 384)] * 8,
        ),
        compiler_params=pltpu.CompilerParams(vmem_limit_bytes=VMEM_LIMIT),
        cost_estimate=pl.CostEstimate(
            flops=2 * 1024 * 1024 * 3072, bytes_accessed=2 * 3072 * 2048, transcendentals=0
        ),
    )(index, att_own, att_other, act_own, act_other, w_out, w_down)


def shards(tokens, ln_gain, w_qkv, q_gain, k_gain, w_up, w_out, w_down):
    x, h, l, c = (lax.axis_index(a) for a in ("x", "h", "l", "c"))
    slot = jnp.where(l == h, 1, 0)
    index = jnp.stack([(x + o) % 4 for o in OFFSETS] + [c, slot]).astype(jnp.int32)

    qkv_all = lax.all_gather(w_qkv.transpose(1, 0, 2).reshape(3, 2, 384, 256), "y", axis=0)
    up_all = lax.all_gather(w_up.reshape(1, 2, 384, 768), "y", axis=0)
    out_all = lax.all_gather(w_out, "y", axis=0)
    down_all = lax.all_gather(w_down, "y", axis=0)

    local = tokens.astype(jnp.float32)
    mean = jnp.mean(local, axis=-1)
    deviation = local - mean[:, None]
    square = jnp.sum(deviation * deviation, axis=-1)
    stats = lax.all_gather(jnp.stack([mean, square]), ("x", "h", "c"), axis=0)
    centre = jnp.mean(stats[:, 0], axis=0)
    spread = jnp.sum(stats[:, 1] + 384 * (stats[:, 0] - centre) ** 2, axis=0) / 6144
    gain = lax.dynamic_slice(ln_gain, ((x * 4 + h * 2 + c) * 384,), (384,))
    normed = ((local - centre[:, None]) * lax.rsqrt(spread + EPS)[:, None] * gain).astype(jnp.bfloat16)

    block_a = move_z(normed, [(1, 0), (0, 2), (3, 1), (2, 3)])
    block_b = move_z(normed, [(0, 0), (1, 2), (2, 1), (3, 3)])
    held = jnp.stack([block_a, block_b])
    own = [shift(held, "x", -o) if o else held for o in OFFSETS]
    other = [shift(piece, "c", 1) for piece in own]

    qkv_mine, qkv_theirs = project(index, own, other, qkv_all)
    attended = attend(qkv_mine, shift(qkv_theirs, "l", 1), q_gain, k_gain)
    attended_other = shift(attended, "l", 1)

    up_mine, up_theirs = project(index, own, other, up_all)
    pre_act = up_mine + shift(up_theirs, "l", 1).astype(jnp.float32)
    activated = jax.nn.gelu(pre_act, approximate=False).astype(jnp.bfloat16)
    activated_other = shift(activated, "l", 1)

    outs = output_terms(index, attended, attended_other, activated, activated_other, out_all, down_all)
    summed = 0.0
    for j, o in enumerate(OFFSETS):
        pair = outs[j].astype(jnp.float32) + shift(outs[4 + j], "c", 1).astype(jnp.float32)
        if o:
            pair = shift(pair.astype(jnp.bfloat16), "x", o).astype(jnp.float32)
        summed = summed + pair
    block_a, block_b = summed[0].astype(jnp.bfloat16), summed[1].astype(jnp.bfloat16)
    got_a = move_z(block_a, [(0, 1), (2, 0), (1, 3), (3, 2)])
    got_b = move_z(block_b, [(0, 0), (2, 1), (1, 2), (3, 3)])
    return (local + got_a.astype(jnp.float32) + got_b.astype(jnp.float32)).astype(jnp.bfloat16)


def solution(mesh):
    fine = Mesh(mesh.devices.reshape(4, 2, 4, 2, 2), AXES)
    row, col = ("y", "l"), ("x", "h", "c")
    in_specs = (
        P(row, col),
        P(),
        P(row, None, col),
        P(),
        P(),
        P(row, col),
        P(col, row),
        P(col, row),
    )
    return jax.shard_map(shards, mesh=fine, in_specs=in_specs, out_specs=P(row, col), check_vma=False)
```

time: 849 us -> 278 us (0.33)
  waiting for transfers between devices: 760 us -> 168 us
  matrix products: 46.5 us -> 0 us
  Pallas kernels: 0 us -> 33.4 us
  blocking collectives: 0 us -> 24.3 us
  starting transfers between devices: 0.2 us -> 17.5 us
    all_gather x5 -> x4, waiting for transfers between devices: 667 us -> 50.9 us  [the longest x1 45.8 us: shards(): down_all = lax.all_gather(w_down, 'y', axis=0)]
    ppermute x0 -> x22, waiting for transfers between devices: none -> 114 us  [the longest x18 83.8 us: shift(): lax.ppermute(value, axis, [(i, (i + by) % size) for i in range(size)])]
    unnamed x7 -> x4, waiting for transfers between devices: 92.9 us -> 2.61 us
    dot_general x5 -> x0, matrix products: 46.5 us -> none  [the longest x1 26.3 us: shards(): jnp.dot(activated, lax.all_gather(w_down, 'row', axis=1, tiled=True), pre...]
    pallas_call x0 -> x4, Pallas kernels: none -> 33.4 us  [the longest x2 20.9 us: project(): pl.pallas_call(project_kernel, out_shape=(jax.ShapeDtypeStruct((512, tota...]
    all_gather x0 -> x1, blocking collectives: none -> 24.3 us  [shards(): stats = lax.all_gather(jnp.stack([mean, square]), ('x', 'h', 'c'), axis=0)]
    ppermute x0 -> x22, starting transfers between devices: none -> 17.4 us  [the longest x18 11.9 us: shift(): lax.ppermute(value, axis, [(i, (i + by) % size) for i in range(size)])]
  transfers between devices with their start and end apart: 6 -> 26, of which waited for: 6 -> 12; matrix products, arithmetic and copies ran while one was open for 6% -> 2% of each run, Pallas kernels for 0% -> 8%
where the time goes in v1:
time: 278 us; the launch traced here: 277 us
  waiting for transfers between devices  168 us (60%)
  Pallas kernels  33.4 us (12%)
  blocking collectives  24.3 us (9%)
  starting transfers between devices  17.5 us (6%)
  local copies, waits for them, and re-layouts  13.4 us (5%)
  between operations  13.3 us (5%)
  other arithmetic  7.43 us (3%)
    ppermute x18, waiting for transfers between devices, shift(): lax.ppermute(value, axis, [(i, (i + by) % size) for i in range(size)])  83.8 us
    all_gather x1, waiting for transfers between devices, shards(): down_all = lax.all_gather(w_down, 'y', axis=0)  45.8 us
    ppermute x4, waiting for transfers between devices, move_z(): lax.ppermute(value, ('l', 'h'), [(place(s), place(d)) for s, d in pairs])  30.4 us
    all_gather x1, blocking collectives, shards(): stats = lax.all_gather(jnp.stack([mean, square]), ('x', 'h', 'c'), axis=0)  24.3 us
    pallas_call x2, Pallas kernels, project(): pl.pallas_call(project_kernel, out_shape=(jax.ShapeDtypeStruct((512, tota...  20.9 us
    unnamed x24, local copies, waits for them, and re-layouts  12.4 us
    ppermute x18, starting transfers between devices, shift(): lax.ppermute(value, axis, [(i, (i + by) % size) for i in range(size)])  11.9 us
    pallas_call x1, Pallas kernels, output_terms(): pl.pallas_call(output_kernel, out_shape=[jax.ShapeDtypeStruct((2, 512, 38...  11.4 us
  transfers between devices with their start and end apart: 26, of which 12 were waited for; matrix products, arithmetic and copies ran while one was open for 2% of the time, Pallas kernels for 8%

profile of v1, /device:TPU:32, one launch (start us, length us, event | category | flops | bytes accessed | tf_op | source)
XLA Modules:
  0.0 277.0 jit_solution(3935045365149446475)
XLA Ops:
  10.5 24.3 %all-gather.3 = f32[16,2,512]{2,1,0:T(2,128)S(1)} all-gather(f32[1,2,512]{2,1,0:T(2,128)S(1)} %maximum_bitcast_fusion), channel_id=2, replica_groups=mesh['y'=4,'l'=2,'x'=4,'h'=2,'c'=2] {'x','h','c'}, dimensions={0}, use_global_device_ids=true | all-gather | bytes 69632 | tf_op jit(solution)/shard_map/all_gather | solution.py:173
  35.1 1.9 collective-permute-start.1
  37.1 19.7 %collective-permute-done.1 = bf16[512,384]{1,0:T(8,128)(2,1)S(1)} collective-permute-done((bf16[512,384]{1,0:T(8,128)(2,1)S(1)}, bf16[512,384]{1,0:T(8,128)(2,1)S(1)}, u32[]{:S(2)}, u32[]{:S(2)}) %collective-permute-start.1) | collective-permute-done | bytes 393248 | tf_op jit(solution)/shard_map/ppermute | solution.py:27
  57.0 2.0 collective-permute-start.3
  59.0 18.4 %collective-permute-done.2.refs_0_ = bf16[2,512,384]{2,1,0:T(8,128)(2,1)S(1)} collective-permute-done((bf16[2,512,384]{2,1,0:T(8,128)(2,1)S(1)}, bf16[2,512,384]{2,1,0:T(8,128)(2,1)S(1)}, u32[]{:S(2)}, u32[]{:S(2)}) %collective-permute-start.2) | collective-permute-done | bytes 786464 | tf_op jit(solution)/shard_map/ppermute | solution.py:22
  77.4 16.8 %collective-permute-done.3.refs_1_ = bf16[2,512,384]{2,1,0:T(8,128)(2,1)S(1)} collective-permute-done((bf16[2,512,384]{2,1,0:T(8,128)(2,1)S(1)}, bf16[2,512,384]{2,1,0:T(8,128)(2,1)S(1)}, u32[]{:S(2)}, u32[]{:S(2)}) %collective-permute-start.3) | collective-permute-done | bytes 786464 | tf_op jit(solution)/shard_map/ppermute | solution.py:22
  97.8 2.4 copy-done.3
  102.4 10.9 %shard_map.84 = (f32[512,768]{1,0:T(8,128)S(1)}, bf16[512,768]{1,0:T(8,128)(2,1)}) custom-call(s32[6]{0:T(128)S(1)} %stack.43.index, bf16[2,512,384]{2,1,0:T(8,128)(2,1)S(1)} %collective-permute-done.2.refs_0_, bf16[2,512,384]{2,1,0:T(8,128)(2,1)S(1)} %copy-done.6, bf16[2,512,384]{2,1,0:T(8,128)(2,1)S(1)} %copy-done.9, ...), custom_call_target="tpu_custom_call" | custom-call | flops 4831838208 | bytes 11010048 | tf_op jit(solution)/shard_map/pallas_call | solution.py:71
  113.3 5.1 %all-gather.9.cloned.1.call-done.refs_8_ = bf16[4,3,2,384,256]{4,3,2,1,0:T(8,128)(2,1)} async-done(((bf16[1,3,2,384,256]{4,3,2,1,0:T(8,128)(2,1)}), bf16[4,3,2,384,256]{4,3,2,1,0:T(8,128)(2,1)}) %all-gather.9.cloned.1.call-update) | async-done | bytes 4718608 | tf_op jit(solution)/shard_map/all_gather | solution.py:164
  118.4 2.3 copy-done.2
  123.0 9.9 %shard_map.82 = (f32[512,768]{1,0:T(8,128)S(1)}, bf16[512,768]{1,0:T(8,128)(2,1)S(1)}) custom-call(s32[6]{0:T(128)S(1)} %stack.43.index, bf16[2,512,384]{2,1,0:T(8,128)(2,1)S(1)} %collective-permute-done.2.refs_0_, bf16[2,512,384]{2,1,0:T(8,128)(2,1)S(1)} %copy-done.7, bf16[2,512,384]{2,1,0:T(8,128)(2,1)S(1)} %copy-done.10, ...), custom_call_target="tpu_custom_call" | custom-call | flops 4831838208 | bytes 11010048 | tf_op jit(solution)/shard_map/pallas_call | solution.py:71
  133.5 4.6 %fusion.2.act_own = bf16[512,768]{1,0:T(8,128)(2,1)S(1)} fusion(f32[512,768]{1,0:T(8,128)S(1)} %get-tuple-element.19, bf16[512,768]{1,0:T(8,128)(2,1)} %collective-permute-done.11), kind=kLoop, calls=%fused_computation.3 | loop fusion | flops 26345472 | bytes 3145728 | tf_op jit(solution)/shard_map/convert_element_type | solution.py:191
  138.1 1.6 collective-permute-start.12
  139.7 13.8 %collective-permute-done.9.got_ref = bf16[512,768]{1,0:T(8,128)(2,1)S(1)} collective-permute-done((bf16[512,768]{1,0:T(8,128)(2,1)S(1)}, bf16[512,768]{1,0:T(8,128)(2,1)S(1)}, u32[]{:S(2)}, u32[]{:S(2)}) %collective-permute-start.9) | collective-permute-done | bytes 786464 | tf_op jit(solution)/shard_map/ppermute | solution.py:22
  155.5 45.8 %all-gather.15.cloned.1.call-done = bf16[3072,768]{1,0:T(8,128)(2,1)} async-done(((bf16[768,768]{1,0:T(8,128)(2,1)}), bf16[3072,768]{1,0:T(8,128)(2,1)}) %all-gather.15.cloned.1.call-update) | async-done | bytes 4718608 | tf_op jit(solution)/shard_map/all_gather | solution.py:167
  201.3 1.4 copy-done.4
  202.7 11.4 %shard_map.85 = (bf16[2,512,384]{2,1,0:T(8,128)(2,1)S(1)}, bf16[2,512,384]{2,1,0:T(8,128)(2,1)S(1)}, bf16[2,512,384]{2,1,0:T(8,128)(2,1)S(1)}, bf16[2,512,384]{2...) custom-call(s32[6]{0:T(128)S(1)} %stack.43.index, ...), custom_call_target="tpu_custom_call" | custom-call | flops 6442450944 | bytes 12582912 | tf_op jit(solution)/shard_map/pallas_call | solution.py:142
  215.2 1.3 collective-permute-done.17
  216.7 3.1 %collective-permute-start.18 = (bf16[2,512,384]{2,1,0:T(8,128)(2,1)S(1)}, bf16[2,512,384]{2,1,0:T(8,128)(2,1)S(1)}, u32[]{:S(2)}, u32[]{:S(2)}) collective-permute-start(bf16[2,512,384]{2,1,0:T(8,128)(2,1)S(1)} %add_convert_fusion.1), channel_id=1, source_target_pairs={{0,8},{4,12},{8,0},{12,4},{1,9},{5,13},{9,1},{13,5},{2,10},{6,14},... | collective-permute-start | bytes 2359304 | tf_op jit(solution)/shard_map/ppermute | solution.py:22
  222.3 16.3 %collective-permute-done.18 = bf16[2,512,384]{2,1,0:T(8,128)(2,1)S(1)} collective-permute-done((bf16[2,512,384]{2,1,0:T(8,128)(2,1)S(1)}, bf16[2,512,384]{2,1,0:T(8,128)(2,1)S(1)}, u32[]{:S(2)}, u32[]{:S(2)}) %collective-permute-start.18) | collective-permute-done | bytes 786464 | tf_op jit(solution)/shard_map/ppermute | solution.py:22
  238.7 16.1 %collective-permute-done.16 = bf16[2,512,384]{2,1,0:T(8,128)(2,1)S(1)} collective-permute-done((bf16[2,512,384]{2,1,0:T(8,128)(2,1)S(1)}, bf16[2,512,384]{2,1,0:T(8,128)(2,1)S(1)}, u32[]{:S(2)}, u32[]{:S(2)}) %collective-permute-start.16) | collective-permute-done | bytes 786464 | tf_op jit(solution)/shard_map/ppermute | solution.py:22
  255.4 3.5 %collective-permute-start.21 = (bf16[512,384]{1,0:T(8,128)(2,1)S(1)}, bf16[512,384]{1,0:T(8,128)(2,1)S(1)}, u32[]{:S(2)}, u32[]{:S(2)}) collective-permute-start(bf16[512,384]{1,0:T(8,128)(2,1)S(1)} %get-tuple-element.30), channel_id=1, source_target_pairs={{0,0},{2,16},{16,2},{18,18},{1,1},{3,17},{17,3},{19,19},{4,4},{6,2... | collective-permute-start | bytes 1179656 | tf_op jit(solution)/shard_map/ppermute | solution.py:27
  258.9 9.3 %collective-permute-done.21 = bf16[512,384]{1,0:T(8,128)(2,1)S(1)} collective-permute-done((bf16[512,384]{1,0:T(8,128)(2,1)S(1)}, bf16[512,384]{1,0:T(8,128)(2,1)S(1)}, u32[]{:S(2)}, u32[]{:S(2)}) %collective-permute-start.21) | collective-permute-done | bytes 393248 | tf_op jit(solution)/shard_map/ppermute | solution.py:27
  268.2 1.4 collective-permute-done.20
  (80 shorter events, 20.6 us)
Async XLA Ops:
  6.5 91.2 %all-gather.11.cloned.1.call-start = ((), (), s32[]{:S(2)}) async-start(), calls=%async_computation.1 | async-start | bytes 5898240 | tf_op jit(solution)/shard_map/all_gather | solution.py:165
  7.3 111.2 %all-gather.9.cloned.1.call-start = ((), (), s32[]{:S(2)}) async-start(), calls=%async_computation | async-start | bytes 5898240 | tf_op jit(solution)/shard_map/all_gather | solution.py:164
  8.0 147.5 %all-gather.13.cloned.1.call-start = ((), (), s32[]{:S(2)}) async-start(), calls=%async_computation.2 | async-start | bytes 1966080 | tf_op jit(solution)/shard_map/all_gather | solution.py:166
  8.8 192.6 %all-gather.15.cloned.1.call-start = ((), (), s32[]{:S(2)}) async-start(), calls=%async_computation.3 | async-start | bytes 5898240 | tf_op jit(solution)/shard_map/all_gather | solution.py:167
  35.1 21.7 %collective-permute-start.1 = (bf16[512,384]{1,0:T(8,128)(2,1)S(1)}, bf16[512,384]{1,0:T(8,128)(2,1)S(1)}, u32[]{:S(2)}, u32[]{:S(2)}) collective-permute-start(bf16[512,384]{1,0:T(8,128)(2,1)S(1)} %fusion.14), channel_id=1, source_target_pairs={{0,0},{16,2},{2,16},{18,18},{1,1},{17,3},{3,17},{19,19},{4,4},{20,... | collective-permute-start | bytes 1179656 | tf_op jit(solution)/shard_map/ppermute | solution.py:27
  37.1 19.8 %collective-permute-start = (bf16[512,384]{1,0:T(8,128)(2,1)S(1)}, bf16[512,384]{1,0:T(8,128)(2,1)S(1)}, u32[]{:S(2)}, u32[]{:S(2)}) collective-permute-start(bf16[512,384]{1,0:T(8,128)(2,1)S(1)} %fusion.14), channel_id=1, source_target_pairs={{16,0},{0,2},{18,16},{2,18},{17,1},{1,3},{19,17},{3,19},{20,4},{4,... | collective-permute-start | bytes 1179656 | tf_op jit(solution)/shard_map/ppermute | solution.py:27
  56.9 20.5 %collective-permute-start.2 = (bf16[2,512,384]{2,1,0:T(8,128)(2,1)S(1)}, bf16[2,512,384]{2,1,0:T(8,128)(2,1)S(1)}, u32[]{:S(2)}, u32[]{:S(2)}) collective-permute-start(bf16[2,512,384]{2,1,0:T(8,128)(2,1)S(1)} %pad_maximum_fusion.refs_3_), channel_id=1, source_target_pairs={{0,12},{4,0},{8,4},{12,8},{1,13},{5,1},{9,5},{13,9},{2,14},{6,2},{... | collective-permute-start | bytes 2359304 | tf_op jit(solution)/shard_map/ppermute | solution.py:22
  57.0 37.2 %collective-permute-start.3 = (bf16[2,512,384]{2,1,0:T(8,128)(2,1)S(1)}, bf16[2,512,384]{2,1,0:T(8,128)(2,1)S(1)}, u32[]{:S(2)}, u32[]{:S(2)}) collective-permute-start(bf16[2,512,384]{2,1,0:T(8,128)(2,1)S(1)} %pad_maximum_fusion.refs_3_), channel_id=1, source_target_pairs={{0,4},{4,8},{8,12},{12,0},{1,5},{5,9},{9,13},{13,1},{2,6},{6,10},{... | collective-permute-start | bytes 2359304 | tf_op jit(solution)/shard_map/ppermute | solution.py:22
  59.0 36.1 %collective-permute-start.4 = (bf16[2,512,384]{2,1,0:T(8,128)(2,1)S(1)}, bf16[2,512,384]{2,1,0:T(8,128)(2,1)S(1)}, u32[]{:S(2)}, u32[]{:S(2)}) collective-permute-start(bf16[2,512,384]{2,1,0:T(8,128)(2,1)S(1)} %pad_maximum_fusion.refs_3_), channel_id=1, source_target_pairs={{0,8},{4,12},{8,0},{12,4},{1,9},{5,13},{9,1},{13,5},{2,10},{6,14},... | collective-permute-start | bytes 2359304 | tf_op jit(solution)/shard_map/ppermute | solution.py:22
  59.0 37.6 %collective-permute-start.8 = (bf16[2,512,384]{2,1,0:T(8,128)(2,1)S(1)}, bf16[2,512,384]{2,1,0:T(8,128)(2,1)}, u32[]{:S(2)}, u32[]{:S(2)}) collective-permute-start(bf16[2,512,384]{2,1,0:T(8,128)(2,1)S(1)} %pad_maximum_fusion.refs_3_), channel_id=1, source_target_pairs={{0,1},{1,0},{2,3},{3,2},{4,5},{5,4},{6,7},{7,6},{8,9},{9,8},{10,11... | collective-permute-start | bytes 2359304 | tf_op jit(solution)/shard_map/ppermute | solution.py:22
  77.4 19.2 %collective-permute-start.5 = (bf16[2,512,384]{2,1,0:T(8,128)(2,1)S(1)}, bf16[2,512,384]{2,1,0:T(8,128)(2,1)}, u32[]{:S(2)}, u32[]{:S(2)}) collective-permute-start(bf16[2,512,384]{2,1,0:T(8,128)(2,1)S(1)} %collective-permute-done.2.refs_0_), channel_id=1, source_target_pairs={{0,1},{1,0},{2,3},{3,2},{4,5},{5,4},{6,7},{7,6},{8,9},{9,8},{10,11... | collective-permute-start | bytes 2359304 | tf_op jit(solution)/shard_map/ppermute | solution.py:22
  95.1 2.6 collective-permute-start.7
  113.3 20.2 %collective-permute-start.11 = (bf16[512,768]{1,0:T(8,128)(2,1)}, bf16[512,768]{1,0:T(8,128)(2,1)}, u32[]{:S(2)}, u32[]{:S(2)}) collective-permute-start(bf16[512,768]{1,0:T(8,128)(2,1)} %get-tuple-element.20), channel_id=1, source_target_pairs={{0,16},{16,0},{1,17},{17,1},{2,18},{18,2},{3,19},{19,3},{4,20},{20... | collective-permute-start | bytes 2359304 | tf_op jit(solution)/shard_map/ppermute | solution.py:22
  133.0 20.5 %collective-permute-start.9 = (bf16[512,768]{1,0:T(8,128)(2,1)S(1)}, bf16[512,768]{1,0:T(8,128)(2,1)S(1)}, u32[]{:S(2)}, u32[]{:S(2)}) collective-permute-start(bf16[512,768]{1,0:T(8,128)(2,1)S(1)} %get-tuple-element.18), channel_id=1, source_target_pairs={{0,16},{16,0},{1,17},{17,1},{2,18},{18,2},{3,19},{19,3},{4,20},{20... | collective-permute-start | bytes 2359304 | tf_op jit(solution)/shard_map/ppermute | solution.py:22
  138.1 63.2 %collective-permute-start.12 = (bf16[512,768]{1,0:T(8,128)(2,1)S(1)}, bf16[512,768]{1,0:T(8,128)(2,1)S(1)}, u32[]{:S(2)}, u32[]{:S(2)}) collective-permute-start(bf16[512,768]{1,0:T(8,128)(2,1)S(1)} %fusion.2.act_own), channel_id=1, source_target_pairs={{0,16},{16,0},{1,17},{17,1},{2,18},{18,2},{3,19},{19,3},{4,20},{20... | collective-permute-start | bytes 2359304 | tf_op jit(solution)/shard_map/ppermute | solution.py:22
  154.7 46.6 %collective-permute-start.10 = (bf16[512,256]{1,0:T(8,128)(2,1)S(1)}, bf16[512,256]{1,0:T(8,128)(2,1)S(1)}, u32[]{:S(2)}, u32[]{:S(2)}) collective-permute-start(bf16[512,256]{1,0:T(8,128)(2,1)S(1)} %shard_map.83.att_own), channel_id=1, source_target_pairs={{0,16},{16,0},{1,17},{17,1},{2,18},{18,2},{3,19},{19,3},{4,20},{20... | collective-permute-start | bytes 786440 | tf_op jit(solution)/shard_map/ppermute | solution.py:22
  214.2 5.5 %collective-permute-start.15 = (bf16[2,512,384]{2,1,0:T(8,128)(2,1)S(1)}, bf16[2,512,384]{2,1,0:T(8,128)(2,1)S(1)}, u32[]{:S(2)}, u32[]{:S(2)}) collective-permute-start(bf16[2,512,384]{2,1,0:T(8,128)(2,1)S(1)} %get-tuple-element.24), channel_id=1, source_target_pairs={{0,1},{1,0},{2,3},{3,2},{4,5},{5,4},{6,7},{7,6},{8,9},{9,8},{10,11... | collective-permute-start | bytes 2359304 | tf_op jit(solution)/shard_map/ppermute | solution.py:22
  214.7 6.5 %collective-permute-start.13 = (bf16[2,512,384]{2,1,0:T(8,128)(2,1)S(1)}, bf16[2,512,384]{2,1,0:T(8,128)(2,1)S(1)}, u32[]{:S(2)}, u32[]{:S(2)}) collective-permute-start(bf16[2,512,384]{2,1,0:T(8,128)(2,1)S(1)} %get-tuple-element.22), channel_id=1, source_target_pairs={{0,1},{1,0},{2,3},{3,2},{4,5},{5,4},{6,7},{7,6},{8,9},{9,8},{10,11... | collective-permute-start | bytes 2359304 | tf_op jit(solution)/shard_map/ppermute | solution.py:22
  214.8 7.6 %collective-permute-start.19 = (bf16[2,512,384]{2,1,0:T(8,128)(2,1)S(1)}, bf16[2,512,384]{2,1,0:T(8,128)(2,1)S(1)}, u32[]{:S(2)}, u32[]{:S(2)}) collective-permute-start(bf16[2,512,384]{2,1,0:T(8,128)(2,1)S(1)} %get-tuple-element.28), channel_id=1, source_target_pairs={{0,1},{1,0},{2,3},{3,2},{4,5},{5,4},{6,7},{7,6},{8,9},{9,8},{10,11... | collective-permute-start | bytes 2359304 | tf_op jit(solution)/shard_map/ppermute | solution.py:22
  216.7 22.0 %collective-permute-start.18 = (bf16[2,512,384]{2,1,0:T(8,128)(2,1)S(1)}, bf16[2,512,384]{2,1,0:T(8,128)(2,1)S(1)}, u32[]{:S(2)}, u32[]{:S(2)}) collective-permute-start(bf16[2,512,384]{2,1,0:T(8,128)(2,1)S(1)} %add_convert_fusion.1), channel_id=1, source_target_pairs={{0,8},{4,12},{8,0},{12,4},{1,9},{5,13},{9,1},{13,5},{2,10},{6,14},... | collective-permute-start | bytes 2359304 | tf_op jit(solution)/shard_map/ppermute | solution.py:22
  220.0 34.8 %collective-permute-start.16 = (bf16[2,512,384]{2,1,0:T(8,128)(2,1)S(1)}, bf16[2,512,384]{2,1,0:T(8,128)(2,1)S(1)}, u32[]{:S(2)}, u32[]{:S(2)}) collective-permute-start(bf16[2,512,384]{2,1,0:T(8,128)(2,1)S(1)} %add_convert_fusion.2), channel_id=1, source_target_pairs={{0,12},{4,0},{8,4},{12,8},{1,13},{5,1},{9,5},{13,9},{2,14},{6,2},{... | collective-permute-start | bytes 2359304 | tf_op jit(solution)/shard_map/ppermute | solution.py:22
  221.4 33.4 %collective-permute-start.14 = (bf16[2,512,384]{2,1,0:T(8,128)(2,1)S(1)}, bf16[2,512,384]{2,1,0:T(8,128)(2,1)S(1)}, u32[]{:S(2)}, u32[]{:S(2)}) collective-permute-start(bf16[2,512,384]{2,1,0:T(8,128)(2,1)S(1)} %add_convert_fusion.3), channel_id=1, source_target_pairs={{0,4},{4,8},{8,12},{12,0},{1,5},{5,9},{9,13},{13,1},{2,6},{6,10},{... | collective-permute-start | bytes 2359304 | tf_op jit(solution)/shard_map/ppermute | solution.py:22
  255.4 12.9 %collective-permute-start.21 = (bf16[512,384]{1,0:T(8,128)(2,1)S(1)}, bf16[512,384]{1,0:T(8,128)(2,1)S(1)}, u32[]{:S(2)}, u32[]{:S(2)}) collective-permute-start(bf16[512,384]{1,0:T(8,128)(2,1)S(1)} %get-tuple-element.30), channel_id=1, source_target_pairs={{0,0},{2,16},{16,2},{18,18},{1,1},{3,17},{17,3},{19,19},{4,4},{6,2... | collective-permute-start | bytes 1179656 | tf_op jit(solution)/shard_map/ppermute | solution.py:27
  258.9 10.8 %collective-permute-start.20 = (bf16[512,384]{1,0:T(8,128)(2,1)S(1)}, bf16[512,384]{1,0:T(8,128)(2,1)S(1)}, u32[]{:S(2)}, u32[]{:S(2)}) collective-permute-start(bf16[512,384]{1,0:T(8,128)(2,1)S(1)} %get-tuple-element.29), channel_id=1, source_target_pairs={{0,16},{2,0},{16,18},{18,2},{1,17},{3,1},{17,19},{19,3},{4,20},{6,... | collective-permute-start | bytes 1179656 | tf_op jit(solution)/shard_map/ppermute | solution.py:27
  (14 other events, 60.0 us)
Sparse Core Ops, SparseCore 0:
  9.0 54.6 all-gather.10
  65.4 53.0 all-gather.8
  120.1 26.9 all-gather.12
  148.6 52.6 all-gather.14

commit v2 on v1

v2 whole, which is shorter than its diff:
```python
import functools
import math

import jax
import jax.numpy as jnp
from jax import lax
from jax.experimental import pallas as pl
from jax.experimental.pallas import tpu as pltpu
from jax.sharding import Mesh, PartitionSpec as P

HD = 128
PATCHES = 256
EPS = 1e-06
AXES = ("y", "l", "x", "h", "c")
SIZES = {"y": 4, "l": 2, "x": 4, "h": 2, "c": 2}
VMEM_LIMIT = 56 << 20
STEPS = (0, 1, 3, 2)
ROWS = 768


def shift(value, axis, by):
    size = SIZES[axis]
    return lax.ppermute(value, axis, [(i, (i + by) % size) for i in range(size)])


def move_z(value, pairs):
    place = lambda z: (z & 1) * 2 + (z >> 1)
    return lax.ppermute(value, ("l", "h"), [(place(s), place(d)) for s, d in pairs])


def norm_rows(value, gain):
    centre = jnp.mean(value, axis=-1, keepdims=True)
    deviation = value - centre
    variance = jnp.mean(deviation * deviation, axis=-1, keepdims=True)
    return deviation * lax.rsqrt(variance + EPS) * gain


def project_kernel(index, *refs):
    own, other, (centre, scale, gain, w_ref) = refs[0:5], refs[5:10], refs[10:14]
    sum_ref, sent_ref, block_ref = refs[14:]
    step, core = pl.program_id(0), index[2]
    for j in range(4):

        @pl.when(step == j)
        def _():
            for pieces, place in ((own, core), (other, 1 - core)):
                for t in range(2):
                    raw = pieces[3 + t][...] if j == 3 else pieces[j][t]
                    value = (raw.astype(jnp.float32) - centre[t]) * scale[t] * gain[0, 0, place]
                    block_ref[0, place, t * 512 : (t + 1) * 512] = value.astype(jnp.bfloat16)

    multiply(step, block_ref, w_ref, sum_ref)

    @pl.when(step == 3)
    def _():
        sent_ref[...] = sum_ref[...].astype(jnp.bfloat16)


def project_again_kernel(index, block_ref, w_ref, mine_ref, theirs_ref, acc_ref):
    step = pl.program_id(0)
    multiply(step, block_ref, w_ref, acc_ref)
    finish(step, index, acc_ref, mine_ref, theirs_ref)


def multiply(step, block_ref, w_ref, acc_ref):
    groups, width = w_ref.shape[1], w_ref.shape[-1]

    @pl.when(step == 0)
    def _():
        acc_ref[...] = jnp.zeros_like(acc_ref)

    for g in range(groups):
        cols = slice(g * width, (g + 1) * width)
        part = jnp.dot(block_ref[0, 0], w_ref[0, g, :384], preferred_element_type=jnp.float32)
        part += jnp.dot(block_ref[0, 1], w_ref[0, g, 384:], preferred_element_type=jnp.float32)
        acc_ref[:, :, cols] += part.reshape(2, 512, width)


def finish(step, index, acc_ref, mine_ref, theirs_ref):
    @pl.when(step == 3)
    def _():
        slot = index[1]
        mine_ref[...] = acc_ref[slot]
        theirs_ref[...] = acc_ref[1 - slot].astype(jnp.bfloat16)


def call(kernel, index, arrays, specs, outs, out_specs, scratch, flops):
    size = lambda a: math.prod(a.shape) * a.dtype.itemsize
    whole = lambda a: pl.BlockSpec(a.shape, lambda j, i, n=len(a.shape): (0,) * n)
    return pl.pallas_call(
        kernel,
        out_shape=outs,
        grid_spec=pltpu.PrefetchScalarGridSpec(
            num_scalar_prefetch=1,
            grid=(4,),
            in_specs=[spec or whole(a) for a, spec in zip(arrays, specs)],
            out_specs=[spec or whole(a) for a, spec in zip(outs, out_specs)],
            scratch_shapes=scratch,
        ),
        compiler_params=pltpu.CompilerParams(vmem_limit_bytes=VMEM_LIMIT),
        cost_estimate=pl.CostEstimate(
            flops=flops,
            bytes_accessed=sum(map(size, arrays)) + sum(map(size, outs)),
            transcendentals=0,
        ),
    )(index, *arrays)


def order(j):
    return j + (j == 2) * 1 - (j == 3) * 1


def by_block(which, *shape):
    return pl.BlockSpec((1, *shape), lambda j, i: ((i[which] + order(j)) % 4,) + (0,) * len(shape))


PARTS = [jax.ShapeDtypeStruct((512, ROWS), t) for t in (jnp.float32, jnp.bfloat16)]
SUMS = [pltpu.VMEM((2, 512, ROWS), jnp.float32)]
BY_STEP = pl.BlockSpec((1, 2, 1024, 384), lambda j, i: (j, 0, 0, 0))


def project(index, own, other, centre, scale, gain, weights):
    return call(
        project_kernel,
        index,
        [*own, *other, centre, scale, gain, weights],
        [None] * 12
        + [pl.BlockSpec((1, 1, 2, 1, 384), lambda j, i: ((i[3] + order(j)) % 4, i[5], 0, 0, 0))]
        + [by_block(3, *weights.shape[1:])],
        [
            jax.ShapeDtypeStruct((2, 512, ROWS), jnp.float32),
            jax.ShapeDtypeStruct((2, 512, ROWS), jnp.bfloat16),
            jax.ShapeDtypeStruct((4, 2, 1024, 384), jnp.bfloat16),
        ],
        [None, None, BY_STEP],
        [],
        2 * 1024 * 3072 * ROWS,
    )


def project_again(index, features, weights):
    return call(
        project_again_kernel,
        index,
        [features, weights],
        [BY_STEP, by_block(3, *weights.shape[1:])],
        PARTS,
        [None, None],
        SUMS,
        2 * 1024 * 3072 * ROWS,
    )


def attend_kernel(mine_ref, got_ref, q_gain_ref, k_gain_ref, out_ref):
    for frame in range(2):
        rows = slice(frame * PATCHES, (frame + 1) * PATCHES)
        for head in range(2):

            def part(which):
                cols = slice(which * 256 + head * HD, which * 256 + (head + 1) * HD)
                return mine_ref[rows, cols] + got_ref[rows, cols].astype(jnp.float32)

            queries = norm_rows(part(0), q_gain_ref[...]).astype(jnp.bfloat16)
            key_vecs = norm_rows(part(1), k_gain_ref[...]).astype(jnp.bfloat16)
            scores = lax.dot_general(
                queries, key_vecs, (((1,), (1,)), ((), ())), preferred_element_type=jnp.float32
            ) / math.sqrt(HD)
            exponent = jnp.exp(scores)
            probs = (exponent / jnp.sum(exponent, axis=-1, keepdims=True)).astype(jnp.bfloat16)
            out_ref[rows, head * HD : (head + 1) * HD] = jnp.dot(
                probs, part(2).astype(jnp.bfloat16), preferred_element_type=jnp.float32
            ).astype(jnp.bfloat16)


def attend(mine, got, q_gain, k_gain):
    return pl.pallas_call(
        attend_kernel,
        out_shape=jax.ShapeDtypeStruct((512, 256), jnp.bfloat16),
        compiler_params=pltpu.CompilerParams(vmem_limit_bytes=VMEM_LIMIT),
        cost_estimate=pl.CostEstimate(
            flops=4 * 4 * 256 * 256 * 128, bytes_accessed=512 * 768 * 6, transcendentals=4 * 256 * 256
        ),
    )(mine, got, q_gain.reshape(1, HD), k_gain.reshape(1, HD))


def output_kernel(block, index, att_own, att_other, act_ref, w_out_ref, *refs):
    pieces, (keep_ref, send_ref) = refs[:5], refs[5:]
    step, first = pl.program_id(0), index[2] == 0

    def terms(*rows):
        att = jnp.where(index[1] == block, att_own[...], att_other[...])
        term = jnp.dot(att, w_out_ref[0], preferred_element_type=jnp.float32)
        start = 0
        for right in rows:
            stop = start + right.shape[0]
            term += jnp.dot(act_ref[0, :, start:stop], right[...], preferred_element_type=jnp.float32)
            start = stop
        term = term.astype(jnp.bfloat16)
        keep_ref[0] = jnp.where(first, term[:, :384], term[:, 384:])
        send_ref[0] = jnp.where(first, term[:, 384:], term[:, :384])

    for j in range(4):
        pl.when(step == j)(lambda: terms(*(pieces[3:] if j == 3 else [pieces[j]])))


def output_terms(index, block, att_own, att_other, activated, w_out, w_down):
    out = jax.ShapeDtypeStruct((4, 512, 384), jnp.bfloat16)
    out_spec = pl.BlockSpec((1, 512, 384), lambda j, i: ((i[4] + order(j)) % 4, 0, 0))
    return call(
        functools.partial(output_kernel, block),
        index,
        [att_own, att_other, activated, w_out, *w_down],
        [None, None, pl.BlockSpec((1, 512, ROWS), lambda j, i: (block, 0, 0)), by_block(0, 256, ROWS)]
        + [None] * 5,
        [out, out],
        [out_spec, out_spec],
        [],
        2 * 512 * 1024 * 4 * ROWS,
    )


def after(value, *others):
    return lax.optimization_barrier((value, *others))[0]


def ring(block, axis, halves, ready=lambda *v: v):
    after, before = ready(shift(block, axis, -1), shift(block, axis, 1))
    return block, after, before, shift(halves(before)[0], axis, 1), shift(halves(after)[1], axis, -1)


def moments(piece):
    value = piece.astype(jnp.float32)
    mean = jnp.mean(value, axis=-1)
    return mean, jnp.sum((value - mean[..., None]) ** 2, axis=-1)


def merge(stats, count):
    means = [s[0] for s in stats]
    centre = 0.25 * (means[0] + means[1] + means[2] + means[3])
    total = stats[0][1] + stats[1][1] + stats[2][1] + stats[3][1]
    for m in means:
        total = total + count * (m - centre) ** 2
    return centre, total


def shards(tokens, ln_gain, w_qkv, q_gain, k_gain, w_up, w_out, w_down):
    y, x, h, l, c = (lax.axis_index(a) for a in ("y", "x", "h", "l", "c"))
    slot = jnp.where(l == h, 1, 0)
    index = jnp.stack([y, slot, c, x, (y - x + 4) % 4, l]).astype(jnp.int32)

    up_all = lax.all_gather(w_up[None], "y", axis=0)
    qkv_all = lax.all_gather(w_qkv.transpose(1, 0, 2), "y", axis=0)

    block_a = move_z(tokens, [(1, 0), (0, 2), (3, 1), (2, 3)])
    block_b = move_z(tokens, [(0, 0), (1, 2), (2, 1), (3, 3)])
    own = ring(jnp.stack([block_a, block_b]), "x", lambda v: (v[0], v[1]))
    other = [shift(piece, "c", 1) for piece in own]

    parts = [moments(piece) for piece in own]
    last = [jnp.stack([a, b]) for a, b in zip(parts[3], parts[4])]
    stats = jnp.stack(merge([*parts[:3], last], 384))
    cross = lax.ppermute(stats, ("l", "c"), [(i, 3 - i) for i in range(4)])
    centre, spread = merge([stats, shift(stats, "c", 1), shift(stats, "l", 1), cross], 1536)
    centre, scale = lax.optimization_barrier((centre, lax.rsqrt(spread / 6144 + EPS)))
    gain = ln_gain.reshape(4, 2, 2, 1, 384)

    up_sum, up_sent, features = project(
        index, own, other, centre[..., None], scale[..., None], gain, up_all
    )
    pre_act = up_sum + shift(up_sent, "l", 1).astype(jnp.float32)
    activated = jax.nn.gelu(pre_act, approximate=False).astype(jnp.bfloat16)

    qkv_mine, qkv_theirs = project_again(index, features, qkv_all)

    out_all = lax.all_gather(after(w_out, qkv_all), "y", axis=0)
    w_down = after(w_down, qkv_all)
    after_w, before_w = shift(w_down, "y", -1), shift(w_down, "y", 1)
    forward = before_w[:384], after_w[384:]
    down = w_down, after_w, before_w, shift(forward[0], "y", 1), shift(forward[1], "y", -1)

    got = after(shift(qkv_theirs, "l", 1), activated, *forward)
    attended = attend(qkv_mine, got, q_gain, k_gain)
    attended_other = shift(attended, "l", 1)

    def start_terms(block):
        keep, send = output_terms(
            index, block, attended, attended_other, activated, out_all, down
        )
        return keep, shift(send, "c", 1)

    def start_sums(keep, got):
        pair = [keep[o].astype(jnp.float32) + got[o].astype(jnp.float32) for o in range(4)]
        return pair[0], [shift(pair[o].astype(jnp.bfloat16), "x", o) for o in (2, 1, 3)]

    def finish_sums(summed, got, pairs):
        for g in got:
            summed = summed + g.astype(jnp.float32)
        return move_z(summed.astype(jnp.bfloat16), pairs).astype(jnp.float32)

    keep_a, got_a = start_terms(0)
    keep_b, got_b = start_terms(1)
    sum_a, sent_a = start_sums(keep_a, got_a)
    sum_b, sent_b = start_sums(keep_b, got_b)
    part_a = finish_sums(sum_a, sent_a, [(0, 1), (2, 0), (1, 3), (3, 2)])
    part_b = finish_sums(sum_b, sent_b, [(0, 0), (2, 1), (1, 2), (3, 3)])
    return (tokens.astype(jnp.float32) + part_a + part_b).astype(jnp.bfloat16)


def solution(mesh):
    fine = Mesh(mesh.devices.reshape(4, 2, 4, 2, 2), AXES)
    row, col = ("y", "l"), ("x", "h", "c")
    in_specs = (
        P(row, col),
        P(),
        P(row, None, col),
        P(),
        P(),
        P(row, col),
        P(col, row),
        P(col, row),
    )
    return jax.shard_map(shards, mesh=fine, in_specs=in_specs, out_specs=P(row, col), check_vma=False)
```

time: 278 us -> 263 us (0.946)
  waiting for transfers between devices: 168 us -> 140 us
  blocking collectives: 24.3 us -> 0 us
  starting transfers between devices: 17.5 us -> 38.6 us
  Pallas kernels: 33.4 us -> 51 us
  local copies, waits for them, and re-layouts: 13.4 us -> 5.88 us
  other arithmetic: 7.43 us -> 12.9 us
    all_gather x1 -> x0, blocking collectives: 24.3 us -> none  [shards(): stats = lax.all_gather(jnp.stack([mean, square]), ('x', 'h', 'c'), axis=0)]
    all_gather x4 -> x3, waiting for transfers between devices: 50.9 us -> 29.9 us  [the longest x1 29.8 us: shards(): qkv_all = lax.all_gather(w_qkv.transpose(1, 0, 2), 'y', axis=0)]
    pallas_call x3 -> x4, Pallas kernels: 32.2 us -> 47.4 us  [call(): pl.pallas_call(kernel, out_shape=outs, grid_spec=pltpu.PrefetchScalarGrid...]
    ppermute x18 -> x26, starting transfers between devices: 11.9 us -> 26.5 us  [shift(): lax.ppermute(value, axis, [(i, (i + by) % size) for i in range(size)])]
    unnamed x24, local copies, waits for them, and re-layouts: 12.4 us -> 1.61 us
    ppermute x4, starting transfers between devices: 5.53 us -> 11.3 us  [move_z(): lax.ppermute(value, ('l', 'h'), [(place(s), place(d)) for s, d in pairs])]
    ppermute x4, waiting for transfers between devices: 30.4 us -> 24.9 us  [move_z(): lax.ppermute(value, ('l', 'h'), [(place(s), place(d)) for s, d in pairs])]
    convert_element_type x1, other arithmetic: 4.56 us -> 7.82 us  [shards(): activated = jax.nn.gelu(pre_act, approximate=False).astype(jnp.bfloat16)]
  transfers between devices with their start and end apart: 26 -> 34, of which waited for: 12 -> 16; matrix products, arithmetic and copies ran while one was open for 2% -> 6% of each run, Pallas kernels for 8% -> 16%
where the time goes in v2:
time: 263 us; the launch traced here: 262 us
  waiting for transfers between devices  140 us (53%)
  Pallas kernels  51 us (19%)
  starting transfers between devices  38.6 us (15%)
  between operations  13.4 us (5%)
  other arithmetic  12.9 us (5%)
  local copies, waits for them, and re-layouts  5.88 us (2%)
    ppermute x26, waiting for transfers between devices, shift(): lax.ppermute(value, axis, [(i, (i + by) % size) for i in range(size)])  83.7 us
    pallas_call x4, Pallas kernels, call(): pl.pallas_call(kernel, out_shape=outs, grid_spec=pltpu.PrefetchScalarGrid...  47.4 us
    all_gather x1, waiting for transfers between devices, shards(): qkv_all = lax.all_gather(w_qkv.transpose(1, 0, 2), 'y', axis=0)  29.8 us
    ppermute x26, starting transfers between devices, shift(): lax.ppermute(value, axis, [(i, (i + by) % size) for i in range(size)])  26.5 us
    ppermute x4, waiting for transfers between devices, move_z(): lax.ppermute(value, ('l', 'h'), [(place(s), place(d)) for s, d in pairs])  24.9 us
    ppermute x4, starting transfers between devices, move_z(): lax.ppermute(value, ('l', 'h'), [(place(s), place(d)) for s, d in pairs])  11.3 us
    convert_element_type x1, other arithmetic, shards(): activated = jax.nn.gelu(pre_act, approximate=False).astype(jnp.bfloat16)  7.82 us
  transfers between devices with their start and end apart: 34, of which 16 were waited for; matrix products, arithmetic and copies ran while one was open for 6% of the time, Pallas kernels for 16%

profile of v2, /device:TPU:32, one launch (start us, length us, event | category | flops | bytes accessed | tf_op | source)
XLA Modules:
  0.0 262.1 jit_solution(17585834116287578817)
XLA Ops:
  8.1 5.4 %collective-permute-start.1 = (bf16[512,384]{1,0:T(8,128)(2,1)}, bf16[512,384]{1,0:T(8,128)(2,1)S(1)}, u32[]{:S(2)}, u32[]{:S(2)}) collective-permute-start(bf16[512,384]{1,0:T(8,128)(2,1)} %param.8), channel_id=1, source_target_pairs={{0,0},{16,2},{2,16},{18,18},{1,1},{17,3},{3,17},{19,19},{4,4},{20,... | collective-permute-start | bytes 1179656 | tf_op jit(solution)/shard_map/ppermute | solution.py:28
  13.6 7.2 %collective-permute-done = bf16[512,384]{1,0:T(8,128)(2,1)S(1)} collective-permute-done((bf16[512,384]{1,0:T(8,128)(2,1)}, bf16[512,384]{1,0:T(8,128)(2,1)S(1)}, u32[]{:S(2)}, u32[]{:S(2)}) %collective-permute-start) | collective-permute-done | bytes 393248 | tf_op jit(solution)/shard_map/ppermute | solution.py:28
  20.8 8.3 %collective-permute-done.1 = bf16[512,384]{1,0:T(8,128)(2,1)S(1)} collective-permute-done((bf16[512,384]{1,0:T(8,128)(2,1)}, bf16[512,384]{1,0:T(8,128)(2,1)S(1)}, u32[]{:S(2)}, u32[]{:S(2)}) %collective-permute-start.1) | collective-permute-done | bytes 393248 | tf_op jit(solution)/shard_map/ppermute | solution.py:28
  33.2 16.8 %collective-permute-done.3.refs_2_ = bf16[2,512,384]{2,1,0:T(8,128)(2,1)S(1)} collective-permute-done((bf16[2,512,384]{2,1,0:T(8,128)(2,1)S(1)}, bf16[2,512,384]{2,1,0:T(8,128)(2,1)S(1)}, u32[]{:S(2)}, u32[]{:S(2)}) %collective-permute-start.3) | collective-permute-done | bytes 786464 | tf_op jit(solution)/shard_map/ppermute | solution.py:23
  50.5 3.0 %collective-permute-start.5 = (bf16[512,384]{1,0:T(8,128)(2,1)S(1)}, bf16[512,384]{1,0:T(8,128)(2,1)S(1)}, u32[]{:S(2)}, u32[]{:S(2)}) collective-permute-start(bf16[512,384]{1,0:T(8,128)(2,1)S(1)} %slice_bitcast_fusion), channel_id=1, source_target_pairs={{0,12},{4,0},{8,4},{12,8},{1,13},{5,1},{9,5},{13,9},{2,14},{6,2},{... | collective-permute-start | bytes 1179656 | tf_op jit(solution)/shard_map/ppermute | solution.py:23
  55.5 6.3 %collective-permute-done.4.refs_3_ = bf16[512,384]{1,0:T(8,128)(2,1)S(1)} collective-permute-done((bf16[512,384]{1,0:T(8,128)(2,1)S(1)}, bf16[512,384]{1,0:T(8,128)(2,1)S(1)}, u32[]{:S(2)}, u32[]{:S(2)}) %collective-permute-start.4) | collective-permute-done | bytes 393248 | tf_op jit(solution)/shard_map/ppermute | solution.py:23
  70.1 17.5 %shard_map.82 = (f32[2,512,768]{2,1,0:T(8,128)}, bf16[2,512,768]{2,1,0:T(8,128)(2,1)}, bf16[4,2,1024,384]{3,2,1,0:T(8,128)(2,1)}) custom-call(s32[6]{0:T(128)} %stack.67.index, bf16[2,512,384]{2,1,0:T(8,128)(2,1)} %copy-done.7, bf16[2,512,384]{2,1,0:T(8,128)(2,1)} %copy-done.1, bf16[2,512,384]{2,1,0:T(8,128)(2,1)} %copy-done, bf16[512,384]{1,0:T(8,128)(2,1)} %copy-done.5, ...), custom_call_target="tpu_custom_call" | custom-call | flops 4831838208 | bytes 22052864 | tf_op jit(solution)/shard_map/pallas_call | solution.py:90
  88.6 29.8 %all-gather.9.cloned.1.call-done = bf16[12,768,256]{2,1,0:T(8,128)(2,1)} async-done(((bf16[3,768,256]{2,1,0:T(8,128)(2,1)}), bf16[12,768,256]{2,1,0:T(8,128)(2,1)}) %all-gather.9.cloned.1.call-update) | async-done | bytes 4718608 | tf_op jit(solution)/shard_map/all_gather | solution.py:252
  121.7 11.7 %shard_map.83 = (f32[512,768]{1,0:T(8,128)}, bf16[512,768]{1,0:T(8,128)(2,1)}) custom-call(s32[6]{0:T(128)} %stack.67.index, bf16[4,2,1024,384]{3,2,1,0:T(8,128)(2,1)} %get-tuple-element.21.block_ref, bf16[4,3,768,256]{3,2,1,0:T(8,128)(2,1)} %bitcast.168), custom_call_target="tpu_custom_call" | custom-call | flops 4831838208 | bytes 13369344 | tf_op jit(solution)/shard_map/pallas_call | solution.py:90
  133.9 26.3 %collective-permute-done.16.refs_2_ = bf16[768,768]{1,0:T(8,128)(2,1)S(1)} collective-permute-done((bf16[768,768]{1,0:T(8,128)(2,1)}, bf16[768,768]{1,0:T(8,128)(2,1)S(1)}, u32[]{:S(2)}, u32[]{:S(2)}) %collective-permute-start.16) | collective-permute-done | bytes 1179680 | tf_op jit(solution)/shard_map/ppermute | solution.py:23
  161.8 3.2 %collective-permute-start.20 = (bf16[384,768]{1,0:T(8,128)(2,1)S(1)}, bf16[384,768]{1,0:T(8,128)(2,1)}, u32[]{:S(2)}, u32[]{:S(2)}) collective-permute-start(bf16[384,768]{1,0:T(8,128)(2,1)S(1)} %slice.113), channel_id=1, source_target_pairs={{0,96},{32,0},{64,32},{96,64},{1,97},{33,1},{65,33},{97,65},{2,98}... | collective-permute-start | bytes 1769480 | tf_op jit(solution)/shard_map/ppermute | solution.py:23
  165.0 7.8 %fusion.2.act_ref = bf16[2,512,768]{2,1,0:T(8,128)(2,1)} fusion(f32[2,512,768]{2,1,0:T(8,128)S(1)} %copy-done.2, bf16[2,512,768]{2,1,0:T(8,128)(2,1)S(1)} %collective-permute-done.15), kind=kLoop, calls=%fused_computation.3 | loop fusion | flops 52690944 | bytes 6291456 | tf_op jit(solution)/shard_map/convert_element_type | solution.py:271
  173.7 3.6 %shard_map.84.att_own = bf16[512,256]{1,0:T(8,128)(2,1)} custom-call(f32[512,768]{1,0:T(8,128)} %get-tuple-element.22.mine_ref, bf16[512,768]{1,0:T(8,128)(2,1)} %copy-done.8, f32[1,128]{1,0:T(1,128)} %bitcast.166, f32[1,128]{1,0:T(1,128)} %bitcast.167), custom_call_target="tpu_custom_call" | custom-call | flops 134217728 | bytes 2359296 | tf_op jit(solution)/shard_map/pallas_call | solution.py:176
  177.7 6.1 %collective-permute-done.18.att_other = bf16[512,256]{1,0:T(8,128)(2,1)S(1)} collective-permute-done((bf16[512,256]{1,0:T(8,128)(2,1)}, bf16[512,256]{1,0:T(8,128)(2,1)S(1)}, u32[]{:S(2)}, u32[]{:S(2)}) %collective-permute-start.18) | collective-permute-done | bytes 262176 | tf_op jit(solution)/shard_map/ppermute | solution.py:23
  184.5 9.0 %shard_map.85 = (bf16[4,512,384]{2,1,0:T(8,128)(2,1)}, bf16[4,512,384]{2,1,0:T(8,128)(2,1)}) custom-call(s32[6]{0:T(128)} %stack.67.index, bf16[512,256]{1,0:T(8,128)(2,1)} %shard_map.84.att_own, bf16[512,256]{1,0:T(8,128)(2,1)} %copy-done.11, bf16[2,512,768]{2,1,0:T(8,128)(2,1)} %fusion.2.act_ref, bf16[4,256,768]{2,1,0:T(8,128)(2,1)} %bitcast.170, ...), custom_call_target="tpu_custom_call" | custom-call | flops 3221225472 | bytes 11534336 | tf_op jit(solution)/shard_map/pallas_call | solution.py:90
  193.6 9.2 %shard_map.86 = (bf16[4,512,384]{2,1,0:T(8,128)(2,1)}, bf16[4,512,384]{2,1,0:T(8,128)(2,1)}) custom-call(s32[6]{0:T(128)} %stack.67.index, bf16[512,256]{1,0:T(8,128)(2,1)} %shard_map.84.att_own, bf16[512,256]{1,0:T(8,128)(2,1)} %copy-done.11, bf16[2,512,768]{2,1,0:T(8,128)(2,1)} %fusion.2.act_ref, bf16[4,256,768]{2,1,0:T(8,128)(2,1)} %bitcast.171, ...), custom_call_target="tpu_custom_call" | custom-call | flops 3221225472 | bytes 11534336 | tf_op jit(solution)/shard_map/pallas_call | solution.py:90
  203.5 3.1 %collective-permute-start.22 = (bf16[512,384]{1,0:T(8,128)(2,1)S(1)}, bf16[512,384]{1,0:T(8,128)(2,1)S(1)}, u32[]{:S(2)}, u32[]{:S(2)}) collective-permute-start(bf16[512,384]{1,0:T(8,128)(2,1)S(1)} %get-tuple-element.35), channel_id=1, source_target_pairs={{0,8},{4,12},{8,0},{12,4},{1,9},{5,13},{9,1},{13,5},{2,10},{6,14},... | collective-permute-start | bytes 1179656 | tf_op jit(solution)/shard_map/ppermute | solution.py:23
  211.0 6.0 %collective-permute-done.22 = bf16[512,384]{1,0:T(8,128)(2,1)S(1)} collective-permute-done((bf16[512,384]{1,0:T(8,128)(2,1)S(1)}, bf16[512,384]{1,0:T(8,128)(2,1)S(1)}, u32[]{:S(2)}, u32[]{:S(2)}) %collective-permute-start.22) | collective-permute-done | bytes 393248 | tf_op jit(solution)/shard_map/ppermute | solution.py:23
  217.1 2.7 %collective-permute-start.29 = (bf16[512,384]{1,0:T(8,128)(2,1)S(1)}, bf16[512,384]{1,0:T(8,128)(2,1)S(1)}, u32[]{:S(2)}, u32[]{:S(2)}) collective-permute-start(bf16[512,384]{1,0:T(8,128)(2,1)S(1)} %get-tuple-element.39), channel_id=1, source_target_pairs={{0,12},{4,0},{8,4},{12,8},{1,13},{5,1},{9,5},{13,9},{2,14},{6,2},{... | collective-permute-start | bytes 1179656 | tf_op jit(solution)/shard_map/ppermute | solution.py:23
  219.8 5.8 %collective-permute-done.23 = bf16[512,384]{1,0:T(8,128)(2,1)S(1)} collective-permute-done((bf16[512,384]{1,0:T(8,128)(2,1)S(1)}, bf16[512,384]{1,0:T(8,128)(2,1)S(1)}, u32[]{:S(2)}, u32[]{:S(2)}) %collective-permute-start.23) | collective-permute-done | bytes 393248 | tf_op jit(solution)/shard_map/ppermute | solution.py:23
  228.2 5.8 %collective-permute-done.27 = bf16[512,384]{1,0:T(8,128)(2,1)S(1)} collective-permute-done((bf16[512,384]{1,0:T(8,128)(2,1)S(1)}, bf16[512,384]{1,0:T(8,128)(2,1)S(1)}, u32[]{:S(2)}, u32[]{:S(2)}) %collective-permute-start.27) | collective-permute-done | bytes 393248 | tf_op jit(solution)/shard_map/ppermute | solution.py:23
  234.0 7.6 %collective-permute-done.28 = bf16[512,384]{1,0:T(8,128)(2,1)S(1)} collective-permute-done((bf16[512,384]{1,0:T(8,128)(2,1)S(1)}, bf16[512,384]{1,0:T(8,128)(2,1)S(1)}, u32[]{:S(2)}, u32[]{:S(2)}) %collective-permute-start.28) | collective-permute-done | bytes 393248 | tf_op jit(solution)/shard_map/ppermute | solution.py:23
  241.9 3.5 %collective-permute-start.30 = (bf16[512,384]{1,0:T(8,128)(2,1)S(1)}, bf16[512,384]{1,0:T(8,128)(2,1)S(1)}, u32[]{:S(2)}, u32[]{:S(2)}) collective-permute-start(bf16[512,384]{1,0:T(8,128)(2,1)S(1)} %fusion.22), channel_id=1, source_target_pairs={{0,0},{2,16},{16,2},{18,18},{1,1},{3,17},{17,3},{19,19},{4,4},{6,2... | collective-permute-start | bytes 1179656 | tf_op jit(solution)/shard_map/ppermute | solution.py:28
  245.4 9.3 %collective-permute-done.30 = bf16[512,384]{1,0:T(8,128)(2,1)S(1)} collective-permute-done((bf16[512,384]{1,0:T(8,128)(2,1)S(1)}, bf16[512,384]{1,0:T(8,128)(2,1)S(1)}, u32[]{:S(2)}, u32[]{:S(2)}) %collective-permute-start.30) | collective-permute-done | bytes 393248 | tf_op jit(solution)/shard_map/ppermute | solution.py:28
  (108 shorter events, 33.7 us)
Async XLA Ops:
  6.5 63.5 %all-gather.7.cloned.1.call-start = ((), (), s32[]{:S(2)}) async-start(), calls=%async_computation | async-start | bytes 5898240 | tf_op jit(solution)/shard_map/all_gather | solution.py:251
  7.3 111.2 %all-gather.9.cloned.1.call-start = ((), (), s32[]{:S(2)}) async-start(), calls=%async_computation.1 | async-start | bytes 5898240 | tf_op jit(solution)/shard_map/all_gather | solution.py:252
  8.0 175.8 %all-gather.11.cloned.1.call-start = ((), (), s32[]{:S(2)}) async-start(), calls=%async_computation.2 | async-start | bytes 1966080 | tf_op jit(solution)/shard_map/all_gather | solution.py:275
  8.1 12.7 %collective-permute-start = (bf16[512,384]{1,0:T(8,128)(2,1)}, bf16[512,384]{1,0:T(8,128)(2,1)S(1)}, u32[]{:S(2)}, u32[]{:S(2)}) collective-permute-start(bf16[512,384]{1,0:T(8,128)(2,1)} %param.8), channel_id=1, source_target_pairs={{16,0},{0,2},{18,16},{2,18},{17,1},{1,3},{19,17},{3,19},{20,4},{4,... | collective-permute-start | bytes 1179656 | tf_op jit(solution)/shard_map/ppermute | solution.py:28
  8.1 21.0 %collective-permute-start.1 = (bf16[512,384]{1,0:T(8,128)(2,1)}, bf16[512,384]{1,0:T(8,128)(2,1)S(1)}, u32[]{:S(2)}, u32[]{:S(2)}) collective-permute-start(bf16[512,384]{1,0:T(8,128)(2,1)} %param.8), channel_id=1, source_target_pairs={{0,0},{16,2},{2,16},{18,18},{1,1},{17,3},{3,17},{19,19},{4,4},{20,... | collective-permute-start | bytes 1179656 | tf_op jit(solution)/shard_map/ppermute | solution.py:28
  29.2 20.8 %collective-permute-start.3 = (bf16[2,512,384]{2,1,0:T(8,128)(2,1)S(1)}, bf16[2,512,384]{2,1,0:T(8,128)(2,1)S(1)}, u32[]{:S(2)}, u32[]{:S(2)}) collective-permute-start(bf16[2,512,384]{2,1,0:T(8,128)(2,1)S(1)} %pad_maximum_fusion.refs_0_), channel_id=1, source_target_pairs={{0,4},{4,8},{8,12},{12,0},{1,5},{5,9},{9,13},{13,1},{2,6},{6,10},{... | collective-permute-start | bytes 2359304 | tf_op jit(solution)/shard_map/ppermute | solution.py:23
  30.8 19.7 %collective-permute-start.2 = (bf16[2,512,384]{2,1,0:T(8,128)(2,1)S(1)}, bf16[2,512,384]{2,1,0:T(8,128)(2,1)S(1)}, u32[]{:S(2)}, u32[]{:S(2)}) collective-permute-start(bf16[2,512,384]{2,1,0:T(8,128)(2,1)S(1)} %pad_maximum_fusion.refs_0_), channel_id=1, source_target_pairs={{0,12},{4,0},{8,4},{12,8},{1,13},{5,1},{9,5},{13,9},{2,14},{6,2},{... | collective-permute-start | bytes 2359304 | tf_op jit(solution)/shard_map/ppermute | solution.py:23
  32.5 37.5 %collective-permute-start.6 = (bf16[2,512,384]{2,1,0:T(8,128)(2,1)S(1)}, bf16[2,512,384]{2,1,0:T(8,128)(2,1)}, u32[]{:S(2)}, u32[]{:S(2)}) collective-permute-start(bf16[2,512,384]{2,1,0:T(8,128)(2,1)S(1)} %pad_maximum_fusion.refs_0_), channel_id=1, source_target_pairs={{0,1},{1,0},{2,3},{3,2},{4,5},{5,4},{6,7},{7,6},{8,9},{9,8},{10,11... | collective-permute-start | bytes 2359304 | tf_op jit(solution)/shard_map/ppermute | solution.py:23
  54.0 16.0 %collective-permute-start.7 = (bf16[2,512,384]{2,1,0:T(8,128)(2,1)S(1)}, bf16[2,512,384]{2,1,0:T(8,128)(2,1)}, u32[]{:S(2)}, u32[]{:S(2)}) collective-permute-start(bf16[2,512,384]{2,1,0:T(8,128)(2,1)S(1)} %collective-permute-done.2.refs_1_), channel_id=1, source_target_pairs={{0,1},{1,0},{2,3},{3,2},{4,5},{5,4},{6,7},{7,6},{8,9},{9,8},{10,11... | collective-permute-start | bytes 2359304 | tf_op jit(solution)/shard_map/ppermute | solution.py:23
  54.1 15.9 %collective-permute-start.8 = (bf16[2,512,384]{2,1,0:T(8,128)(2,1)S(1)}, bf16[2,512,384]{2,1,0:T(8,128)(2,1)}, u32[]{:S(2)}, u32[]{:S(2)}) collective-permute-start(bf16[2,512,384]{2,1,0:T(8,128)(2,1)S(1)} %collective-permute-done.3.refs_2_), channel_id=1, source_target_pairs={{0,1},{1,0},{2,3},{3,2},{4,5},{5,4},{6,7},{7,6},{8,9},{9,8},{10,11... | collective-permute-start | bytes 2359304 | tf_op jit(solution)/shard_map/ppermute | solution.py:23
  87.6 77.4 %collective-permute-start.15 = (bf16[2,512,768]{2,1,0:T(8,128)(2,1)}, bf16[2,512,768]{2,1,0:T(8,128)(2,1)S(1)}, u32[]{:S(2)}, u32[]{:S(2)}) collective-permute-start(bf16[2,512,768]{2,1,0:T(8,128)(2,1)} %get-tuple-element.25), channel_id=1, source_target_pairs={{0,16},{16,0},{1,17},{17,1},{2,18},{18,2},{3,19},{19,3},{4,20},{20... | collective-permute-start | bytes 4718600 | tf_op jit(solution)/shard_map/ppermute | solution.py:23
  118.4 41.8 %collective-permute-start.16 = (bf16[768,768]{1,0:T(8,128)(2,1)}, bf16[768,768]{1,0:T(8,128)(2,1)S(1)}, u32[]{:S(2)}, u32[]{:S(2)}) collective-permute-start(bf16[768,768]{1,0:T(8,128)(2,1)} %refs_0_.1), channel_id=1, source_target_pairs={{0,32},{32,64},{64,96},{96,0},{1,33},{33,65},{65,97},{97,1},{2,34}... | collective-permute-start | bytes 3538952 | tf_op jit(solution)/shard_map/ppermute | solution.py:23
  119.4 41.0 %collective-permute-start.17 = (bf16[768,768]{1,0:T(8,128)(2,1)}, bf16[768,768]{1,0:T(8,128)(2,1)}, u32[]{:S(2)}, u32[]{:S(2)}) collective-permute-start(bf16[768,768]{1,0:T(8,128)(2,1)} %refs_0_.1), channel_id=1, source_target_pairs={{0,96},{32,0},{64,32},{96,64},{1,97},{33,1},{65,33},{97,65},{2,98}... | collective-permute-start | bytes 3538952 | tf_op jit(solution)/shard_map/ppermute | solution.py:23
  133.5 39.3 %collective-permute-start.14 = (bf16[512,768]{1,0:T(8,128)(2,1)}, bf16[512,768]{1,0:T(8,128)(2,1)S(1)}, u32[]{:S(2)}, u32[]{:S(2)}) collective-permute-start(bf16[512,768]{1,0:T(8,128)(2,1)} %get-tuple-element.23), channel_id=1, source_target_pairs={{0,16},{16,0},{1,17},{17,1},{2,18},{18,2},{3,19},{19,3},{4,20},{20... | collective-permute-start | bytes 2359304 | tf_op jit(solution)/shard_map/ppermute | solution.py:23
  160.3 17.5 %collective-permute-start.19 = (bf16[384,768]{1,0:T(8,128)(2,1)S(1)}, bf16[384,768]{1,0:T(8,128)(2,1)}, u32[]{:S(2)}, u32[]{:S(2)}) collective-permute-start(bf16[384,768]{1,0:T(8,128)(2,1)S(1)} %slice.112), channel_id=1, source_target_pairs={{0,32},{32,64},{64,96},{96,0},{1,33},{33,65},{65,97},{97,1},{2,34}... | collective-permute-start | bytes 1769480 | tf_op jit(solution)/shard_map/ppermute | solution.py:23
  161.8 16.0 %collective-permute-start.20 = (bf16[384,768]{1,0:T(8,128)(2,1)S(1)}, bf16[384,768]{1,0:T(8,128)(2,1)}, u32[]{:S(2)}, u32[]{:S(2)}) collective-permute-start(bf16[384,768]{1,0:T(8,128)(2,1)S(1)} %slice.113), channel_id=1, source_target_pairs={{0,96},{32,0},{64,32},{96,64},{1,97},{33,1},{65,33},{97,65},{2,98}... | collective-permute-start | bytes 1769480 | tf_op jit(solution)/shard_map/ppermute | solution.py:23
  203.5 13.6 %collective-permute-start.22 = (bf16[512,384]{1,0:T(8,128)(2,1)S(1)}, bf16[512,384]{1,0:T(8,128)(2,1)S(1)}, u32[]{:S(2)}, u32[]{:S(2)}) collective-permute-start(bf16[512,384]{1,0:T(8,128)(2,1)S(1)} %get-tuple-element.35), channel_id=1, source_target_pairs={{0,8},{4,12},{8,0},{12,4},{1,9},{5,13},{9,1},{13,5},{2,10},{6,14},... | collective-permute-start | bytes 1179656 | tf_op jit(solution)/shard_map/ppermute | solution.py:23
  206.5 19.0 %collective-permute-start.23 = (bf16[512,384]{1,0:T(8,128)(2,1)S(1)}, bf16[512,384]{1,0:T(8,128)(2,1)S(1)}, u32[]{:S(2)}, u32[]{:S(2)}) collective-permute-start(bf16[512,384]{1,0:T(8,128)(2,1)S(1)} %get-tuple-element.37), channel_id=1, source_target_pairs={{0,4},{4,8},{8,12},{12,0},{1,5},{5,9},{9,13},{13,1},{2,6},{6,10},{... | collective-permute-start | bytes 1179656 | tf_op jit(solution)/shard_map/ppermute | solution.py:23
  207.1 18.4 %collective-permute-start.24 = (bf16[512,384]{1,0:T(8,128)(2,1)S(1)}, bf16[512,384]{1,0:T(8,128)(2,1)S(1)}, u32[]{:S(2)}, u32[]{:S(2)}) collective-permute-start(bf16[512,384]{1,0:T(8,128)(2,1)S(1)} %get-tuple-element.36), channel_id=1, source_target_pairs={{0,12},{4,0},{8,4},{12,8},{1,13},{5,1},{9,5},{13,9},{2,14},{6,2},{... | collective-permute-start | bytes 1179656 | tf_op jit(solution)/shard_map/ppermute | solution.py:23
  210.1 23.9 %collective-permute-start.27 = (bf16[512,384]{1,0:T(8,128)(2,1)S(1)}, bf16[512,384]{1,0:T(8,128)(2,1)S(1)}, u32[]{:S(2)}, u32[]{:S(2)}) collective-permute-start(bf16[512,384]{1,0:T(8,128)(2,1)S(1)} %get-tuple-element.38), channel_id=1, source_target_pairs={{0,8},{4,12},{8,0},{12,4},{1,9},{5,13},{9,1},{13,5},{2,10},{6,14},... | collective-permute-start | bytes 1179656 | tf_op jit(solution)/shard_map/ppermute | solution.py:23
  210.2 31.3 %collective-permute-start.28 = (bf16[512,384]{1,0:T(8,128)(2,1)S(1)}, bf16[512,384]{1,0:T(8,128)(2,1)S(1)}, u32[]{:S(2)}, u32[]{:S(2)}) collective-permute-start(bf16[512,384]{1,0:T(8,128)(2,1)S(1)} %get-tuple-element.40), channel_id=1, source_target_pairs={{0,4},{4,8},{8,12},{12,0},{1,5},{5,9},{9,13},{13,1},{2,6},{6,10},{... | collective-permute-start | bytes 1179656 | tf_op jit(solution)/shard_map/ppermute | solution.py:23
  217.1 24.6 %collective-permute-start.29 = (bf16[512,384]{1,0:T(8,128)(2,1)S(1)}, bf16[512,384]{1,0:T(8,128)(2,1)S(1)}, u32[]{:S(2)}, u32[]{:S(2)}) collective-permute-start(bf16[512,384]{1,0:T(8,128)(2,1)S(1)} %get-tuple-element.39), channel_id=1, source_target_pairs={{0,12},{4,0},{8,4},{12,8},{1,13},{5,1},{9,5},{13,9},{2,14},{6,2},{... | collective-permute-start | bytes 1179656 | tf_op jit(solution)/shard_map/ppermute | solution.py:23
  225.8 19.5 %collective-permute-start.25 = (bf16[512,384]{1,0:T(8,128)(2,1)S(1)}, bf16[512,384]{1,0:T(8,128)(2,1)S(1)}, u32[]{:S(2)}, u32[]{:S(2)}) collective-permute-start(bf16[512,384]{1,0:T(8,128)(2,1)S(1)} %fusion.25), channel_id=1, source_target_pairs={{0,16},{2,0},{16,18},{18,2},{1,17},{3,1},{17,19},{19,3},{4,20},{6,... | collective-permute-start | bytes 1179656 | tf_op jit(solution)/shard_map/ppermute | solution.py:28
  241.9 12.8 %collective-permute-start.30 = (bf16[512,384]{1,0:T(8,128)(2,1)S(1)}, bf16[512,384]{1,0:T(8,128)(2,1)S(1)}, u32[]{:S(2)}, u32[]{:S(2)}) collective-permute-start(bf16[512,384]{1,0:T(8,128)(2,1)S(1)} %fusion.22), channel_id=1, source_target_pairs={{0,0},{2,16},{16,2},{18,18},{1,1},{3,17},{17,3},{19,19},{4,4},{6,2... | collective-permute-start | bytes 1179656 | tf_op jit(solution)/shard_map/ppermute | solution.py:28
  (22 other events, 253.4 us)
Sparse Core Ops, SparseCore 0:
  9.0 54.6 all-gather.6
  65.4 53.0 all-gather.8
  121.8 38.0 all-gather.10

commit v3 on v2

--- a/solution.py
+++ b/solution.py
@@ -183,15 +183,15 @@
     )(mine, got, q_gain.reshape(1, HD), k_gain.reshape(1, HD))
 
 
-def output_kernel(block, index, att_own, att_other, act_ref, w_out_ref, *refs):
-    pieces, (keep_ref, send_ref) = refs[:5], refs[5:]
+def output_kernel(block, index, att_own, att_other, act_ref, *refs):
+    w_out, w_down, (keep_ref, send_ref) = refs[:4], refs[4:9], refs[9:]
     step, first = pl.program_id(0), index[2] == 0
 
-    def terms(*rows):
+    def terms(w_att, *w_act):
         att = jnp.where(index[1] == block, att_own[...], att_other[...])
-        term = jnp.dot(att, w_out_ref[0], preferred_element_type=jnp.float32)
+        term = jnp.dot(att, w_att[...], preferred_element_type=jnp.float32)
         start = 0
-        for right in rows:
+        for right in w_act:
             stop = start + right.shape[0]
             term += jnp.dot(act_ref[0, :, start:stop], right[...], preferred_element_type=jnp.float32)
             start = stop
@@ -200,7 +200,7 @@
         send_ref[0] = jnp.where(first, term[:, 384:], term[:, :384])
 
     for j in range(4):
-        pl.when(step == j)(lambda: terms(*(pieces[3:] if j == 3 else [pieces[j]])))
+        pl.when(step == j)(lambda: terms(w_out[j], *(w_down[3:] if j == 3 else [w_down[j]])))
 
 
 def output_terms(index, block, att_own, att_other, activated, w_out, w_down):
@@ -209,9 +209,8 @@
     return call(
         functools.partial(output_kernel, block),
         index,
-        [att_own, att_other, activated, w_out, *w_down],
-        [None, None, pl.BlockSpec((1, 512, ROWS), lambda j, i: (block, 0, 0)), by_block(0, 256, ROWS)]
-        + [None] * 5,
+        [att_own, att_other, activated, *w_out, *w_down],
+        [None, None, pl.BlockSpec((1, 512, ROWS), lambda j, i: (block, 0, 0))] + [None] * 9,
         [out, out],
         [out_spec, out_spec],
         [],
@@ -253,7 +252,9 @@
 
     block_a = move_z(tokens, [(1, 0), (0, 2), (3, 1), (2, 3)])
     block_b = move_z(tokens, [(0, 0), (1, 2), (2, 1), (3, 3)])
-    own = ring(jnp.stack([block_a, block_b]), "x", lambda v: (v[0], v[1]))
+    out_pieces = [w_out] + [shift(w_out, "y", -o) for o in STEPS[1:]]
+    held = after(jnp.stack([block_a, block_b]), *out_pieces)
+    own = ring(held, "x", lambda v: (v[0], v[1]))
     other = [shift(piece, "c", 1) for piece in own]
 
     parts = [moments(piece) for piece in own]
@@ -272,9 +273,8 @@
 
     qkv_mine, qkv_theirs = project_again(index, features, qkv_all)
 
-    out_all = lax.all_gather(after(w_out, qkv_all), "y", axis=0)
     w_down = after(w_down, qkv_all)
-    after_w, before_w = shift(w_down, "y", -1), shift(w_down, "y", 1)
+    after_w, before_w = after((shift(w_down, "y", -1), shift(w_down, "y", 1)), activated)
     forward = before_w[:384], after_w[384:]
     down = w_down, after_w, before_w, shift(forward[0], "y", 1), shift(forward[1], "y", -1)
 
@@ -284,25 +284,28 @@
 
     def start_terms(block):
         keep, send = output_terms(
-            index, block, attended, attended_other, activated, out_all, down
+            index, block, attended, attended_other, activated, out_pieces, down
         )
         return keep, shift(send, "c", 1)
 
     def start_sums(keep, got):
         pair = [keep[o].astype(jnp.float32) + got[o].astype(jnp.float32) for o in range(4)]
-        return pair[0], [shift(pair[o].astype(jnp.bfloat16), "x", o) for o in (2, 1, 3)]
-
-    def finish_sums(summed, got, pairs):
-        for g in got:
-            summed = summed + g.astype(jnp.float32)
-        return move_z(summed.astype(jnp.bfloat16), pairs).astype(jnp.float32)
+        far = pair[2].astype(jnp.bfloat16)
+        return pair, shift(far[:256], "x", 1), shift(far[256:], "x", -1)
+
+    def finish_sums(pair, first, second, pairs):
+        f32 = lambda v: v.astype(jnp.float32)
+        up = jnp.concatenate([pair[1][:256] + f32(first), pair[1][256:]]).astype(jnp.bfloat16)
+        down = jnp.concatenate([pair[3][:256], pair[3][256:] + f32(second)]).astype(jnp.bfloat16)
+        summed = pair[0] + f32(shift(up, "x", 1)) + f32(shift(down, "x", -1))
+        return f32(move_z(summed.astype(jnp.bfloat16), pairs))
 
     keep_a, got_a = start_terms(0)
     keep_b, got_b = start_terms(1)
-    sum_a, sent_a = start_sums(keep_a, got_a)
-    sum_b, sent_b = start_sums(keep_b, got_b)
-    part_a = finish_sums(sum_a, sent_a, [(0, 1), (2, 0), (1, 3), (3, 2)])
-    part_b = finish_sums(sum_b, sent_b, [(0, 0), (2, 1), (1, 2), (3, 3)])
+    sums_a = start_sums(keep_a, got_a)
+    sums_b = start_sums(keep_b, got_b)
+    part_a = finish_sums(*sums_a, [(0, 1), (2, 0), (1, 3), (3, 2)])
+    part_b = finish_sums(*sums_b, [(0, 0), (2, 1), (1, 2), (3, 3)])
     return (tokens.astype(jnp.float32) + part_a + part_b).astype(jnp.bfloat16)
 
 

time: 263 us -> 244 us (0.928)
  waiting for transfers between devices: 140 us -> 112 us
  starting transfers between devices: 38.6 us -> 45.6 us
    ppermute x26 -> x31, waiting for transfers between devices: 83.7 us -> 66.1 us  [shift(): lax.ppermute(value, axis, [(i, (i + by) % size) for i in range(size)])]
    ppermute x26 -> x31, starting transfers between devices: 26.5 us -> 33.6 us  [shift(): lax.ppermute(value, axis, [(i, (i + by) % size) for i in range(size)])]
    ppermute x4, waiting for transfers between devices: 24.9 us -> 19.1 us  [move_z(): lax.ppermute(value, ('l', 'h'), [(place(s), place(d)) for s, d in pairs])]
    all_gather x1, waiting for transfers between devices: 29.8 us -> 25.3 us  [shards(): qkv_all = lax.all_gather(w_qkv.transpose(1, 0, 2), 'y', axis=0)]
  transfers between devices with their start and end apart: 34 -> 38, of which waited for: 16 -> 21; matrix products, arithmetic and copies ran while one was open for 6% -> 7% of each run, Pallas kernels for 16% -> 18%
where the time goes in v3:
time: 244 us
  waiting for transfers between devices  112 us (46%)
  Pallas kernels  52.2 us (21%)
  starting transfers between devices  45.6 us (19%)
  between operations  13.8 us (6%)
  other arithmetic  13 us (5%)
  local copies, waits for them, and re-layouts  6.7 us (3%)
    ppermute x31, waiting for transfers between devices, shift(): lax.ppermute(value, axis, [(i, (i + by) % size) for i in range(size)])  66.1 us
    pallas_call x4, Pallas kernels, call(): pl.pallas_call(kernel, out_shape=outs, grid_spec=pltpu.PrefetchScalarGrid...  48.7 us
    ppermute x31, starting transfers between devices, shift(): lax.ppermute(value, axis, [(i, (i + by) % size) for i in range(size)])  33.6 us
    all_gather x1, waiting for transfers between devices, shards(): qkv_all = lax.all_gather(w_qkv.transpose(1, 0, 2), 'y', axis=0)  25.3 us
    ppermute x4, waiting for transfers between devices, move_z(): lax.ppermute(value, ('l', 'h'), [(place(s), place(d)) for s, d in pairs])  19.1 us
    ppermute x4, starting transfers between devices, move_z(): lax.ppermute(value, ('l', 'h'), [(place(s), place(d)) for s, d in pairs])  11.3 us
    convert_element_type x1, other arithmetic, shards(): activated = jax.nn.gelu(pre_act, approximate=False).astype(jnp.bfloat16)  7.8 us
  transfers between devices with their start and end apart: 38, of which 21 were waited for; matrix products, arithmetic and copies ran while one was open for 7% of the time, Pallas kernels for 18%

profile of v3, /device:TPU:32, one launch (start us, length us, event | category | flops | bytes accessed | tf_op | source)
XLA Modules:
  0.0 243.8 jit_solution(9067954660001399514)
XLA Ops:
  8.1 5.4 %collective-permute-start.1 = (bf16[512,384]{1,0:T(8,128)(2,1)}, bf16[512,384]{1,0:T(8,128)(2,1)S(1)}, u32[]{:S(2)}, u32[]{:S(2)}) collective-permute-start(bf16[512,384]{1,0:T(8,128)(2,1)} %param.8), channel_id=1, source_target_pairs={{0,0},{16,2},{2,16},{18,18},{1,1},{17,3},{3,17},{19,19},{4,4},{20,... | collective-permute-start | bytes 1179656 | tf_op jit(solution)/shard_map/ppermute | solution.py:28
  13.5 3.1 %collective-permute-start.2 = (bf16[256,768]{1,0:T(8,128)(2,1)}, bf16[256,768]{1,0:T(8,128)(2,1)S(1)}, u32[]{:S(2)}, u32[]{:S(2)}) collective-permute-start(bf16[256,768]{1,0:T(8,128)(2,1)} %refs_0_.3), channel_id=1, source_target_pairs={{0,96},{32,0},{64,32},{96,64},{1,97},{33,1},{65,33},{97,65},{2,98}... | collective-permute-start | bytes 1179656 | tf_op jit(solution)/shard_map/ppermute | solution.py:23
  20.7 8.3 %collective-permute-done.1 = bf16[512,384]{1,0:T(8,128)(2,1)S(1)} collective-permute-done((bf16[512,384]{1,0:T(8,128)(2,1)}, bf16[512,384]{1,0:T(8,128)(2,1)S(1)}, u32[]{:S(2)}, u32[]{:S(2)}) %collective-permute-start.1) | collective-permute-done | bytes 393248 | tf_op jit(solution)/shard_map/ppermute | solution.py:28
  29.2 5.4 %collective-permute-done.2.refs_1_ = bf16[256,768]{1,0:T(8,128)(2,1)S(1)} collective-permute-done((bf16[256,768]{1,0:T(8,128)(2,1)}, bf16[256,768]{1,0:T(8,128)(2,1)S(1)}, u32[]{:S(2)}, u32[]{:S(2)}) %collective-permute-start.2) | collective-permute-done | bytes 393248 | tf_op jit(solution)/shard_map/ppermute | solution.py:23
  34.6 2.8 %collective-permute-done.3.refs_2_ = bf16[256,768]{1,0:T(8,128)(2,1)S(1)} collective-permute-done((bf16[256,768]{1,0:T(8,128)(2,1)}, bf16[256,768]{1,0:T(8,128)(2,1)S(1)}, u32[]{:S(2)}, u32[]{:S(2)}) %collective-permute-start.3) | collective-permute-done | bytes 393248 | tf_op jit(solution)/shard_map/ppermute | solution.py:23
  37.4 9.7 %collective-permute-done.4.refs_3_ = bf16[256,768]{1,0:T(8,128)(2,1)S(1)} collective-permute-done((bf16[256,768]{1,0:T(8,128)(2,1)}, bf16[256,768]{1,0:T(8,128)(2,1)S(1)}, u32[]{:S(2)}, u32[]{:S(2)}) %collective-permute-start.4) | collective-permute-done | bytes 393248 | tf_op jit(solution)/shard_map/ppermute | solution.py:23
  51.1 13.6 %collective-permute-done.6.refs_2_ = bf16[2,512,384]{2,1,0:T(8,128)(2,1)S(1)} collective-permute-done((bf16[2,512,384]{2,1,0:T(8,128)(2,1)S(1)}, bf16[2,512,384]{2,1,0:T(8,128)(2,1)S(1)}, u32[]{:S(2)}, u32[]{:S(2)}) %collective-permute-start.6) | collective-permute-done | bytes 786464 | tf_op jit(solution)/shard_map/ppermute | solution.py:23
  70.1 3.6 %collective-permute-done.7.refs_3_ = bf16[512,384]{1,0:T(8,128)(2,1)S(1)} collective-permute-done((bf16[512,384]{1,0:T(8,128)(2,1)S(1)}, bf16[512,384]{1,0:T(8,128)(2,1)S(1)}, u32[]{:S(2)}, u32[]{:S(2)}) %collective-permute-start.7) | collective-permute-done | bytes 393248 | tf_op jit(solution)/shard_map/ppermute | solution.py:23
  82.2 18.3 %shard_map.82 = (f32[2,512,768]{2,1,0:T(8,128)}, bf16[2,512,768]{2,1,0:T(8,128)(2,1)}, bf16[4,2,1024,384]{3,2,1,0:T(8,128)(2,1)}) custom-call(s32[6]{0:T(128)} %stack.67.index, bf16[2,512,384]{2,1,0:T(8,128)(2,1)} %copy-done, bf16[2,512,384]{2,1,0:T(8,128)(2,1)} %copy-done.2, bf16[2,512,384]{2,1,0:T(8,128)(2,1)} %copy-done.1, bf16[512,384]{1,0:T(8,128)(2,1)} %copy-done.4, ...), custom_call_target="tpu_custom_call" | custom-call | flops 4831838208 | bytes 22052864 | tf_op jit(solution)/shard_map/pallas_call | solution.py:90
  101.4 25.3 %all-gather.7.cloned.1.call-done = bf16[12,768,256]{2,1,0:T(8,128)(2,1)} async-done(((bf16[3,768,256]{2,1,0:T(8,128)(2,1)}), bf16[12,768,256]{2,1,0:T(8,128)(2,1)}) %all-gather.7.cloned.1.call-update) | async-done | bytes 4718608 | tf_op jit(solution)/shard_map/all_gather | solution.py:251
  128.8 11.8 %shard_map.83 = (f32[512,768]{1,0:T(8,128)}, bf16[512,768]{1,0:T(8,128)(2,1)}) custom-call(s32[6]{0:T(128)} %stack.67.index, bf16[4,2,1024,384]{3,2,1,0:T(8,128)(2,1)} %get-tuple-element.24.block_ref, bf16[4,3,768,256]{3,2,1,0:T(8,128)(2,1)} %bitcast.187), custom_call_target="tpu_custom_call" | custom-call | flops 4831838208 | bytes 13369344 | tf_op jit(solution)/shard_map/pallas_call | solution.py:90
  141.0 7.8 %fusion.2.act_ref = bf16[2,512,768]{2,1,0:T(8,128)(2,1)} fusion(f32[2,512,768]{2,1,0:T(8,128)S(1)} %copy-done.3, bf16[2,512,768]{2,1,0:T(8,128)(2,1)S(1)} %collective-permute-done.18), kind=kLoop, calls=%fused_computation.3 | loop fusion | flops 52690944 | bytes 6291456 | tf_op jit(solution)/shard_map/convert_element_type | solution.py:272
  148.8 5.8 %collective-permute-done.19.refs_5_ = bf16[768,768]{1,0:T(8,128)(2,1)S(1)} collective-permute-done((bf16[768,768]{1,0:T(8,128)(2,1)}, bf16[768,768]{1,0:T(8,128)(2,1)S(1)}, u32[]{:S(2)}, u32[]{:S(2)}) %collective-permute-start.19) | collective-permute-done | bytes 1179680 | tf_op jit(solution)/shard_map/ppermute | solution.py:23
  158.1 3.2 %collective-permute-start.23 = (bf16[384,768]{1,0:T(8,128)(2,1)S(1)}, bf16[384,768]{1,0:T(8,128)(2,1)S(1)}, u32[]{:S(2)}, u32[]{:S(2)}) collective-permute-start(bf16[384,768]{1,0:T(8,128)(2,1)S(1)} %slice.163), channel_id=1, source_target_pairs={{0,96},{32,0},{64,32},{96,64},{1,97},{33,1},{65,33},{97,65},{2,98}... | collective-permute-start | bytes 1769480 | tf_op jit(solution)/shard_map/ppermute | solution.py:23
  162.2 3.6 %shard_map.84.att_own = bf16[512,256]{1,0:T(8,128)(2,1)} custom-call(f32[512,768]{1,0:T(8,128)} %get-tuple-element.25.mine_ref, bf16[512,768]{1,0:T(8,128)(2,1)} %copy-done.8, f32[1,128]{1,0:T(1,128)} %bitcast.185, f32[1,128]{1,0:T(1,128)} %bitcast.186), custom_call_target="tpu_custom_call" | custom-call | flops 134217728 | bytes 2359296 | tf_op jit(solution)/shard_map/pallas_call | solution.py:176
  165.9 6.5 %collective-permute-done.21.att_other = bf16[512,256]{1,0:T(8,128)(2,1)S(1)} collective-permute-done((bf16[512,256]{1,0:T(8,128)(2,1)}, bf16[512,256]{1,0:T(8,128)(2,1)S(1)}, u32[]{:S(2)}, u32[]{:S(2)}) %collective-permute-start.21) | collective-permute-done | bytes 262176 | tf_op jit(solution)/shard_map/ppermute | solution.py:23
  174.8 9.2 %shard_map.85 = (bf16[4,512,384]{2,1,0:T(8,128)(2,1)}, bf16[4,512,384]{2,1,0:T(8,128)(2,1)}) custom-call(s32[6]{0:T(128)} %stack.67.index, bf16[512,256]{1,0:T(8,128)(2,1)} %shard_map.84.att_own, bf16[512,256]{1,0:T(8,128)(2,1)} %copy-done.16, bf16[2,512,768]{2,1,0:T(8,128)(2,1)} %fusion.2.act_ref, bf16[256,768]{1,0:T(8,128)(2,1)} %refs_0_.3, ...), custom_call_target="tpu_custom_call" | custom-call | flops 3221225472 | bytes 11534336 | tf_op jit(solution)/shard_map/pallas_call | solution.py:90
  184.1 9.4 %shard_map.86 = (bf16[4,512,384]{2,1,0:T(8,128)(2,1)}, bf16[4,512,384]{2,1,0:T(8,128)(2,1)}) custom-call(s32[6]{0:T(128)} %stack.67.index, bf16[512,256]{1,0:T(8,128)(2,1)} %shard_map.84.att_own, bf16[512,256]{1,0:T(8,128)(2,1)} %copy-done.16, bf16[2,512,768]{2,1,0:T(8,128)(2,1)} %fusion.2.act_ref, bf16[256,768]{1,0:T(8,128)(2,1)} %refs_0_.3, ...), custom_call_target="tpu_custom_call" | custom-call | flops 3221225472 | bytes 11534336 | tf_op jit(solution)/shard_map/pallas_call | solution.py:90
  203.7 3.0 %collective-permute-start.28 = (bf16[512,384]{1,0:T(8,128)(2,1)S(1)}, bf16[512,384]{1,0:T(8,128)(2,1)S(1)}, u32[]{:S(2)}, u32[]{:S(2)}) collective-permute-start(bf16[512,384]{1,0:T(8,128)(2,1)S(1)} %pad_maximum_fusion.2), channel_id=1, source_target_pairs={{0,12},{4,0},{8,4},{12,8},{1,13},{5,1},{9,5},{13,9},{2,14},{6,2},{... | collective-permute-start | bytes 1179656 | tf_op jit(solution)/shard_map/ppermute | solution.py:23
  207.9 3.0 %collective-permute-start.34 = (bf16[512,384]{1,0:T(8,128)(2,1)S(1)}, bf16[512,384]{1,0:T(8,128)(2,1)S(1)}, u32[]{:S(2)}, u32[]{:S(2)}) collective-permute-start(bf16[512,384]{1,0:T(8,128)(2,1)S(1)} %pad_maximum_fusion.4), channel_id=1, source_target_pairs={{0,12},{4,0},{8,4},{12,8},{1,13},{5,1},{9,5},{13,9},{2,14},{6,2},{... | collective-permute-start | bytes 1179656 | tf_op jit(solution)/shard_map/ppermute | solution.py:23
  210.9 5.6 %collective-permute-done.26 = bf16[512,384]{1,0:T(8,128)(2,1)S(1)} collective-permute-done((bf16[512,384]{1,0:T(8,128)(2,1)S(1)}, bf16[512,384]{1,0:T(8,128)(2,1)S(1)}, u32[]{:S(2)}, u32[]{:S(2)}) %collective-permute-start.26) | collective-permute-done | bytes 393248 | tf_op jit(solution)/shard_map/ppermute | solution.py:23
  219.1 4.4 %collective-permute-done.32 = bf16[512,384]{1,0:T(8,128)(2,1)S(1)} collective-permute-done((bf16[512,384]{1,0:T(8,128)(2,1)S(1)}, bf16[512,384]{1,0:T(8,128)(2,1)S(1)}, u32[]{:S(2)}, u32[]{:S(2)}) %collective-permute-start.32) | collective-permute-done | bytes 393248 | tf_op jit(solution)/shard_map/ppermute | solution.py:23
  223.7 3.5 %collective-permute-start.35 = (bf16[512,384]{1,0:T(8,128)(2,1)S(1)}, bf16[512,384]{1,0:T(8,128)(2,1)S(1)}, u32[]{:S(2)}, u32[]{:S(2)}) collective-permute-start(bf16[512,384]{1,0:T(8,128)(2,1)S(1)} %fusion.21), channel_id=1, source_target_pairs={{0,0},{2,16},{16,2},{18,18},{1,1},{3,17},{17,3},{19,19},{4,4},{6,2... | collective-permute-start | bytes 1179656 | tf_op jit(solution)/shard_map/ppermute | solution.py:28
  227.2 8.8 %collective-permute-done.35 = bf16[512,384]{1,0:T(8,128)(2,1)S(1)} collective-permute-done((bf16[512,384]{1,0:T(8,128)(2,1)S(1)}, bf16[512,384]{1,0:T(8,128)(2,1)S(1)}, u32[]{:S(2)}, u32[]{:S(2)}) %collective-permute-start.35) | collective-permute-done | bytes 393248 | tf_op jit(solution)/shard_map/ppermute | solution.py:28
  (139 shorter events, 48.8 us)
Async XLA Ops:
  6.5 75.6 %all-gather.5.cloned.1.call-start = ((), (), s32[]{:S(2)}) async-start(), calls=%async_computation | async-start | bytes 5898240 | tf_op jit(solution)/shard_map/all_gather | solution.py:250
  7.3 119.5 %all-gather.7.cloned.1.call-start = ((), (), s32[]{:S(2)}) async-start(), calls=%async_computation.1 | async-start | bytes 5898240 | tf_op jit(solution)/shard_map/all_gather | solution.py:251
  8.0 12.7 %collective-permute-start = (bf16[512,384]{1,0:T(8,128)(2,1)}, bf16[512,384]{1,0:T(8,128)(2,1)S(1)}, u32[]{:S(2)}, u32[]{:S(2)}) collective-permute-start(bf16[512,384]{1,0:T(8,128)(2,1)} %param.8), channel_id=1, source_target_pairs={{16,0},{0,2},{18,16},{2,18},{17,1},{1,3},{19,17},{3,19},{20,4},{4,... | collective-permute-start | bytes 1179656 | tf_op jit(solution)/shard_map/ppermute | solution.py:28
  8.1 21.0 %collective-permute-start.1 = (bf16[512,384]{1,0:T(8,128)(2,1)}, bf16[512,384]{1,0:T(8,128)(2,1)S(1)}, u32[]{:S(2)}, u32[]{:S(2)}) collective-permute-start(bf16[512,384]{1,0:T(8,128)(2,1)} %param.8), channel_id=1, source_target_pairs={{0,0},{16,2},{2,16},{18,18},{1,1},{17,3},{3,17},{19,19},{4,4},{20,... | collective-permute-start | bytes 1179656 | tf_op jit(solution)/shard_map/ppermute | solution.py:28
  13.5 21.1 %collective-permute-start.2 = (bf16[256,768]{1,0:T(8,128)(2,1)}, bf16[256,768]{1,0:T(8,128)(2,1)S(1)}, u32[]{:S(2)}, u32[]{:S(2)}) collective-permute-start(bf16[256,768]{1,0:T(8,128)(2,1)} %refs_0_.3), channel_id=1, source_target_pairs={{0,96},{32,0},{64,32},{96,64},{1,97},{33,1},{65,33},{97,65},{2,98}... | collective-permute-start | bytes 1179656 | tf_op jit(solution)/shard_map/ppermute | solution.py:23
  16.6 20.8 %collective-permute-start.3 = (bf16[256,768]{1,0:T(8,128)(2,1)}, bf16[256,768]{1,0:T(8,128)(2,1)S(1)}, u32[]{:S(2)}, u32[]{:S(2)}) collective-permute-start(bf16[256,768]{1,0:T(8,128)(2,1)} %refs_0_.3), channel_id=1, source_target_pairs={{0,32},{32,64},{64,96},{96,0},{1,33},{33,65},{65,97},{97,1},{2,34}... | collective-permute-start | bytes 1179656 | tf_op jit(solution)/shard_map/ppermute | solution.py:23
  16.6 30.5 %collective-permute-start.4 = (bf16[256,768]{1,0:T(8,128)(2,1)}, bf16[256,768]{1,0:T(8,128)(2,1)S(1)}, u32[]{:S(2)}, u32[]{:S(2)}) collective-permute-start(bf16[256,768]{1,0:T(8,128)(2,1)} %refs_0_.3), channel_id=1, source_target_pairs={{0,64},{32,96},{64,0},{96,32},{1,65},{33,97},{65,1},{97,33},{2,66}... | collective-permute-start | bytes 1179656 | tf_op jit(solution)/shard_map/ppermute | solution.py:23
  47.1 17.5 %collective-permute-start.6 = (bf16[2,512,384]{2,1,0:T(8,128)(2,1)S(1)}, bf16[2,512,384]{2,1,0:T(8,128)(2,1)S(1)}, u32[]{:S(2)}, u32[]{:S(2)}) collective-permute-start(bf16[2,512,384]{2,1,0:T(8,128)(2,1)S(1)} %pad_maximum_fusion.refs_0_), channel_id=1, source_target_pairs={{0,4},{4,8},{8,12},{12,0},{1,5},{5,9},{9,13},{13,1},{2,6},{6,10},{... | collective-permute-start | bytes 2359304 | tf_op jit(solution)/shard_map/ppermute | solution.py:23
  48.6 17.6 %collective-permute-start.5 = (bf16[2,512,384]{2,1,0:T(8,128)(2,1)S(1)}, bf16[2,512,384]{2,1,0:T(8,128)(2,1)S(1)}, u32[]{:S(2)}, u32[]{:S(2)}) collective-permute-start(bf16[2,512,384]{2,1,0:T(8,128)(2,1)S(1)} %pad_maximum_fusion.refs_0_), channel_id=1, source_target_pairs={{0,12},{4,0},{8,4},{12,8},{1,13},{5,1},{9,5},{13,9},{2,14},{6,2},{... | collective-permute-start | bytes 2359304 | tf_op jit(solution)/shard_map/ppermute | solution.py:23
  50.4 31.8 %collective-permute-start.9 = (bf16[2,512,384]{2,1,0:T(8,128)(2,1)S(1)}, bf16[2,512,384]{2,1,0:T(8,128)(2,1)}, u32[]{:S(2)}, u32[]{:S(2)}) collective-permute-start(bf16[2,512,384]{2,1,0:T(8,128)(2,1)S(1)} %pad_maximum_fusion.refs_0_), channel_id=1, source_target_pairs={{0,1},{1,0},{2,3},{3,2},{4,5},{5,4},{6,7},{7,6},{8,9},{9,8},{10,11... | collective-permute-start | bytes 2359304 | tf_op jit(solution)/shard_map/ppermute | solution.py:23
  68.6 13.6 %collective-permute-start.10 = (bf16[2,512,384]{2,1,0:T(8,128)(2,1)S(1)}, bf16[2,512,384]{2,1,0:T(8,128)(2,1)}, u32[]{:S(2)}, u32[]{:S(2)}) collective-permute-start(bf16[2,512,384]{2,1,0:T(8,128)(2,1)S(1)} %collective-permute-done.5.refs_1_), channel_id=1, source_target_pairs={{0,1},{1,0},{2,3},{3,2},{4,5},{5,4},{6,7},{7,6},{8,9},{9,8},{10,11... | collective-permute-start | bytes 2359304 | tf_op jit(solution)/shard_map/ppermute | solution.py:23
  68.7 13.5 %collective-permute-start.11 = (bf16[2,512,384]{2,1,0:T(8,128)(2,1)S(1)}, bf16[2,512,384]{2,1,0:T(8,128)(2,1)}, u32[]{:S(2)}, u32[]{:S(2)}) collective-permute-start(bf16[2,512,384]{2,1,0:T(8,128)(2,1)S(1)} %collective-permute-done.6.refs_2_), channel_id=1, source_target_pairs={{0,1},{1,0},{2,3},{3,2},{4,5},{5,4},{6,7},{7,6},{8,9},{9,8},{10,11... | collective-permute-start | bytes 2359304 | tf_op jit(solution)/shard_map/ppermute | solution.py:23
  100.5 40.5 %collective-permute-start.18 = (bf16[2,512,768]{2,1,0:T(8,128)(2,1)}, bf16[2,512,768]{2,1,0:T(8,128)(2,1)S(1)}, u32[]{:S(2)}, u32[]{:S(2)}) collective-permute-start(bf16[2,512,768]{2,1,0:T(8,128)(2,1)} %get-tuple-element.28), channel_id=1, source_target_pairs={{0,16},{16,0},{1,17},{17,1},{2,18},{18,2},{3,19},{19,3},{4,20},{20... | collective-permute-start | bytes 4718600 | tf_op jit(solution)/shard_map/ppermute | solution.py:23
  126.7 27.9 %collective-permute-start.19 = (bf16[768,768]{1,0:T(8,128)(2,1)}, bf16[768,768]{1,0:T(8,128)(2,1)S(1)}, u32[]{:S(2)}, u32[]{:S(2)}) collective-permute-start(bf16[768,768]{1,0:T(8,128)(2,1)} %refs_4_.1), channel_id=1, source_target_pairs={{0,96},{32,0},{64,32},{96,64},{1,97},{33,1},{65,33},{97,65},{2,98}... | collective-permute-start | bytes 3538952 | tf_op jit(solution)/shard_map/ppermute | solution.py:23
  127.9 29.0 %collective-permute-start.20 = (bf16[768,768]{1,0:T(8,128)(2,1)}, bf16[768,768]{1,0:T(8,128)(2,1)}, u32[]{:S(2)}, u32[]{:S(2)}) collective-permute-start(bf16[768,768]{1,0:T(8,128)(2,1)} %refs_4_.1), channel_id=1, source_target_pairs={{0,32},{32,64},{64,96},{96,0},{1,33},{33,65},{65,97},{97,1},{2,34}... | collective-permute-start | bytes 3538952 | tf_op jit(solution)/shard_map/ppermute | solution.py:23
  140.5 20.8 %collective-permute-start.17 = (bf16[512,768]{1,0:T(8,128)(2,1)}, bf16[512,768]{1,0:T(8,128)(2,1)S(1)}, u32[]{:S(2)}, u32[]{:S(2)}) collective-permute-start(bf16[512,768]{1,0:T(8,128)(2,1)} %get-tuple-element.26), channel_id=1, source_target_pairs={{0,16},{16,0},{1,17},{17,1},{2,18},{18,2},{3,19},{19,3},{4,20},{20... | collective-permute-start | bytes 2359304 | tf_op jit(solution)/shard_map/ppermute | solution.py:23
  158.0 15.2 %collective-permute-start.22 = (bf16[384,768]{1,0:T(8,128)(2,1)S(1)}, bf16[384,768]{1,0:T(8,128)(2,1)S(1)}, u32[]{:S(2)}, u32[]{:S(2)}) collective-permute-start(bf16[384,768]{1,0:T(8,128)(2,1)S(1)} %slice.162), channel_id=1, source_target_pairs={{0,32},{32,64},{64,96},{96,0},{1,33},{33,65},{65,97},{97,1},{2,34}... | collective-permute-start | bytes 1769480 | tf_op jit(solution)/shard_map/ppermute | solution.py:23
  158.1 15.1 %collective-permute-start.23 = (bf16[384,768]{1,0:T(8,128)(2,1)S(1)}, bf16[384,768]{1,0:T(8,128)(2,1)S(1)}, u32[]{:S(2)}, u32[]{:S(2)}) collective-permute-start(bf16[384,768]{1,0:T(8,128)(2,1)S(1)} %slice.163), channel_id=1, source_target_pairs={{0,96},{32,0},{64,32},{96,64},{1,97},{33,1},{65,33},{97,65},{2,98}... | collective-permute-start | bytes 1769480 | tf_op jit(solution)/shard_map/ppermute | solution.py:23
  203.2 13.3 %collective-permute-start.26 = (bf16[512,384]{1,0:T(8,128)(2,1)S(1)}, bf16[512,384]{1,0:T(8,128)(2,1)S(1)}, u32[]{:S(2)}, u32[]{:S(2)}) collective-permute-start(bf16[512,384]{1,0:T(8,128)(2,1)S(1)} %pad_maximum_fusion.1), channel_id=1, source_target_pairs={{0,4},{4,8},{8,12},{12,0},{1,5},{5,9},{9,13},{13,1},{2,6},{6,10},{... | collective-permute-start | bytes 1179656 | tf_op jit(solution)/shard_map/ppermute | solution.py:23
  203.7 12.9 %collective-permute-start.28 = (bf16[512,384]{1,0:T(8,128)(2,1)S(1)}, bf16[512,384]{1,0:T(8,128)(2,1)S(1)}, u32[]{:S(2)}, u32[]{:S(2)}) collective-permute-start(bf16[512,384]{1,0:T(8,128)(2,1)S(1)} %pad_maximum_fusion.2), channel_id=1, source_target_pairs={{0,12},{4,0},{8,4},{12,8},{1,13},{5,1},{9,5},{13,9},{2,14},{6,2},{... | collective-permute-start | bytes 1179656 | tf_op jit(solution)/shard_map/ppermute | solution.py:23
  207.4 16.1 %collective-permute-start.32 = (bf16[512,384]{1,0:T(8,128)(2,1)S(1)}, bf16[512,384]{1,0:T(8,128)(2,1)S(1)}, u32[]{:S(2)}, u32[]{:S(2)}) collective-permute-start(bf16[512,384]{1,0:T(8,128)(2,1)S(1)} %pad_maximum_fusion.3), channel_id=1, source_target_pairs={{0,4},{4,8},{8,12},{12,0},{1,5},{5,9},{9,13},{13,1},{2,6},{6,10},{... | collective-permute-start | bytes 1179656 | tf_op jit(solution)/shard_map/ppermute | solution.py:23
  207.9 15.6 %collective-permute-start.34 = (bf16[512,384]{1,0:T(8,128)(2,1)S(1)}, bf16[512,384]{1,0:T(8,128)(2,1)S(1)}, u32[]{:S(2)}, u32[]{:S(2)}) collective-permute-start(bf16[512,384]{1,0:T(8,128)(2,1)S(1)} %pad_maximum_fusion.4), channel_id=1, source_target_pairs={{0,12},{4,0},{8,4},{12,8},{1,13},{5,1},{9,5},{13,9},{2,14},{6,2},{... | collective-permute-start | bytes 1179656 | tf_op jit(solution)/shard_map/ppermute | solution.py:23
  216.7 10.4 %collective-permute-start.29 = (bf16[512,384]{1,0:T(8,128)(2,1)S(1)}, bf16[512,384]{1,0:T(8,128)(2,1)S(1)}, u32[]{:S(2)}, u32[]{:S(2)}) collective-permute-start(bf16[512,384]{1,0:T(8,128)(2,1)S(1)} %fusion.23), channel_id=1, source_target_pairs={{0,16},{2,0},{16,18},{18,2},{1,17},{3,1},{17,19},{19,3},{4,20},{6,... | collective-permute-start | bytes 1179656 | tf_op jit(solution)/shard_map/ppermute | solution.py:28
  223.7 12.3 %collective-permute-start.35 = (bf16[512,384]{1,0:T(8,128)(2,1)S(1)}, bf16[512,384]{1,0:T(8,128)(2,1)S(1)}, u32[]{:S(2)}, u32[]{:S(2)}) collective-permute-start(bf16[512,384]{1,0:T(8,128)(2,1)S(1)} %fusion.21), channel_id=1, source_target_pairs={{0,0},{2,16},{16,2},{18,18},{1,1},{3,17},{17,3},{19,19},{4,4},{6,2... | collective-permute-start | bytes 1179656 | tf_op jit(solution)/shard_map/ppermute | solution.py:28
  (31 other events, 335.4 us)
Sparse Core Ops, SparseCore 0:
  9.0 65.7 all-gather.4
  76.5 50.2 all-gather.6

commit v4 on v3

--- a/solution.py
+++ b/solution.py
@@ -36,9 +36,14 @@
 
 
 def project_kernel(index, *refs):
-    own, other, (centre, scale, gain, w_ref) = refs[0:5], refs[5:10], refs[10:14]
-    sum_ref, sent_ref, block_ref = refs[14:]
+    own, other, (stats, gain, w_ref) = refs[0:5], refs[5:10], refs[10:13]
+    sum_ref, sent_ref, block_ref, turned = refs[13:]
     step, core = pl.program_id(0), index[2]
+
+    @pl.when(step == 0)
+    def _():
+        turned[...] = stats[...].T
+
     for j in range(4):
 
         @pl.when(step == j)
@@ -46,7 +51,8 @@
             for pieces, place in ((own, core), (other, 1 - core)):
                 for t in range(2):
                     raw = pieces[3 + t][...] if j == 3 else pieces[j][t]
-                    value = (raw.astype(jnp.float32) - centre[t]) * scale[t] * gain[0, 0, place]
+                    centre, scale = turned[:, t : t + 1], turned[:, 2 + t : 3 + t]
+                    value = (raw.astype(jnp.float32) - centre) * scale * gain[0, 0, place]
                     block_ref[0, place, t * 512 : (t + 1) * 512] = value.astype(jnp.bfloat16)
 
     multiply(step, block_ref, w_ref, sum_ref)
@@ -119,12 +125,12 @@
 BY_STEP = pl.BlockSpec((1, 2, 1024, 384), lambda j, i: (j, 0, 0, 0))
 
 
-def project(index, own, other, centre, scale, gain, weights):
+def project(index, own, other, stats, gain, weights):
     return call(
         project_kernel,
         index,
-        [*own, *other, centre, scale, gain, weights],
-        [None] * 12
+        [*own, *other, stats, gain, weights],
+        [None] * 11
         + [pl.BlockSpec((1, 1, 2, 1, 384), lambda j, i: ((i[3] + order(j)) % 4, i[5], 0, 0, 0))]
         + [by_block(3, *weights.shape[1:])],
         [
@@ -133,7 +139,7 @@
             jax.ShapeDtypeStruct((4, 2, 1024, 384), jnp.bfloat16),
         ],
         [None, None, BY_STEP],
-        [],
+        [pltpu.VMEM((512, 8), jnp.float32)],
         2 * 1024 * 3072 * ROWS,
     )
 
@@ -183,38 +189,42 @@
     )(mine, got, q_gain.reshape(1, HD), k_gain.reshape(1, HD))
 
 
-def output_kernel(block, index, att_own, att_other, act_ref, *refs):
-    w_out, w_down, (keep_ref, send_ref) = refs[:4], refs[4:9], refs[9:]
+def output_kernel(index, att_own, att_other, act_ref, w_down, *refs):
+    w_out, w_rest, outs, w_ref = refs[:5], refs[5:9], refs[9:13], refs[13]
     step, first = pl.program_id(0), index[2] == 0
-
-    def terms(w_att, *w_act):
+    for j in range(4):
+
+        @pl.when(step == j)
+        def _():
+            if j == 3:
+                w_ref[:128] = w_out[3][...]
+                w_ref[128:256] = w_out[4][...]
+            else:
+                w_ref[:256] = w_out[j][...]
+            w_ref[256:] = w_rest[j][...]
+
+    for block in range(2):
         att = jnp.where(index[1] == block, att_own[...], att_other[...])
-        term = jnp.dot(att, w_att[...], preferred_element_type=jnp.float32)
-        start = 0
-        for right in w_act:
-            stop = start + right.shape[0]
-            term += jnp.dot(act_ref[0, :, start:stop], right[...], preferred_element_type=jnp.float32)
-            start = stop
+        term = jnp.dot(act_ref[block, :, :512], w_down[0], preferred_element_type=jnp.float32)
+        mixed = jnp.concatenate([att, act_ref[block, :, 512:]], axis=1)
+        term += jnp.dot(mixed, w_ref[...], preferred_element_type=jnp.float32)
         term = term.astype(jnp.bfloat16)
-        keep_ref[0] = jnp.where(first, term[:, :384], term[:, 384:])
-        send_ref[0] = jnp.where(first, term[:, 384:], term[:, :384])
-
-    for j in range(4):
-        pl.when(step == j)(lambda: terms(w_out[j], *(w_down[3:] if j == 3 else [w_down[j]])))
-
-
-def output_terms(index, block, att_own, att_other, activated, w_out, w_down):
+        outs[2 * block][0] = jnp.where(first, term[:, :384], term[:, 384:])
+        outs[2 * block + 1][0] = jnp.where(first, term[:, 384:], term[:, :384])
+
+
+def output_terms(index, att_own, att_other, activated, w_down, w_out, w_rest):
     out = jax.ShapeDtypeStruct((4, 512, 384), jnp.bfloat16)
     out_spec = pl.BlockSpec((1, 512, 384), lambda j, i: ((i[4] + order(j)) % 4, 0, 0))
     return call(
-        functools.partial(output_kernel, block),
+        output_kernel,
         index,
-        [att_own, att_other, activated, *w_out, *w_down],
-        [None, None, pl.BlockSpec((1, 512, ROWS), lambda j, i: (block, 0, 0))] + [None] * 9,
-        [out, out],
-        [out_spec, out_spec],
-        [],
-        2 * 512 * 1024 * 4 * ROWS,
+        [att_own, att_other, activated, w_down, *w_out, *w_rest],
+        [None] * 3 + [by_block(0, 512, ROWS)] + [None] * 9,
+        [out] * 4,
+        [out_spec] * 4,
+        [pltpu.VMEM((512, ROWS), jnp.bfloat16)],
+        2 * 1024 * 1024 * 4 * ROWS,
     )
 
 
@@ -249,12 +259,12 @@
 
     up_all = lax.all_gather(w_up[None], "y", axis=0)
     qkv_all = lax.all_gather(w_qkv.transpose(1, 0, 2), "y", axis=0)
+    down_all = lax.all_gather(w_down[:512], "y", axis=0)
 
     block_a = move_z(tokens, [(1, 0), (0, 2), (3, 1), (2, 3)])
     block_b = move_z(tokens, [(0, 0), (1, 2), (2, 1), (3, 3)])
-    out_pieces = [w_out] + [shift(w_out, "y", -o) for o in STEPS[1:]]
-    held = after(jnp.stack([block_a, block_b]), *out_pieces)
-    own = ring(held, "x", lambda v: (v[0], v[1]))
+    out_near = shift(w_out, "y", -1), shift(w_out, "y", 1)
+    own = ring(after(jnp.stack([block_a, block_b]), *out_near), "x", lambda v: (v[0], v[1]))
     other = [shift(piece, "c", 1) for piece in own]
 
     parts = [moments(piece) for piece in own]
@@ -262,31 +272,26 @@
     stats = jnp.stack(merge([*parts[:3], last], 384))
     cross = lax.ppermute(stats, ("l", "c"), [(i, 3 - i) for i in range(4)])
     centre, spread = merge([stats, shift(stats, "c", 1), shift(stats, "l", 1), cross], 1536)
-    centre, scale = lax.optimization_barrier((centre, lax.rsqrt(spread / 6144 + EPS)))
+    stats = jnp.concatenate([centre, lax.rsqrt(spread / 6144 + EPS), centre, centre])
     gain = ln_gain.reshape(4, 2, 2, 1, 384)
 
     up_sum, up_sent, features = project(
-        index, own, other, centre[..., None], scale[..., None], gain, up_all
-    )
+        index, own, other, stats, gain, up_all
+    )
+    out_near = after(out_near, up_sum)
+    out_far = shift(out_near[1][:128], "y", 1), shift(out_near[0][128:], "y", -1)
+    out_pieces = w_out, *out_near, *out_far
+    qkv_all = after(qkv_all, *out_far)
+    rest = after(w_down[512:], qkv_all)
+    down_pieces = [rest] + [shift(rest, "y", -o) for o in STEPS[1:]]
+
     pre_act = up_sum + shift(up_sent, "l", 1).astype(jnp.float32)
     activated = jax.nn.gelu(pre_act, approximate=False).astype(jnp.bfloat16)
 
     qkv_mine, qkv_theirs = project_again(index, features, qkv_all)
-
-    w_down = after(w_down, qkv_all)
-    after_w, before_w = after((shift(w_down, "y", -1), shift(w_down, "y", 1)), activated)
-    forward = before_w[:384], after_w[384:]
-    down = w_down, after_w, before_w, shift(forward[0], "y", 1), shift(forward[1], "y", -1)
-
-    got = after(shift(qkv_theirs, "l", 1), activated, *forward)
+    got = after(shift(qkv_theirs, "l", 1), activated)
     attended = attend(qkv_mine, got, q_gain, k_gain)
     attended_other = shift(attended, "l", 1)
-
-    def start_terms(block):
-        keep, send = output_terms(
-            index, block, attended, attended_other, activated, out_pieces, down
-        )
-        return keep, shift(send, "c", 1)
 
     def start_sums(keep, got):
         pair = [keep[o].astype(jnp.float32) + got[o].astype(jnp.float32) for o in range(4)]
@@ -300,10 +305,11 @@
         summed = pair[0] + f32(shift(up, "x", 1)) + f32(shift(down, "x", -1))
         return f32(move_z(summed.astype(jnp.bfloat16), pairs))
 
-    keep_a, got_a = start_terms(0)
-    keep_b, got_b = start_terms(1)
-    sums_a = start_sums(keep_a, got_a)
-    sums_b = start_sums(keep_b, got_b)
+    keep_a, send_a, keep_b, send_b = output_terms(
+        index, attended, attended_other, activated, down_all, out_pieces, down_pieces
+    )
+    sums_a = start_sums(keep_a, shift(send_a, "c", 1))
+    sums_b = start_sums(keep_b, shift(send_b, "c", 1))
     part_a = finish_sums(*sums_a, [(0, 1), (2, 0), (1, 3), (3, 2)])
     part_b = finish_sums(*sums_b, [(0, 0), (2, 1), (1, 2), (3, 3)])
     return (tokens.astype(jnp.float32) + part_a + part_b).astype(jnp.bfloat16)

time: 244 us -> 238 us (0.975)
  Pallas kernels: 52.2 us -> 45.2 us
  waiting for transfers between devices: 112 us -> 106 us
  other arithmetic: 13 us -> 16.6 us
  starting transfers between devices: 45.6 us -> 49 us
    ppermute x31, waiting for transfers between devices: 66.1 us -> 48.7 us  [shift(): lax.ppermute(value, axis, [(i, (i + by) % size) for i in range(size)])]
    pallas_call x4 -> x3, Pallas kernels: 48.7 us -> 41.6 us  [call(): pl.pallas_call(kernel, out_shape=outs, grid_spec=pltpu.PrefetchScalarGrid...]
    all_gather x0 -> x1, waiting for transfers between devices: none -> 7.02 us  [shards(): down_all = lax.all_gather(w_down[:512], 'y', axis=0)]
    ppermute x31, starting transfers between devices: 33.6 us -> 37 us  [shift(): lax.ppermute(value, axis, [(i, (i + by) % size) for i in range(size)])]
  transfers between devices with their start and end apart: 38 -> 39, of which waited for: 21 -> 18; matrix products, arithmetic and copies ran while one was open for 7% -> 8% of each run, Pallas kernels for 18% -> 14%
where the time goes in v4:
time: 238 us; the launch traced here: 237 us
  waiting for transfers between devices  106 us (45%)
  starting transfers between devices  49 us (21%)
  Pallas kernels  45.2 us (19%)
  other arithmetic  16.6 us (7%)
  between operations  13.6 us (6%)
  local copies, waits for them, and re-layouts  6.67 us (3%)
    ppermute x31, waiting for transfers between devices, shift(): lax.ppermute(value, axis, [(i, (i + by) % size) for i in range(size)])  48.7 us
    pallas_call x3, Pallas kernels, call(): pl.pallas_call(kernel, out_shape=outs, grid_spec=pltpu.PrefetchScalarGrid...  41.6 us
    ppermute x31, starting transfers between devices, shift(): lax.ppermute(value, axis, [(i, (i + by) % size) for i in range(size)])  37 us
    all_gather x1, waiting for transfers between devices, shards(): qkv_all = lax.all_gather(w_qkv.transpose(1, 0, 2), 'y', axis=0)  27.5 us
    ppermute x4, waiting for transfers between devices, move_z(): lax.ppermute(value, ('l', 'h'), [(place(s), place(d)) for s, d in pairs])  20.8 us
    ppermute x4, starting transfers between devices, move_z(): lax.ppermute(value, ('l', 'h'), [(place(s), place(d)) for s, d in pairs])  11.3 us
    convert_element_type x1, other arithmetic, shards(): activated = jax.nn.gelu(pre_act, approximate=False).astype(jnp.bfloat16)  7.84 us
    all_gather x1, waiting for transfers between devices, shards(): down_all = lax.all_gather(w_down[:512], 'y', axis=0)  7.02 us
  transfers between devices with their start and end apart: 39, of which 18 were waited for; matrix products, arithmetic and copies ran while one was open for 8% of the time, Pallas kernels for 14%

profile of v4, /device:TPU:32, one launch (start us, length us, event | category | flops | bytes accessed | tf_op | source)
XLA Modules:
  0.0 237.2 jit_solution(2828843395259989645)
XLA Ops:
  8.1 5.4 %collective-permute-start.1 = (bf16[512,384]{1,0:T(8,128)(2,1)}, bf16[512,384]{1,0:T(8,128)(2,1)S(1)}, u32[]{:S(2)}, u32[]{:S(2)}) collective-permute-start(bf16[512,384]{1,0:T(8,128)(2,1)} %param.8), channel_id=1, source_target_pairs={{0,0},{16,2},{2,16},{18,18},{1,1},{17,3},{3,17},{19,19},{4,4},{20,... | collective-permute-start | bytes 1179656 | tf_op jit(solution)/shard_map/ppermute | solution.py:28
  13.6 3.1 %collective-permute-start.2 = (bf16[256,768]{1,0:T(8,128)(2,1)}, bf16[256,768]{1,0:T(8,128)(2,1)S(1)}, u32[]{:S(2)}, u32[]{:S(2)}) collective-permute-start(bf16[256,768]{1,0:T(8,128)(2,1)} %refs_0_.1), channel_id=1, source_target_pairs={{0,96},{32,0},{64,32},{96,64},{1,97},{33,1},{65,33},{97,65},{2,98}... | collective-permute-start | bytes 1179656 | tf_op jit(solution)/shard_map/ppermute | solution.py:23
  16.7 4.1 %collective-permute-done = bf16[512,384]{1,0:T(8,128)(2,1)S(1)} collective-permute-done((bf16[512,384]{1,0:T(8,128)(2,1)}, bf16[512,384]{1,0:T(8,128)(2,1)S(1)}, u32[]{:S(2)}, u32[]{:S(2)}) %collective-permute-start) | collective-permute-done | bytes 393248 | tf_op jit(solution)/shard_map/ppermute | solution.py:28
  20.8 8.3 %collective-permute-done.1 = bf16[512,384]{1,0:T(8,128)(2,1)S(1)} collective-permute-done((bf16[512,384]{1,0:T(8,128)(2,1)}, bf16[512,384]{1,0:T(8,128)(2,1)S(1)}, u32[]{:S(2)}, u32[]{:S(2)}) %collective-permute-start.1) | collective-permute-done | bytes 393248 | tf_op jit(solution)/shard_map/ppermute | solution.py:28
  29.2 3.6 %collective-permute-done.3.refs_2_ = bf16[256,768]{1,0:T(8,128)(2,1)} collective-permute-done((bf16[256,768]{1,0:T(8,128)(2,1)}, bf16[256,768]{1,0:T(8,128)(2,1)}, u32[]{:S(2)}, u32[]{:S(2)}) %collective-permute-start.3) | collective-permute-done | bytes 393248 | tf_op jit(solution)/shard_map/ppermute | solution.py:23
  36.7 13.5 %collective-permute-done.5.refs_2_ = bf16[2,512,384]{2,1,0:T(8,128)(2,1)S(1)} collective-permute-done((bf16[2,512,384]{2,1,0:T(8,128)(2,1)S(1)}, bf16[2,512,384]{2,1,0:T(8,128)(2,1)S(1)}, u32[]{:S(2)}, u32[]{:S(2)}) %collective-permute-start.5) | collective-permute-done | bytes 786464 | tf_op jit(solution)/shard_map/ppermute | solution.py:23
  55.8 3.6 %collective-permute-done.6.refs_3_ = bf16[512,384]{1,0:T(8,128)(2,1)S(1)} collective-permute-done((bf16[512,384]{1,0:T(8,128)(2,1)S(1)}, bf16[512,384]{1,0:T(8,128)(2,1)S(1)}, u32[]{:S(2)}, u32[]{:S(2)}) %collective-permute-start.6) | collective-permute-done | bytes 393248 | tf_op jit(solution)/shard_map/ppermute | solution.py:23
  69.3 17.5 %shard_map.82 = (f32[2,512,768]{2,1,0:T(8,128)}, bf16[2,512,768]{2,1,0:T(8,128)(2,1)}, bf16[4,2,1024,384]{3,2,1,0:T(8,128)(2,1)}) custom-call(s32[6]{0:T(128)} %stack.67.index, bf16[2,512,384]{2,1,0:T(8,128)(2,1)} %copy-done, bf16[2,512,384]{2,1,0:T(8,128)(2,1)} %copy-done.2, bf16[2,512,384]{2,1,0:T(8,128)(2,1)} %copy-done.1, bf16[512,384]{1,0:T(8,128)(2,1)} %copy-done.4, ...), custom_call_target="tpu_custom_call" | custom-call | flops 4831838208 | bytes 22061056 | tf_op jit(solution)/shard_map/pallas_call | solution.py:96
  88.7 2.9 %collective-permute-start.16 = (bf16[128,768]{1,0:T(8,128)(2,1)S(1)}, bf16[128,768]{1,0:T(8,128)(2,1)S(1)}, u32[]{:S(2)}, u32[]{:S(2)}) collective-permute-start(bf16[128,768]{1,0:T(8,128)(2,1)S(1)} %slice.168), channel_id=1, source_target_pairs={{0,32},{32,64},{64,96},{96,0},{1,33},{33,65},{65,97},{97,1},{2,34}... | collective-permute-start | bytes 589832 | tf_op jit(solution)/shard_map/ppermute | solution.py:23
  95.1 27.5 %all-gather.9.cloned.1.call-done = bf16[12,768,256]{2,1,0:T(8,128)(2,1)} async-done(((bf16[3,768,256]{2,1,0:T(8,128)(2,1)}), bf16[12,768,256]{2,1,0:T(8,128)(2,1)}) %all-gather.9.cloned.1.call-update) | async-done | bytes 4718608 | tf_op jit(solution)/shard_map/all_gather | solution.py:261
  126.9 12.0 %shard_map.83 = (f32[512,768]{1,0:T(8,128)}, bf16[512,768]{1,0:T(8,128)(2,1)}) custom-call(s32[6]{0:T(128)} %stack.67.index, bf16[4,2,1024,384]{3,2,1,0:T(8,128)(2,1)} %get-tuple-element.21.block_ref, bf16[4,3,768,256]{3,2,1,0:T(8,128)(2,1)} %bitcast.184), custom_call_target="tpu_custom_call" | custom-call | flops 4831838208 | bytes 13369344 | tf_op jit(solution)/shard_map/pallas_call | solution.py:96
  139.7 7.8 %fusion.2.act_ref = bf16[2,512,768]{2,1,0:T(8,128)(2,1)} fusion(f32[2,512,768]{2,1,0:T(8,128)S(1)} %copy-done.3, bf16[2,512,768]{2,1,0:T(8,128)(2,1)S(1)} %collective-permute-done.19), kind=kLoop, calls=%fused_computation.3 | loop fusion | flops 52690944 | bytes 6291456 | tf_op jit(solution)/shard_map/convert_element_type | solution.py:289
  147.5 10.2 %collective-permute-done.18.got_ref = bf16[512,768]{1,0:T(8,128)(2,1)S(1)} collective-permute-done((bf16[512,768]{1,0:T(8,128)(2,1)}, bf16[512,768]{1,0:T(8,128)(2,1)S(1)}, u32[]{:S(2)}, u32[]{:S(2)}) %collective-permute-start.18) | collective-permute-done | bytes 786464 | tf_op jit(solution)/shard_map/ppermute | solution.py:23
  158.6 3.6 %shard_map.84.att_own = bf16[512,256]{1,0:T(8,128)(2,1)} custom-call(f32[512,768]{1,0:T(8,128)} %get-tuple-element.26.mine_ref, bf16[512,768]{1,0:T(8,128)(2,1)} %copy-done.8, f32[1,128]{1,0:T(1,128)} %bitcast.182, f32[1,128]{1,0:T(1,128)} %bitcast.183), custom_call_target="tpu_custom_call" | custom-call | flops 134217728 | bytes 2359296 | tf_op jit(solution)/shard_map/pallas_call | solution.py:182
  162.8 7.0 %all-gather.11.cloned.1.call-done = bf16[2048,768]{1,0:T(8,128)(2,1)} async-done(((bf16[512,768]{1,0:T(8,128)(2,1)}), bf16[2048,768]{1,0:T(8,128)(2,1)}) %all-gather.11.cloned.1.call-update) | async-done | bytes 3145744 | tf_op jit(solution)/shard_map/all_gather | solution.py:262
  171.0 12.1 %shard_map.85 = (bf16[4,512,384]{2,1,0:T(8,128)(2,1)}, bf16[4,512,384]{2,1,0:T(8,128)(2,1)}, bf16[4,512,384]{2,1,0:T(8,128)(2,1)}, bf16[4,512,384]{2,1,0:T(8,128)(2,1)}) custom-call(s32[6]{0:T(128)} %stack.67.index, bf16[512,256]{1,0:T(8,128)(2,1)} %shard_map.84.att_own, bf16[512,256]{1,0:T(8,128)(2,1)} %copy-done.24, bf16[2,512,768]{2,1,0:T(8,128)(2,1)} %fusion.2.act_ref, ...), custom_call_target="tpu_custom_call" | custom-call | flops 6442450944 | bytes 14680064 | tf_op jit(solution)/shard_map/pallas_call | solution.py:96
  183.7 3.1 %collective-permute-done.24 = bf16[4,512,384]{2,1,0:T(8,128)(2,1)S(1)} collective-permute-done((bf16[4,512,384]{2,1,0:T(8,128)(2,1)}, bf16[4,512,384]{2,1,0:T(8,128)(2,1)S(1)}, u32[]{:S(2)}, u32[]{:S(2)}) %collective-permute-start.24) | collective-permute-done | bytes 1572896 | tf_op jit(solution)/shard_map/ppermute | solution.py:23
  192.4 3.1 %collective-permute-start.33 = (bf16[256,384]{1,0:T(8,128)(2,1)S(1)}, bf16[256,384]{1,0:T(8,128)(2,1)S(1)}, u32[]{:S(2)}, u32[]{:S(2)}) collective-permute-start(bf16[256,384]{1,0:T(8,128)(2,1)S(1)} %get-tuple-element.46), channel_id=1, source_target_pairs={{0,12},{4,0},{8,4},{12,8},{1,13},{5,1},{9,5},{13,9},{2,14},{6,2},{... | collective-permute-start | bytes 589832 | tf_op jit(solution)/shard_map/ppermute | solution.py:23
  197.9 3.1 %collective-permute-start.28 = (bf16[512,384]{1,0:T(8,128)(2,1)S(1)}, bf16[512,384]{1,0:T(8,128)(2,1)S(1)}, u32[]{:S(2)}, u32[]{:S(2)}) collective-permute-start(bf16[512,384]{1,0:T(8,128)(2,1)S(1)} %pad_maximum_fusion.2), channel_id=1, source_target_pairs={{0,12},{4,0},{8,4},{12,8},{1,13},{5,1},{9,5},{13,9},{2,14},{6,2},{... | collective-permute-start | bytes 1179656 | tf_op jit(solution)/shard_map/ppermute | solution.py:23
  202.2 3.1 %collective-permute-start.34 = (bf16[512,384]{1,0:T(8,128)(2,1)S(1)}, bf16[512,384]{1,0:T(8,128)(2,1)S(1)}, u32[]{:S(2)}, u32[]{:S(2)}) collective-permute-start(bf16[512,384]{1,0:T(8,128)(2,1)S(1)} %pad_maximum_fusion.4), channel_id=1, source_target_pairs={{0,12},{4,0},{8,4},{12,8},{1,13},{5,1},{9,5},{13,9},{2,14},{6,2},{... | collective-permute-start | bytes 1179656 | tf_op jit(solution)/shard_map/ppermute | solution.py:23
  205.2 5.6 %collective-permute-done.26 = bf16[512,384]{1,0:T(8,128)(2,1)S(1)} collective-permute-done((bf16[512,384]{1,0:T(8,128)(2,1)S(1)}, bf16[512,384]{1,0:T(8,128)(2,1)S(1)}, u32[]{:S(2)}, u32[]{:S(2)}) %collective-permute-start.26) | collective-permute-done | bytes 393248 | tf_op jit(solution)/shard_map/ppermute | solution.py:23
  214.4 3.3 %collective-permute-done.32 = bf16[512,384]{1,0:T(8,128)(2,1)S(1)} collective-permute-done((bf16[512,384]{1,0:T(8,128)(2,1)S(1)}, bf16[512,384]{1,0:T(8,128)(2,1)S(1)}, u32[]{:S(2)}, u32[]{:S(2)}) %collective-permute-start.32) | collective-permute-done | bytes 393248 | tf_op jit(solution)/shard_map/ppermute | solution.py:23
  217.9 3.5 %collective-permute-start.35 = (bf16[512,384]{1,0:T(8,128)(2,1)S(1)}, bf16[512,384]{1,0:T(8,128)(2,1)S(1)}, u32[]{:S(2)}, u32[]{:S(2)}) collective-permute-start(bf16[512,384]{1,0:T(8,128)(2,1)S(1)} %fusion.21), channel_id=1, source_target_pairs={{0,0},{2,16},{16,2},{18,18},{1,1},{3,17},{17,3},{19,19},{4,4},{6,2... | collective-permute-start | bytes 1179656 | tf_op jit(solution)/shard_map/ppermute | solution.py:28
  221.4 8.4 %collective-permute-done.35 = bf16[512,384]{1,0:T(8,128)(2,1)S(1)} collective-permute-done((bf16[512,384]{1,0:T(8,128)(2,1)S(1)}, bf16[512,384]{1,0:T(8,128)(2,1)S(1)}, u32[]{:S(2)}, u32[]{:S(2)}) %collective-permute-start.35) | collective-permute-done | bytes 393248 | tf_op jit(solution)/shard_map/ppermute | solution.py:28
  (162 shorter events, 48.1 us)
Async XLA Ops:
  6.5 62.7 %all-gather.7.cloned.1.call-start = ((), (), s32[]{:S(2)}) async-start(), calls=%async_computation | async-start | bytes 5898240 | tf_op jit(solution)/shard_map/all_gather | solution.py:260
  7.3 115.4 %all-gather.9.cloned.1.call-start = ((), (), s32[]{:S(2)}) async-start(), calls=%async_computation.1 | async-start | bytes 5898240 | tf_op jit(solution)/shard_map/all_gather | solution.py:261
  8.0 161.8 %all-gather.11.cloned.1.call-start = ((), (), s32[]{:S(2)}) async-start(), calls=%async_computation.2 | async-start | bytes 3932160 | tf_op jit(solution)/shard_map/all_gather | solution.py:262
  8.1 12.7 %collective-permute-start = (bf16[512,384]{1,0:T(8,128)(2,1)}, bf16[512,384]{1,0:T(8,128)(2,1)S(1)}, u32[]{:S(2)}, u32[]{:S(2)}) collective-permute-start(bf16[512,384]{1,0:T(8,128)(2,1)} %param.8), channel_id=1, source_target_pairs={{16,0},{0,2},{18,16},{2,18},{17,1},{1,3},{19,17},{3,19},{20,4},{4,... | collective-permute-start | bytes 1179656 | tf_op jit(solution)/shard_map/ppermute | solution.py:28
  8.1 21.0 %collective-permute-start.1 = (bf16[512,384]{1,0:T(8,128)(2,1)}, bf16[512,384]{1,0:T(8,128)(2,1)S(1)}, u32[]{:S(2)}, u32[]{:S(2)}) collective-permute-start(bf16[512,384]{1,0:T(8,128)(2,1)} %param.8), channel_id=1, source_target_pairs={{0,0},{16,2},{2,16},{18,18},{1,1},{17,3},{3,17},{19,19},{4,4},{20,... | collective-permute-start | bytes 1179656 | tf_op jit(solution)/shard_map/ppermute | solution.py:28
  13.6 15.7 %collective-permute-start.2 = (bf16[256,768]{1,0:T(8,128)(2,1)}, bf16[256,768]{1,0:T(8,128)(2,1)S(1)}, u32[]{:S(2)}, u32[]{:S(2)}) collective-permute-start(bf16[256,768]{1,0:T(8,128)(2,1)} %refs_0_.1), channel_id=1, source_target_pairs={{0,96},{32,0},{64,32},{96,64},{1,97},{33,1},{65,33},{97,65},{2,98}... | collective-permute-start | bytes 1179656 | tf_op jit(solution)/shard_map/ppermute | solution.py:23
  16.7 16.1 %collective-permute-start.3 = (bf16[256,768]{1,0:T(8,128)(2,1)}, bf16[256,768]{1,0:T(8,128)(2,1)}, u32[]{:S(2)}, u32[]{:S(2)}) collective-permute-start(bf16[256,768]{1,0:T(8,128)(2,1)} %refs_0_.1), channel_id=1, source_target_pairs={{0,32},{32,64},{64,96},{96,0},{1,33},{33,65},{65,97},{97,1},{2,34}... | collective-permute-start | bytes 1179656 | tf_op jit(solution)/shard_map/ppermute | solution.py:23
  32.8 17.5 %collective-permute-start.5 = (bf16[2,512,384]{2,1,0:T(8,128)(2,1)S(1)}, bf16[2,512,384]{2,1,0:T(8,128)(2,1)S(1)}, u32[]{:S(2)}, u32[]{:S(2)}) collective-permute-start(bf16[2,512,384]{2,1,0:T(8,128)(2,1)S(1)} %pad_maximum_fusion.refs_0_), channel_id=1, source_target_pairs={{0,4},{4,8},{8,12},{12,0},{1,5},{5,9},{9,13},{13,1},{2,6},{6,10},{... | collective-permute-start | bytes 2359304 | tf_op jit(solution)/shard_map/ppermute | solution.py:23
  34.3 17.6 %collective-permute-start.4 = (bf16[2,512,384]{2,1,0:T(8,128)(2,1)S(1)}, bf16[2,512,384]{2,1,0:T(8,128)(2,1)S(1)}, u32[]{:S(2)}, u32[]{:S(2)}) collective-permute-start(bf16[2,512,384]{2,1,0:T(8,128)(2,1)S(1)} %pad_maximum_fusion.refs_0_), channel_id=1, source_target_pairs={{0,12},{4,0},{8,4},{12,8},{1,13},{5,1},{9,5},{13,9},{2,14},{6,2},{... | collective-permute-start | bytes 2359304 | tf_op jit(solution)/shard_map/ppermute | solution.py:23
  36.0 33.2 %collective-permute-start.8 = (bf16[2,512,384]{2,1,0:T(8,128)(2,1)S(1)}, bf16[2,512,384]{2,1,0:T(8,128)(2,1)}, u32[]{:S(2)}, u32[]{:S(2)}) collective-permute-start(bf16[2,512,384]{2,1,0:T(8,128)(2,1)S(1)} %pad_maximum_fusion.refs_0_), channel_id=1, source_target_pairs={{0,1},{1,0},{2,3},{3,2},{4,5},{5,4},{6,7},{7,6},{8,9},{9,8},{10,11... | collective-permute-start | bytes 2359304 | tf_op jit(solution)/shard_map/ppermute | solution.py:23
  54.2 15.0 %collective-permute-start.10 = (bf16[2,512,384]{2,1,0:T(8,128)(2,1)S(1)}, bf16[2,512,384]{2,1,0:T(8,128)(2,1)}, u32[]{:S(2)}, u32[]{:S(2)}) collective-permute-start(bf16[2,512,384]{2,1,0:T(8,128)(2,1)S(1)} %collective-permute-done.5.refs_2_), channel_id=1, source_target_pairs={{0,1},{1,0},{2,3},{3,2},{4,5},{5,4},{6,7},{7,6},{8,9},{9,8},{10,11... | collective-permute-start | bytes 2359304 | tf_op jit(solution)/shard_map/ppermute | solution.py:23
  54.3 14.9 %collective-permute-start.9 = (bf16[2,512,384]{2,1,0:T(8,128)(2,1)S(1)}, bf16[2,512,384]{2,1,0:T(8,128)(2,1)}, u32[]{:S(2)}, u32[]{:S(2)}) collective-permute-start(bf16[2,512,384]{2,1,0:T(8,128)(2,1)S(1)} %collective-permute-done.4.refs_1_), channel_id=1, source_target_pairs={{0,1},{1,0},{2,3},{3,2},{4,5},{5,4},{6,7},{7,6},{8,9},{9,8},{10,11... | collective-permute-start | bytes 2359304 | tf_op jit(solution)/shard_map/ppermute | solution.py:23
  86.8 52.9 %collective-permute-start.19 = (bf16[2,512,768]{2,1,0:T(8,128)(2,1)}, bf16[2,512,768]{2,1,0:T(8,128)(2,1)S(1)}, u32[]{:S(2)}, u32[]{:S(2)}) collective-permute-start(bf16[2,512,768]{2,1,0:T(8,128)(2,1)} %get-tuple-element.28), channel_id=1, source_target_pairs={{0,16},{16,0},{1,17},{17,1},{2,18},{18,2},{3,19},{19,3},{4,20},{20... | collective-permute-start | bytes 4718600 | tf_op jit(solution)/shard_map/ppermute | solution.py:23
  88.7 34.0 %collective-permute-start.16 = (bf16[128,768]{1,0:T(8,128)(2,1)S(1)}, bf16[128,768]{1,0:T(8,128)(2,1)S(1)}, u32[]{:S(2)}, u32[]{:S(2)}) collective-permute-start(bf16[128,768]{1,0:T(8,128)(2,1)S(1)} %slice.168), channel_id=1, source_target_pairs={{0,32},{32,64},{64,96},{96,0},{1,33},{33,65},{65,97},{97,1},{2,34}... | collective-permute-start | bytes 589832 | tf_op jit(solution)/shard_map/ppermute | solution.py:23
  91.5 31.1 %collective-permute-start.17 = (bf16[128,768]{1,0:T(8,128)(2,1)S(1)}, bf16[128,768]{1,0:T(8,128)(2,1)S(1)}, u32[]{:S(2)}, u32[]{:S(2)}) collective-permute-start(bf16[128,768]{1,0:T(8,128)(2,1)S(1)} %slice.169), channel_id=1, source_target_pairs={{0,96},{32,0},{64,32},{96,64},{1,97},{33,1},{65,33},{97,65},{2,98}... | collective-permute-start | bytes 589832 | tf_op jit(solution)/shard_map/ppermute | solution.py:23
  122.7 47.1 %collective-permute-start.21 = (bf16[256,768]{1,0:T(8,128)(2,1)S(1)}, bf16[256,768]{1,0:T(8,128)(2,1)S(1)}, u32[]{:S(2)}, u32[]{:S(2)}) collective-permute-start(bf16[256,768]{1,0:T(8,128)(2,1)S(1)} %slice.171.refs_5_), channel_id=1, source_target_pairs={{0,96},{32,0},{64,32},{96,64},{1,97},{33,1},{65,33},{97,65},{2,98}... | collective-permute-start | bytes 1179656 | tf_op jit(solution)/shard_map/ppermute | solution.py:23
  123.9 45.9 %collective-permute-start.22 = (bf16[256,768]{1,0:T(8,128)(2,1)S(1)}, bf16[256,768]{1,0:T(8,128)(2,1)S(1)}, u32[]{:S(2)}, u32[]{:S(2)}) collective-permute-start(bf16[256,768]{1,0:T(8,128)(2,1)S(1)} %slice.171.refs_5_), channel_id=1, source_target_pairs={{0,32},{32,64},{64,96},{96,0},{1,33},{33,65},{65,97},{97,1},{2,34}... | collective-permute-start | bytes 1179656 | tf_op jit(solution)/shard_map/ppermute | solution.py:23
  124.8 45.0 %collective-permute-start.23 = (bf16[256,768]{1,0:T(8,128)(2,1)S(1)}, bf16[256,768]{1,0:T(8,128)(2,1)S(1)}, u32[]{:S(2)}, u32[]{:S(2)}) collective-permute-start(bf16[256,768]{1,0:T(8,128)(2,1)S(1)} %slice.171.refs_5_), channel_id=1, source_target_pairs={{0,64},{32,96},{64,0},{96,32},{1,65},{33,97},{65,1},{97,33},{2,66}... | collective-permute-start | bytes 1179656 | tf_op jit(solution)/shard_map/ppermute | solution.py:23
  138.9 18.9 %collective-permute-start.18 = (bf16[512,768]{1,0:T(8,128)(2,1)}, bf16[512,768]{1,0:T(8,128)(2,1)S(1)}, u32[]{:S(2)}, u32[]{:S(2)}) collective-permute-start(bf16[512,768]{1,0:T(8,128)(2,1)} %get-tuple-element.27), channel_id=1, source_target_pairs={{0,16},{16,0},{1,17},{17,1},{2,18},{18,2},{3,19},{19,3},{4,20},{20... | collective-permute-start | bytes 2359304 | tf_op jit(solution)/shard_map/ppermute | solution.py:23
  197.5 13.3 %collective-permute-start.26 = (bf16[512,384]{1,0:T(8,128)(2,1)S(1)}, bf16[512,384]{1,0:T(8,128)(2,1)S(1)}, u32[]{:S(2)}, u32[]{:S(2)}) collective-permute-start(bf16[512,384]{1,0:T(8,128)(2,1)S(1)} %pad_maximum_fusion.1), channel_id=1, source_target_pairs={{0,4},{4,8},{8,12},{12,0},{1,5},{5,9},{9,13},{13,1},{2,6},{6,10},{... | collective-permute-start | bytes 1179656 | tf_op jit(solution)/shard_map/ppermute | solution.py:23
  197.9 12.9 %collective-permute-start.28 = (bf16[512,384]{1,0:T(8,128)(2,1)S(1)}, bf16[512,384]{1,0:T(8,128)(2,1)S(1)}, u32[]{:S(2)}, u32[]{:S(2)}) collective-permute-start(bf16[512,384]{1,0:T(8,128)(2,1)S(1)} %pad_maximum_fusion.2), channel_id=1, source_target_pairs={{0,12},{4,0},{8,4},{12,8},{1,13},{5,1},{9,5},{13,9},{2,14},{6,2},{... | collective-permute-start | bytes 1179656 | tf_op jit(solution)/shard_map/ppermute | solution.py:23
  201.7 15.9 %collective-permute-start.32 = (bf16[512,384]{1,0:T(8,128)(2,1)S(1)}, bf16[512,384]{1,0:T(8,128)(2,1)S(1)}, u32[]{:S(2)}, u32[]{:S(2)}) collective-permute-start(bf16[512,384]{1,0:T(8,128)(2,1)S(1)} %pad_maximum_fusion.3), channel_id=1, source_target_pairs={{0,4},{4,8},{8,12},{12,0},{1,5},{5,9},{9,13},{13,1},{2,6},{6,10},{... | collective-permute-start | bytes 1179656 | tf_op jit(solution)/shard_map/ppermute | solution.py:23
  202.2 15.5 %collective-permute-start.34 = (bf16[512,384]{1,0:T(8,128)(2,1)S(1)}, bf16[512,384]{1,0:T(8,128)(2,1)S(1)}, u32[]{:S(2)}, u32[]{:S(2)}) collective-permute-start(bf16[512,384]{1,0:T(8,128)(2,1)S(1)} %pad_maximum_fusion.4), channel_id=1, source_target_pairs={{0,12},{4,0},{8,4},{12,8},{1,13},{5,1},{9,5},{13,9},{2,14},{6,2},{... | collective-permute-start | bytes 1179656 | tf_op jit(solution)/shard_map/ppermute | solution.py:23
  217.9 11.9 %collective-permute-start.35 = (bf16[512,384]{1,0:T(8,128)(2,1)S(1)}, bf16[512,384]{1,0:T(8,128)(2,1)S(1)}, u32[]{:S(2)}, u32[]{:S(2)}) collective-permute-start(bf16[512,384]{1,0:T(8,128)(2,1)S(1)} %fusion.21), channel_id=1, source_target_pairs={{0,0},{2,16},{16,2},{18,18},{1,1},{3,17},{17,3},{19,19},{4,4},{6,2... | collective-permute-start | bytes 1179656 | tf_op jit(solution)/shard_map/ppermute | solution.py:28
  (42 other events, 433.6 us)
Sparse Core Ops, SparseCore 0:
  9.0 57.3 all-gather.6
  68.1 54.5 all-gather.8
  124.3 45.4 all-gather.10

commit v5 on v4

--- a/solution.py
+++ b/solution.py
@@ -90,7 +90,7 @@
         theirs_ref[...] = acc_ref[1 - slot].astype(jnp.bfloat16)
 
 
-def call(kernel, index, arrays, specs, outs, out_specs, scratch, flops):
+def call(kernel, index, arrays, specs, outs, out_specs, scratch, flops, vmem=VMEM_LIMIT):
     size = lambda a: math.prod(a.shape) * a.dtype.itemsize
     whole = lambda a: pl.BlockSpec(a.shape, lambda j, i, n=len(a.shape): (0,) * n)
     return pl.pallas_call(
@@ -103,7 +103,7 @@
             out_specs=[spec or whole(a) for a, spec in zip(outs, out_specs)],
             scratch_shapes=scratch,
         ),
-        compiler_params=pltpu.CompilerParams(vmem_limit_bytes=VMEM_LIMIT),
+        compiler_params=pltpu.CompilerParams(vmem_limit_bytes=vmem),
         cost_estimate=pl.CostEstimate(
             flops=flops,
             bytes_accessed=sum(map(size, arrays)) + sum(map(size, outs)),
@@ -203,14 +203,22 @@
                 w_ref[:256] = w_out[j][...]
             w_ref[256:] = w_rest[j][...]
 
+    own_first = index[1] == 0
+    att = jnp.concatenate(
+        [
+            jnp.where(own_first, att_own[...], att_other[...]),
+            jnp.where(own_first, att_other[...], att_own[...]),
+        ]
+    )
+    act = act_ref[...].reshape(1024, ROWS)
+    term = jnp.dot(act[:, :512], w_down[0], preferred_element_type=jnp.float32)
+    mixed = jnp.concatenate([att, act[:, 512:]], axis=1)
+    term += jnp.dot(mixed, w_ref[...], preferred_element_type=jnp.float32)
+    term = term.astype(jnp.bfloat16)
     for block in range(2):
-        att = jnp.where(index[1] == block, att_own[...], att_other[...])
-        term = jnp.dot(act_ref[block, :, :512], w_down[0], preferred_element_type=jnp.float32)
-        mixed = jnp.concatenate([att, act_ref[block, :, 512:]], axis=1)
-        term += jnp.dot(mixed, w_ref[...], preferred_element_type=jnp.float32)
-        term = term.astype(jnp.bfloat16)
-        outs[2 * block][0] = jnp.where(first, term[:, :384], term[:, 384:])
-        outs[2 * block + 1][0] = jnp.where(first, term[:, 384:], term[:, :384])
+        part = term[block * 512 : (block + 1) * 512]
+        outs[2 * block][0] = jnp.where(first, part[:, :384], part[:, 384:])
+        outs[2 * block + 1][0] = jnp.where(first, part[:, 384:], part[:, :384])
 
 
 def output_terms(index, att_own, att_other, activated, w_down, w_out, w_rest):
@@ -225,6 +233,7 @@
         [out_spec] * 4,
         [pltpu.VMEM((512, ROWS), jnp.bfloat16)],
         2 * 1024 * 1024 * 4 * ROWS,
+        vmem=50 << 20,
     )
 
 

time: 238 us -> 236 us (level)
  other arithmetic: 16.6 us -> 19.6 us
  transfers between devices with their start and end apart: 39 -> 39, of which waited for: 18 -> 18; matrix products, arithmetic and copies ran while one was open for 8% -> 9% of each run, Pallas kernels for 14% -> 14%
where the time goes in v5:
time: 236 us
  waiting for transfers between devices  104 us (44%)
  starting transfers between devices  48.9 us (21%)
  Pallas kernels  44.1 us (19%)
  other arithmetic  19.6 us (8%)
  between operations  13.6 us (6%)
  local copies, waits for them, and re-layouts  5.45 us (2%)
    ppermute x31, waiting for transfers between devices, shift(): lax.ppermute(value, axis, [(i, (i + by) % size) for i in range(size)])  47.7 us
    pallas_call x3, Pallas kernels, call(): pl.pallas_call(kernel, out_shape=outs, grid_spec=pltpu.PrefetchScalarGrid...  40.5 us
    ppermute x31, starting transfers between devices, shift(): lax.ppermute(value, axis, [(i, (i + by) % size) for i in range(size)])  36.8 us
    all_gather x1, waiting for transfers between devices, shards(): qkv_all = lax.all_gather(w_qkv.transpose(1, 0, 2), 'y', axis=0)  26.4 us
    ppermute x4, waiting for transfers between devices, move_z(): lax.ppermute(value, ('l', 'h'), [(place(s), place(d)) for s, d in pairs])  20.9 us
    ppermute x4, starting transfers between devices, move_z(): lax.ppermute(value, ('l', 'h'), [(place(s), place(d)) for s, d in pairs])  11.3 us
    convert_element_type x1, other arithmetic, shards(): activated = jax.nn.gelu(pre_act, approximate=False).astype(jnp.bfloat16)  8.83 us
    all_gather x1, waiting for transfers between devices, shards(): down_all = lax.all_gather(w_down[:512], 'y', axis=0)  7.23 us
  transfers between devices with their start and end apart: 39, of which 18 were waited for; matrix products, arithmetic and copies ran while one was open for 9% of the time, Pallas kernels for 14%

profile of v5, /device:TPU:32, one launch (start us, length us, event | category | flops | bytes accessed | tf_op | source)
XLA Modules:
  0.0 235.7 jit_solution(11428728772983878337)
XLA Ops:
  8.1 5.4 %collective-permute-start.1 = (bf16[512,384]{1,0:T(8,128)(2,1)}, bf16[512,384]{1,0:T(8,128)(2,1)S(1)}, u32[]{:S(2)}, u32[]{:S(2)}) collective-permute-start(bf16[512,384]{1,0:T(8,128)(2,1)} %param.8), channel_id=1, source_target_pairs={{0,0},{16,2},{2,16},{18,18},{1,1},{17,3},{3,17},{19,19},{4,4},{20,... | collective-permute-start | bytes 1179656 | tf_op jit(solution)/shard_map/ppermute | solution.py:28
  13.6 3.1 %collective-permute-start.2 = (bf16[256,768]{1,0:T(8,128)(2,1)}, bf16[256,768]{1,0:T(8,128)(2,1)S(1)}, u32[]{:S(2)}, u32[]{:S(2)}) collective-permute-start(bf16[256,768]{1,0:T(8,128)(2,1)} %refs_0_.1), channel_id=1, source_target_pairs={{0,96},{32,0},{64,32},{96,64},{1,97},{33,1},{65,33},{97,65},{2,98}... | collective-permute-start | bytes 1179656 | tf_op jit(solution)/shard_map/ppermute | solution.py:23
  16.7 4.1 %collective-permute-done = bf16[512,384]{1,0:T(8,128)(2,1)S(1)} collective-permute-done((bf16[512,384]{1,0:T(8,128)(2,1)}, bf16[512,384]{1,0:T(8,128)(2,1)S(1)}, u32[]{:S(2)}, u32[]{:S(2)}) %collective-permute-start) | collective-permute-done | bytes 393248 | tf_op jit(solution)/shard_map/ppermute | solution.py:28
  20.8 8.3 %collective-permute-done.1 = bf16[512,384]{1,0:T(8,128)(2,1)S(1)} collective-permute-done((bf16[512,384]{1,0:T(8,128)(2,1)}, bf16[512,384]{1,0:T(8,128)(2,1)S(1)}, u32[]{:S(2)}, u32[]{:S(2)}) %collective-permute-start.1) | collective-permute-done | bytes 393248 | tf_op jit(solution)/shard_map/ppermute | solution.py:28
  29.2 3.5 %collective-permute-done.3.refs_2_ = bf16[256,768]{1,0:T(8,128)(2,1)S(1)} collective-permute-done((bf16[256,768]{1,0:T(8,128)(2,1)}, bf16[256,768]{1,0:T(8,128)(2,1)S(1)}, u32[]{:S(2)}, u32[]{:S(2)}) %collective-permute-start.3) | collective-permute-done | bytes 393248 | tf_op jit(solution)/shard_map/ppermute | solution.py:23
  36.6 13.5 %collective-permute-done.5.refs_2_ = bf16[2,512,384]{2,1,0:T(8,128)(2,1)S(1)} collective-permute-done((bf16[2,512,384]{2,1,0:T(8,128)(2,1)S(1)}, bf16[2,512,384]{2,1,0:T(8,128)(2,1)S(1)}, u32[]{:S(2)}, u32[]{:S(2)}) %collective-permute-start.5) | collective-permute-done | bytes 786464 | tf_op jit(solution)/shard_map/ppermute | solution.py:23
  55.7 3.6 %collective-permute-done.6.refs_3_ = bf16[512,384]{1,0:T(8,128)(2,1)S(1)} collective-permute-done((bf16[512,384]{1,0:T(8,128)(2,1)S(1)}, bf16[512,384]{1,0:T(8,128)(2,1)S(1)}, u32[]{:S(2)}, u32[]{:S(2)}) %collective-permute-start.6) | collective-permute-done | bytes 393248 | tf_op jit(solution)/shard_map/ppermute | solution.py:23
  70.8 17.6 %shard_map.82 = (f32[2,512,768]{2,1,0:T(8,128)}, bf16[2,512,768]{2,1,0:T(8,128)(2,1)}, bf16[4,2,1024,384]{3,2,1,0:T(8,128)(2,1)}) custom-call(s32[6]{0:T(128)} %stack.67.index, bf16[2,512,384]{2,1,0:T(8,128)(2,1)} %copy-done.3, bf16[2,512,384]{2,1,0:T(8,128)(2,1)} %copy-done.5, bf16[2,512,384]{2,1,0:T(8,128)(2,1)} %copy-done.4, bf16[512,384]{1,0:T(8,128)(2,1)} %copy-done.7, ...), custom_call_target="tpu_custom_call" | custom-call | flops 4831838208 | bytes 22061056 | tf_op jit(solution)/shard_map/pallas_call | solution.py:96
  89.4 3.7 %collective-permute-start.16 = (bf16[128,768]{1,0:T(8,128)(2,1)S(1)}, bf16[128,768]{1,0:T(8,128)(2,1)S(1)}, u32[]{:S(2)}, u32[]{:S(2)}) collective-permute-start(bf16[128,768]{1,0:T(8,128)(2,1)S(1)} %slice.168), channel_id=1, source_target_pairs={{0,32},{32,64},{64,96},{96,0},{1,33},{33,65},{65,97},{97,1},{2,34}... | collective-permute-start | bytes 589832 | tf_op jit(solution)/shard_map/ppermute | solution.py:23
  96.3 26.4 %all-gather.9.cloned.1.call-done = bf16[12,768,256]{2,1,0:T(8,128)(2,1)} async-done(((bf16[3,768,256]{2,1,0:T(8,128)(2,1)}), bf16[12,768,256]{2,1,0:T(8,128)(2,1)}) %all-gather.9.cloned.1.call-update) | async-done | bytes 4718608 | tf_op jit(solution)/shard_map/all_gather | solution.py:270
  126.8 11.9 %shard_map.83 = (f32[512,768]{1,0:T(8,128)}, bf16[512,768]{1,0:T(8,128)(2,1)}) custom-call(s32[6]{0:T(128)} %stack.67.index, bf16[4,2,1024,384]{3,2,1,0:T(8,128)(2,1)} %get-tuple-element.21.block_ref, bf16[4,3,768,256]{3,2,1,0:T(8,128)(2,1)} %bitcast.184), custom_call_target="tpu_custom_call" | custom-call | flops 4831838208 | bytes 13369344 | tf_op jit(solution)/shard_map/pallas_call | solution.py:96
  139.4 8.8 %fusion.2.act_ref = bf16[2,512,768]{2,1,0:T(8,128)(2,1)} fusion(f32[2,512,768]{2,1,0:T(8,128)S(1)} %copy-done.6, bf16[2,512,768]{2,1,0:T(8,128)(2,1)} %collective-permute-done.19), kind=kLoop, calls=%fused_computation.3 | loop fusion | flops 52690944 | bytes 6291456 | tf_op jit(solution)/shard_map/convert_element_type | solution.py:298
  148.3 9.2 %collective-permute-done.18.got_ref = bf16[512,768]{1,0:T(8,128)(2,1)S(1)} collective-permute-done((bf16[512,768]{1,0:T(8,128)(2,1)}, bf16[512,768]{1,0:T(8,128)(2,1)S(1)}, u32[]{:S(2)}, u32[]{:S(2)}) %collective-permute-start.18) | collective-permute-done | bytes 786464 | tf_op jit(solution)/shard_map/ppermute | solution.py:23
  158.4 3.6 %shard_map.84.att_own = bf16[512,256]{1,0:T(8,128)(2,1)} custom-call(f32[512,768]{1,0:T(8,128)} %get-tuple-element.26.mine_ref, bf16[512,768]{1,0:T(8,128)(2,1)} %copy-done.10, f32[1,128]{1,0:T(1,128)} %bitcast.182, f32[1,128]{1,0:T(1,128)} %bitcast.183), custom_call_target="tpu_custom_call" | custom-call | flops 134217728 | bytes 2359296 | tf_op jit(solution)/shard_map/pallas_call | solution.py:182
  162.5 7.2 %all-gather.11.cloned.1.call-done = bf16[2048,768]{1,0:T(8,128)(2,1)} async-done(((bf16[512,768]{1,0:T(8,128)(2,1)}), bf16[2048,768]{1,0:T(8,128)(2,1)}) %all-gather.11.cloned.1.call-update) | async-done | bytes 3145744 | tf_op jit(solution)/shard_map/all_gather | solution.py:271
  170.7 11.0 %shard_map.85 = (bf16[4,512,384]{2,1,0:T(8,128)(2,1)}, bf16[4,512,384]{2,1,0:T(8,128)(2,1)}, bf16[4,512,384]{2,1,0:T(8,128)(2,1)}, bf16[4,512,384]{2,1,0:T(8,128)(2,1)}) custom-call(s32[6]{0:T(128)S(1)} %copy-done.1, bf16[512,256]{1,0:T(8,128)(2,1)S(1)} %copy-done, bf16[512,256]{1,0:T(8,128)(2,1)S(1)} %collective-permute-done.20.att_other, ...), custom_call_target="tpu_custom_call" | custom-call | flops 6442450944 | bytes 14680064 | tf_op jit(solution)/shard_map/pallas_call | solution.py:96
  182.2 3.1 %collective-permute-done.24 = bf16[4,512,384]{2,1,0:T(8,128)(2,1)S(1)} collective-permute-done((bf16[4,512,384]{2,1,0:T(8,128)(2,1)}, bf16[4,512,384]{2,1,0:T(8,128)(2,1)S(1)}, u32[]{:S(2)}, u32[]{:S(2)}) %collective-permute-start.24) | collective-permute-done | bytes 1572896 | tf_op jit(solution)/shard_map/ppermute | solution.py:23
  191.0 3.0 %collective-permute-start.33 = (bf16[256,384]{1,0:T(8,128)(2,1)S(1)}, bf16[256,384]{1,0:T(8,128)(2,1)S(1)}, u32[]{:S(2)}, u32[]{:S(2)}) collective-permute-start(bf16[256,384]{1,0:T(8,128)(2,1)S(1)} %get-tuple-element.46), channel_id=1, source_target_pairs={{0,12},{4,0},{8,4},{12,8},{1,13},{5,1},{9,5},{13,9},{2,14},{6,2},{... | collective-permute-start | bytes 589832 | tf_op jit(solution)/shard_map/ppermute | solution.py:23
  196.5 3.0 %collective-permute-start.28 = (bf16[512,384]{1,0:T(8,128)(2,1)S(1)}, bf16[512,384]{1,0:T(8,128)(2,1)S(1)}, u32[]{:S(2)}, u32[]{:S(2)}) collective-permute-start(bf16[512,384]{1,0:T(8,128)(2,1)S(1)} %pad_maximum_fusion.2), channel_id=1, source_target_pairs={{0,12},{4,0},{8,4},{12,8},{1,13},{5,1},{9,5},{13,9},{2,14},{6,2},{... | collective-permute-start | bytes 1179656 | tf_op jit(solution)/shard_map/ppermute | solution.py:23
  200.7 3.0 %collective-permute-start.34 = (bf16[512,384]{1,0:T(8,128)(2,1)S(1)}, bf16[512,384]{1,0:T(8,128)(2,1)S(1)}, u32[]{:S(2)}, u32[]{:S(2)}) collective-permute-start(bf16[512,384]{1,0:T(8,128)(2,1)S(1)} %pad_maximum_fusion.4), channel_id=1, source_target_pairs={{0,12},{4,0},{8,4},{12,8},{1,13},{5,1},{9,5},{13,9},{2,14},{6,2},{... | collective-permute-start | bytes 1179656 | tf_op jit(solution)/shard_map/ppermute | solution.py:23
  203.7 5.6 %collective-permute-done.26 = bf16[512,384]{1,0:T(8,128)(2,1)S(1)} collective-permute-done((bf16[512,384]{1,0:T(8,128)(2,1)S(1)}, bf16[512,384]{1,0:T(8,128)(2,1)S(1)}, u32[]{:S(2)}, u32[]{:S(2)}) %collective-permute-start.26) | collective-permute-done | bytes 393248 | tf_op jit(solution)/shard_map/ppermute | solution.py:23
  212.9 3.3 %collective-permute-done.32 = bf16[512,384]{1,0:T(8,128)(2,1)S(1)} collective-permute-done((bf16[512,384]{1,0:T(8,128)(2,1)S(1)}, bf16[512,384]{1,0:T(8,128)(2,1)S(1)}, u32[]{:S(2)}, u32[]{:S(2)}) %collective-permute-start.32) | collective-permute-done | bytes 393248 | tf_op jit(solution)/shard_map/ppermute | solution.py:23
  216.4 3.5 %collective-permute-start.35 = (bf16[512,384]{1,0:T(8,128)(2,1)S(1)}, bf16[512,384]{1,0:T(8,128)(2,1)S(1)}, u32[]{:S(2)}, u32[]{:S(2)}) collective-permute-start(bf16[512,384]{1,0:T(8,128)(2,1)S(1)} %fusion.21), channel_id=1, source_target_pairs={{0,0},{2,16},{16,2},{18,18},{1,1},{3,17},{17,3},{19,19},{4,4},{6,2... | collective-permute-start | bytes 1179656 | tf_op jit(solution)/shard_map/ppermute | solution.py:28
  219.9 8.4 %collective-permute-done.35 = bf16[512,384]{1,0:T(8,128)(2,1)S(1)} collective-permute-done((bf16[512,384]{1,0:T(8,128)(2,1)S(1)}, bf16[512,384]{1,0:T(8,128)(2,1)S(1)}, u32[]{:S(2)}, u32[]{:S(2)}) %collective-permute-start.35) | collective-permute-done | bytes 393248 | tf_op jit(solution)/shard_map/ppermute | solution.py:28
  (150 shorter events, 48.2 us)
Async XLA Ops:
  6.5 64.2 %all-gather.7.cloned.1.call-start = ((), (), s32[]{:S(2)}) async-start(), calls=%async_computation | async-start | bytes 5898240 | tf_op jit(solution)/shard_map/all_gather | solution.py:269
  7.3 115.4 %all-gather.9.cloned.1.call-start = ((), (), s32[]{:S(2)}) async-start(), calls=%async_computation.1 | async-start | bytes 5898240 | tf_op jit(solution)/shard_map/all_gather | solution.py:270
  8.0 161.7 %all-gather.11.cloned.1.call-start = ((), (), s32[]{:S(2)}) async-start(), calls=%async_computation.2 | async-start | bytes 3932160 | tf_op jit(solution)/shard_map/all_gather | solution.py:271
  8.1 12.7 %collective-permute-start = (bf16[512,384]{1,0:T(8,128)(2,1)}, bf16[512,384]{1,0:T(8,128)(2,1)S(1)}, u32[]{:S(2)}, u32[]{:S(2)}) collective-permute-start(bf16[512,384]{1,0:T(8,128)(2,1)} %param.8), channel_id=1, source_target_pairs={{16,0},{0,2},{18,16},{2,18},{17,1},{1,3},{19,17},{3,19},{20,4},{4,... | collective-permute-start | bytes 1179656 | tf_op jit(solution)/shard_map/ppermute | solution.py:28
  8.1 21.0 %collective-permute-start.1 = (bf16[512,384]{1,0:T(8,128)(2,1)}, bf16[512,384]{1,0:T(8,128)(2,1)S(1)}, u32[]{:S(2)}, u32[]{:S(2)}) collective-permute-start(bf16[512,384]{1,0:T(8,128)(2,1)} %param.8), channel_id=1, source_target_pairs={{0,0},{16,2},{2,16},{18,18},{1,1},{17,3},{3,17},{19,19},{4,4},{20,... | collective-permute-start | bytes 1179656 | tf_op jit(solution)/shard_map/ppermute | solution.py:28
  13.6 15.7 %collective-permute-start.2 = (bf16[256,768]{1,0:T(8,128)(2,1)}, bf16[256,768]{1,0:T(8,128)(2,1)S(1)}, u32[]{:S(2)}, u32[]{:S(2)}) collective-permute-start(bf16[256,768]{1,0:T(8,128)(2,1)} %refs_0_.1), channel_id=1, source_target_pairs={{0,96},{32,0},{64,32},{96,64},{1,97},{33,1},{65,33},{97,65},{2,98}... | collective-permute-start | bytes 1179656 | tf_op jit(solution)/shard_map/ppermute | solution.py:23
  16.7 16.0 %collective-permute-start.3 = (bf16[256,768]{1,0:T(8,128)(2,1)}, bf16[256,768]{1,0:T(8,128)(2,1)S(1)}, u32[]{:S(2)}, u32[]{:S(2)}) collective-permute-start(bf16[256,768]{1,0:T(8,128)(2,1)} %refs_0_.1), channel_id=1, source_target_pairs={{0,32},{32,64},{64,96},{96,0},{1,33},{33,65},{65,97},{97,1},{2,34}... | collective-permute-start | bytes 1179656 | tf_op jit(solution)/shard_map/ppermute | solution.py:23
  32.7 17.5 %collective-permute-start.5 = (bf16[2,512,384]{2,1,0:T(8,128)(2,1)S(1)}, bf16[2,512,384]{2,1,0:T(8,128)(2,1)S(1)}, u32[]{:S(2)}, u32[]{:S(2)}) collective-permute-start(bf16[2,512,384]{2,1,0:T(8,128)(2,1)S(1)} %pad_maximum_fusion.refs_0_), channel_id=1, source_target_pairs={{0,4},{4,8},{8,12},{12,0},{1,5},{5,9},{9,13},{13,1},{2,6},{6,10},{... | collective-permute-start | bytes 2359304 | tf_op jit(solution)/shard_map/ppermute | solution.py:23
  34.2 17.6 %collective-permute-start.4 = (bf16[2,512,384]{2,1,0:T(8,128)(2,1)S(1)}, bf16[2,512,384]{2,1,0:T(8,128)(2,1)S(1)}, u32[]{:S(2)}, u32[]{:S(2)}) collective-permute-start(bf16[2,512,384]{2,1,0:T(8,128)(2,1)S(1)} %pad_maximum_fusion.refs_0_), channel_id=1, source_target_pairs={{0,12},{4,0},{8,4},{12,8},{1,13},{5,1},{9,5},{13,9},{2,14},{6,2},{... | collective-permute-start | bytes 2359304 | tf_op jit(solution)/shard_map/ppermute | solution.py:23
  35.9 34.8 %collective-permute-start.8 = (bf16[2,512,384]{2,1,0:T(8,128)(2,1)S(1)}, bf16[2,512,384]{2,1,0:T(8,128)(2,1)}, u32[]{:S(2)}, u32[]{:S(2)}) collective-permute-start(bf16[2,512,384]{2,1,0:T(8,128)(2,1)S(1)} %pad_maximum_fusion.refs_0_), channel_id=1, source_target_pairs={{0,1},{1,0},{2,3},{3,2},{4,5},{5,4},{6,7},{7,6},{8,9},{9,8},{10,11... | collective-permute-start | bytes 2359304 | tf_op jit(solution)/shard_map/ppermute | solution.py:23
  54.1 16.6 %collective-permute-start.10 = (bf16[2,512,384]{2,1,0:T(8,128)(2,1)S(1)}, bf16[2,512,384]{2,1,0:T(8,128)(2,1)}, u32[]{:S(2)}, u32[]{:S(2)}) collective-permute-start(bf16[2,512,384]{2,1,0:T(8,128)(2,1)S(1)} %collective-permute-done.5.refs_2_), channel_id=1, source_target_pairs={{0,1},{1,0},{2,3},{3,2},{4,5},{5,4},{6,7},{7,6},{8,9},{9,8},{10,11... | collective-permute-start | bytes 2359304 | tf_op jit(solution)/shard_map/ppermute | solution.py:23
  54.2 16.5 %collective-permute-start.9 = (bf16[2,512,384]{2,1,0:T(8,128)(2,1)S(1)}, bf16[2,512,384]{2,1,0:T(8,128)(2,1)}, u32[]{:S(2)}, u32[]{:S(2)}) collective-permute-start(bf16[2,512,384]{2,1,0:T(8,128)(2,1)S(1)} %collective-permute-done.4.refs_1_), channel_id=1, source_target_pairs={{0,1},{1,0},{2,3},{3,2},{4,5},{5,4},{6,7},{7,6},{8,9},{9,8},{10,11... | collective-permute-start | bytes 2359304 | tf_op jit(solution)/shard_map/ppermute | solution.py:23
  88.3 51.1 %collective-permute-start.19 = (bf16[2,512,768]{2,1,0:T(8,128)(2,1)}, bf16[2,512,768]{2,1,0:T(8,128)(2,1)}, u32[]{:S(2)}, u32[]{:S(2)}) collective-permute-start(bf16[2,512,768]{2,1,0:T(8,128)(2,1)} %get-tuple-element.28), channel_id=1, source_target_pairs={{0,16},{16,0},{1,17},{17,1},{2,18},{18,2},{3,19},{19,3},{4,20},{20... | collective-permute-start | bytes 4718600 | tf_op jit(solution)/shard_map/ppermute | solution.py:23
  89.4 33.2 %collective-permute-start.16 = (bf16[128,768]{1,0:T(8,128)(2,1)S(1)}, bf16[128,768]{1,0:T(8,128)(2,1)S(1)}, u32[]{:S(2)}, u32[]{:S(2)}) collective-permute-start(bf16[128,768]{1,0:T(8,128)(2,1)S(1)} %slice.168), channel_id=1, source_target_pairs={{0,32},{32,64},{64,96},{96,0},{1,33},{33,65},{65,97},{97,1},{2,34}... | collective-permute-start | bytes 589832 | tf_op jit(solution)/shard_map/ppermute | solution.py:23
  93.2 29.5 %collective-permute-start.17 = (bf16[128,768]{1,0:T(8,128)(2,1)S(1)}, bf16[128,768]{1,0:T(8,128)(2,1)S(1)}, u32[]{:S(2)}, u32[]{:S(2)}) collective-permute-start(bf16[128,768]{1,0:T(8,128)(2,1)S(1)} %slice.169), channel_id=1, source_target_pairs={{0,96},{32,0},{64,32},{96,64},{1,97},{33,1},{65,33},{97,65},{2,98}... | collective-permute-start | bytes 589832 | tf_op jit(solution)/shard_map/ppermute | solution.py:23
  122.7 47.1 %collective-permute-start.21 = (bf16[256,768]{1,0:T(8,128)(2,1)S(1)}, bf16[256,768]{1,0:T(8,128)(2,1)S(1)}, u32[]{:S(2)}, u32[]{:S(2)}) collective-permute-start(bf16[256,768]{1,0:T(8,128)(2,1)S(1)} %slice.171.refs_5_), channel_id=1, source_target_pairs={{0,96},{32,0},{64,32},{96,64},{1,97},{33,1},{65,33},{97,65},{2,98}... | collective-permute-start | bytes 1179656 | tf_op jit(solution)/shard_map/ppermute | solution.py:23
  123.8 45.9 %collective-permute-start.22 = (bf16[256,768]{1,0:T(8,128)(2,1)S(1)}, bf16[256,768]{1,0:T(8,128)(2,1)S(1)}, u32[]{:S(2)}, u32[]{:S(2)}) collective-permute-start(bf16[256,768]{1,0:T(8,128)(2,1)S(1)} %slice.171.refs_5_), channel_id=1, source_target_pairs={{0,32},{32,64},{64,96},{96,0},{1,33},{33,65},{65,97},{97,1},{2,34}... | collective-permute-start | bytes 1179656 | tf_op jit(solution)/shard_map/ppermute | solution.py:23
  124.7 45.0 %collective-permute-start.23 = (bf16[256,768]{1,0:T(8,128)(2,1)S(1)}, bf16[256,768]{1,0:T(8,128)(2,1)S(1)}, u32[]{:S(2)}, u32[]{:S(2)}) collective-permute-start(bf16[256,768]{1,0:T(8,128)(2,1)S(1)} %slice.171.refs_5_), channel_id=1, source_target_pairs={{0,64},{32,96},{64,0},{96,32},{1,65},{33,97},{65,1},{97,33},{2,66}... | collective-permute-start | bytes 1179656 | tf_op jit(solution)/shard_map/ppermute | solution.py:23
  138.8 18.7 %collective-permute-start.18 = (bf16[512,768]{1,0:T(8,128)(2,1)}, bf16[512,768]{1,0:T(8,128)(2,1)S(1)}, u32[]{:S(2)}, u32[]{:S(2)}) collective-permute-start(bf16[512,768]{1,0:T(8,128)(2,1)} %get-tuple-element.27), channel_id=1, source_target_pairs={{0,16},{16,0},{1,17},{17,1},{2,18},{18,2},{3,19},{19,3},{4,20},{20... | collective-permute-start | bytes 2359304 | tf_op jit(solution)/shard_map/ppermute | solution.py:23
  196.0 13.3 %collective-permute-start.26 = (bf16[512,384]{1,0:T(8,128)(2,1)S(1)}, bf16[512,384]{1,0:T(8,128)(2,1)S(1)}, u32[]{:S(2)}, u32[]{:S(2)}) collective-permute-start(bf16[512,384]{1,0:T(8,128)(2,1)S(1)} %pad_maximum_fusion.1), channel_id=1, source_target_pairs={{0,4},{4,8},{8,12},{12,0},{1,5},{5,9},{9,13},{13,1},{2,6},{6,10},{... | collective-permute-start | bytes 1179656 | tf_op jit(solution)/shard_map/ppermute | solution.py:23
  196.5 12.9 %collective-permute-start.28 = (bf16[512,384]{1,0:T(8,128)(2,1)S(1)}, bf16[512,384]{1,0:T(8,128)(2,1)S(1)}, u32[]{:S(2)}, u32[]{:S(2)}) collective-permute-start(bf16[512,384]{1,0:T(8,128)(2,1)S(1)} %pad_maximum_fusion.2), channel_id=1, source_target_pairs={{0,12},{4,0},{8,4},{12,8},{1,13},{5,1},{9,5},{13,9},{2,14},{6,2},{... | collective-permute-start | bytes 1179656 | tf_op jit(solution)/shard_map/ppermute | solution.py:23
  200.3 15.9 %collective-permute-start.32 = (bf16[512,384]{1,0:T(8,128)(2,1)S(1)}, bf16[512,384]{1,0:T(8,128)(2,1)S(1)}, u32[]{:S(2)}, u32[]{:S(2)}) collective-permute-start(bf16[512,384]{1,0:T(8,128)(2,1)S(1)} %pad_maximum_fusion.3), channel_id=1, source_target_pairs={{0,4},{4,8},{8,12},{12,0},{1,5},{5,9},{9,13},{13,1},{2,6},{6,10},{... | collective-permute-start | bytes 1179656 | tf_op jit(solution)/shard_map/ppermute | solution.py:23
  200.7 15.5 %collective-permute-start.34 = (bf16[512,384]{1,0:T(8,128)(2,1)S(1)}, bf16[512,384]{1,0:T(8,128)(2,1)S(1)}, u32[]{:S(2)}, u32[]{:S(2)}) collective-permute-start(bf16[512,384]{1,0:T(8,128)(2,1)S(1)} %pad_maximum_fusion.4), channel_id=1, source_target_pairs={{0,12},{4,0},{8,4},{12,8},{1,13},{5,1},{9,5},{13,9},{2,14},{6,2},{... | collective-permute-start | bytes 1179656 | tf_op jit(solution)/shard_map/ppermute | solution.py:23
  216.4 11.9 %collective-permute-start.35 = (bf16[512,384]{1,0:T(8,128)(2,1)S(1)}, bf16[512,384]{1,0:T(8,128)(2,1)S(1)}, u32[]{:S(2)}, u32[]{:S(2)}) collective-permute-start(bf16[512,384]{1,0:T(8,128)(2,1)S(1)} %fusion.21), channel_id=1, source_target_pairs={{0,0},{2,16},{16,2},{18,18},{1,1},{3,17},{17,3},{19,19},{4,4},{6,2... | collective-permute-start | bytes 1179656 | tf_op jit(solution)/shard_map/ppermute | solution.py:28
  (36 other events, 354.6 us)
Sparse Core Ops, SparseCore 0:
  9.0 57.3 all-gather.6
  68.1 54.5 all-gather.8
  124.3 45.3 all-gather.10

commit v6 on v5

--- a/solution.py
+++ b/solution.py
@@ -182,7 +182,7 @@
     return pl.pallas_call(
         attend_kernel,
         out_shape=jax.ShapeDtypeStruct((512, 256), jnp.bfloat16),
-        compiler_params=pltpu.CompilerParams(vmem_limit_bytes=VMEM_LIMIT),
+        compiler_params=pltpu.CompilerParams(vmem_limit_bytes=16 << 20),
         cost_estimate=pl.CostEstimate(
             flops=4 * 4 * 256 * 256 * 128, bytes_accessed=512 * 768 * 6, transcendentals=4 * 256 * 256
         ),

time: 236 us -> 236 us (level)
  waiting for transfers between devices: 104 us -> 109 us
  Pallas kernels: 44.1 us -> 41.6 us
    all_gather x1, waiting for transfers between devices: 26.4 us -> 30.2 us  [shards(): qkv_all = lax.all_gather(w_qkv.transpose(1, 0, 2), 'y', axis=0)]
    all_gather x1, waiting for transfers between devices: 7.23 us -> 10.2 us  [shards(): down_all = lax.all_gather(w_down[:512], 'y', axis=0)]
  transfers between devices with their start and end apart: 39 -> 39, of which waited for: 18 -> 18; matrix products, arithmetic and copies ran while one was open for 9% -> 9% of each run, Pallas kernels for 14% -> 13%
where the time goes in v6:
time: 236 us
  waiting for transfers between devices  109 us (46%)
  starting transfers between devices  47.9 us (20%)
  Pallas kernels  41.6 us (18%)
  other arithmetic  19.1 us (8%)
  between operations  13.6 us (6%)
  local copies, waits for them, and re-layouts  4.86 us (2%)
    ppermute x31, waiting for transfers between devices, shift(): lax.ppermute(value, axis, [(i, (i + by) % size) for i in range(size)])  45.5 us
    pallas_call x3, Pallas kernels, call(): pl.pallas_call(kernel, out_shape=outs, grid_spec=pltpu.PrefetchScalarGrid...  40.4 us
    ppermute x31, starting transfers between devices, shift(): lax.ppermute(value, axis, [(i, (i + by) % size) for i in range(size)])  35.9 us
    all_gather x1, waiting for transfers between devices, shards(): qkv_all = lax.all_gather(w_qkv.transpose(1, 0, 2), 'y', axis=0)  30.2 us
    ppermute x4, waiting for transfers between devices, move_z(): lax.ppermute(value, ('l', 'h'), [(place(s), place(d)) for s, d in pairs])  20.9 us
    ppermute x4, starting transfers between devices, move_z(): lax.ppermute(value, ('l', 'h'), [(place(s), place(d)) for s, d in pairs])  11.3 us
    all_gather x1, waiting for transfers between devices, shards(): down_all = lax.all_gather(w_down[:512], 'y', axis=0)  10.2 us
    convert_element_type x1, other arithmetic, shards(): activated = jax.nn.gelu(pre_act, approximate=False).astype(jnp.bfloat16)  8.81 us
  transfers between devices with their start and end apart: 39, of which 18 were waited for; matrix products, arithmetic and copies ran while one was open for 9% of the time, Pallas kernels for 13%

profile of v6, /device:TPU:32, one launch (start us, length us, event | category | flops | bytes accessed | tf_op | source)
XLA Modules:
  0.0 235.7 jit_solution(13537667858183831875)
XLA Ops:
  8.1 5.4 %collective-permute-start.1 = (bf16[512,384]{1,0:T(8,128)(2,1)}, bf16[512,384]{1,0:T(8,128)(2,1)S(1)}, u32[]{:S(2)}, u32[]{:S(2)}) collective-permute-start(bf16[512,384]{1,0:T(8,128)(2,1)} %param.8), channel_id=1, source_target_pairs={{0,0},{16,2},{2,16},{18,18},{1,1},{17,3},{3,17},{19,19},{4,4},{20,... | collective-permute-start | bytes 1179656 | tf_op jit(solution)/shard_map/ppermute | solution.py:28
  13.6 3.1 %collective-permute-start.2 = (bf16[256,768]{1,0:T(8,128)(2,1)}, bf16[256,768]{1,0:T(8,128)(2,1)S(1)}, u32[]{:S(2)}, u32[]{:S(2)}) collective-permute-start(bf16[256,768]{1,0:T(8,128)(2,1)} %refs_0_.1), channel_id=1, source_target_pairs={{0,96},{32,0},{64,32},{96,64},{1,97},{33,1},{65,33},{97,65},{2,98}... | collective-permute-start | bytes 1179656 | tf_op jit(solution)/shard_map/ppermute | solution.py:23
  16.7 4.1 %collective-permute-done = bf16[512,384]{1,0:T(8,128)(2,1)S(1)} collective-permute-done((bf16[512,384]{1,0:T(8,128)(2,1)}, bf16[512,384]{1,0:T(8,128)(2,1)S(1)}, u32[]{:S(2)}, u32[]{:S(2)}) %collective-permute-start) | collective-permute-done | bytes 393248 | tf_op jit(solution)/shard_map/ppermute | solution.py:28
  20.8 8.3 %collective-permute-done.1 = bf16[512,384]{1,0:T(8,128)(2,1)S(1)} collective-permute-done((bf16[512,384]{1,0:T(8,128)(2,1)}, bf16[512,384]{1,0:T(8,128)(2,1)S(1)}, u32[]{:S(2)}, u32[]{:S(2)}) %collective-permute-start.1) | collective-permute-done | bytes 393248 | tf_op jit(solution)/shard_map/ppermute | solution.py:28
  29.2 3.5 %collective-permute-done.3.refs_2_ = bf16[256,768]{1,0:T(8,128)(2,1)S(1)} collective-permute-done((bf16[256,768]{1,0:T(8,128)(2,1)}, bf16[256,768]{1,0:T(8,128)(2,1)S(1)}, u32[]{:S(2)}, u32[]{:S(2)}) %collective-permute-start.3) | collective-permute-done | bytes 393248 | tf_op jit(solution)/shard_map/ppermute | solution.py:23
  36.6 13.5 %collective-permute-done.5.refs_2_ = bf16[2,512,384]{2,1,0:T(8,128)(2,1)S(1)} collective-permute-done((bf16[2,512,384]{2,1,0:T(8,128)(2,1)S(1)}, bf16[2,512,384]{2,1,0:T(8,128)(2,1)S(1)}, u32[]{:S(2)}, u32[]{:S(2)}) %collective-permute-start.5) | collective-permute-done | bytes 786464 | tf_op jit(solution)/shard_map/ppermute | solution.py:23
  68.7 17.5 %shard_map.82 = (f32[2,512,768]{2,1,0:T(8,128)}, bf16[2,512,768]{2,1,0:T(8,128)(2,1)}, bf16[4,2,1024,384]{3,2,1,0:T(8,128)(2,1)}) custom-call(s32[6]{0:T(128)} %stack.67.index, bf16[2,512,384]{2,1,0:T(8,128)(2,1)} %copy-done.7, bf16[2,512,384]{2,1,0:T(8,128)(2,1)} %collective-permute-done.4.refs_1_, bf16[2,512,384]{2,1,0:T(8,128)(2,1)} %copy-done.8, ...), custom_call_target="tpu_custom_call" | custom-call | flops 4831838208 | bytes 22061056 | tf_op jit(solution)/shard_map/pallas_call | solution.py:96
  86.7 2.6 %collective-permute-start.16 = (bf16[128,768]{1,0:T(8,128)(2,1)S(1)}, bf16[128,768]{1,0:T(8,128)(2,1)S(1)}, u32[]{:S(2)}, u32[]{:S(2)}) collective-permute-start(bf16[128,768]{1,0:T(8,128)(2,1)S(1)} %slice.168), channel_id=1, source_target_pairs={{0,32},{32,64},{64,96},{96,0},{1,33},{33,65},{65,97},{97,1},{2,34}... | collective-permute-start | bytes 589832 | tf_op jit(solution)/shard_map/ppermute | solution.py:23
  92.5 30.2 %all-gather.9.cloned.1.call-done = bf16[12,768,256]{2,1,0:T(8,128)(2,1)} async-done(((bf16[3,768,256]{2,1,0:T(8,128)(2,1)}), bf16[12,768,256]{2,1,0:T(8,128)(2,1)}) %all-gather.9.cloned.1.call-update) | async-done | bytes 4718608 | tf_op jit(solution)/shard_map/all_gather | solution.py:270
  124.8 2.1 collective-permute-start.23
  126.9 11.9 %shard_map.83 = (f32[512,768]{1,0:T(8,128)}, bf16[512,768]{1,0:T(8,128)(2,1)}) custom-call(s32[6]{0:T(128)} %stack.67.index, bf16[4,2,1024,384]{3,2,1,0:T(8,128)(2,1)} %get-tuple-element.21.block_ref, bf16[4,3,768,256]{3,2,1,0:T(8,128)(2,1)} %bitcast.184), custom_call_target="tpu_custom_call" | custom-call | flops 4831838208 | bytes 13369344 | tf_op jit(solution)/shard_map/pallas_call | solution.py:96
  139.6 8.8 %fusion.2.act_ref = bf16[2,512,768]{2,1,0:T(8,128)(2,1)} fusion(f32[2,512,768]{2,1,0:T(8,128)S(1)} %copy-done.9, bf16[2,512,768]{2,1,0:T(8,128)(2,1)} %collective-permute-done.19), kind=kLoop, calls=%fused_computation.3 | loop fusion | flops 52690944 | bytes 6291456 | tf_op jit(solution)/shard_map/convert_element_type | solution.py:298
  148.5 9.3 %collective-permute-done.18.got_ref = bf16[512,768]{1,0:T(8,128)(2,1)S(1)} collective-permute-done((bf16[512,768]{1,0:T(8,128)(2,1)}, bf16[512,768]{1,0:T(8,128)(2,1)S(1)}, u32[]{:S(2)}, u32[]{:S(2)}) %collective-permute-start.18) | collective-permute-done | bytes 786464 | tf_op jit(solution)/shard_map/ppermute | solution.py:23
  159.6 10.2 %all-gather.11.cloned.1.call-done = bf16[2048,768]{1,0:T(8,128)(2,1)} async-done(((bf16[512,768]{1,0:T(8,128)(2,1)}), bf16[2048,768]{1,0:T(8,128)(2,1)}) %all-gather.11.cloned.1.call-update) | async-done | bytes 3145744 | tf_op jit(solution)/shard_map/all_gather | solution.py:271
  170.8 10.9 %shard_map.85 = (bf16[4,512,384]{2,1,0:T(8,128)(2,1)}, bf16[4,512,384]{2,1,0:T(8,128)(2,1)}, bf16[4,512,384]{2,1,0:T(8,128)(2,1)}, bf16[4,512,384]{2,1,0:T(8,128)(2,1)}) custom-call(s32[6]{0:T(128)S(1)} %copy-done.3, bf16[512,256]{1,0:T(8,128)(2,1)S(1)} %shard_map.84.att_own, bf16[512,256]{1,0:T(8,128)(2,1)S(1)} %collective-permute-done.20.att_other, ...), custom_call_target="tpu_custom_call" | custom-call | flops 6442450944 | bytes 14680064 | tf_op jit(solution)/shard_map/pallas_call | solution.py:96
  182.2 3.1 %collective-permute-done.24 = bf16[4,512,384]{2,1,0:T(8,128)(2,1)S(1)} collective-permute-done((bf16[4,512,384]{2,1,0:T(8,128)(2,1)}, bf16[4,512,384]{2,1,0:T(8,128)(2,1)S(1)}, u32[]{:S(2)}, u32[]{:S(2)}) %collective-permute-start.24) | collective-permute-done | bytes 1572896 | tf_op jit(solution)/shard_map/ppermute | solution.py:23
  191.0 3.0 %collective-permute-start.33 = (bf16[256,384]{1,0:T(8,128)(2,1)S(1)}, bf16[256,384]{1,0:T(8,128)(2,1)S(1)}, u32[]{:S(2)}, u32[]{:S(2)}) collective-permute-start(bf16[256,384]{1,0:T(8,128)(2,1)S(1)} %get-tuple-element.46), channel_id=1, source_target_pairs={{0,12},{4,0},{8,4},{12,8},{1,13},{5,1},{9,5},{13,9},{2,14},{6,2},{... | collective-permute-start | bytes 589832 | tf_op jit(solution)/shard_map/ppermute | solution.py:23
  196.5 3.0 %collective-permute-start.28 = (bf16[512,384]{1,0:T(8,128)(2,1)S(1)}, bf16[512,384]{1,0:T(8,128)(2,1)S(1)}, u32[]{:S(2)}, u32[]{:S(2)}) collective-permute-start(bf16[512,384]{1,0:T(8,128)(2,1)S(1)} %pad_maximum_fusion.2), channel_id=1, source_target_pairs={{0,12},{4,0},{8,4},{12,8},{1,13},{5,1},{9,5},{13,9},{2,14},{6,2},{... | collective-permute-start | bytes 1179656 | tf_op jit(solution)/shard_map/ppermute | solution.py:23
  200.7 3.0 %collective-permute-start.34 = (bf16[512,384]{1,0:T(8,128)(2,1)S(1)}, bf16[512,384]{1,0:T(8,128)(2,1)S(1)}, u32[]{:S(2)}, u32[]{:S(2)}) collective-permute-start(bf16[512,384]{1,0:T(8,128)(2,1)S(1)} %pad_maximum_fusion.4), channel_id=1, source_target_pairs={{0,12},{4,0},{8,4},{12,8},{1,13},{5,1},{9,5},{13,9},{2,14},{6,2},{... | collective-permute-start | bytes 1179656 | tf_op jit(solution)/shard_map/ppermute | solution.py:23
  203.7 5.6 %collective-permute-done.26 = bf16[512,384]{1,0:T(8,128)(2,1)S(1)} collective-permute-done((bf16[512,384]{1,0:T(8,128)(2,1)S(1)}, bf16[512,384]{1,0:T(8,128)(2,1)S(1)}, u32[]{:S(2)}, u32[]{:S(2)}) %collective-permute-start.26) | collective-permute-done | bytes 393248 | tf_op jit(solution)/shard_map/ppermute | solution.py:23
  210.5 2.3 collective-permute-start.29
  212.9 3.3 %collective-permute-done.32 = bf16[512,384]{1,0:T(8,128)(2,1)S(1)} collective-permute-done((bf16[512,384]{1,0:T(8,128)(2,1)S(1)}, bf16[512,384]{1,0:T(8,128)(2,1)S(1)}, u32[]{:S(2)}, u32[]{:S(2)}) %collective-permute-start.32) | collective-permute-done | bytes 393248 | tf_op jit(solution)/shard_map/ppermute | solution.py:23
  216.4 3.5 %collective-permute-start.35 = (bf16[512,384]{1,0:T(8,128)(2,1)S(1)}, bf16[512,384]{1,0:T(8,128)(2,1)S(1)}, u32[]{:S(2)}, u32[]{:S(2)}) collective-permute-start(bf16[512,384]{1,0:T(8,128)(2,1)S(1)} %fusion.21), channel_id=1, source_target_pairs={{0,0},{2,16},{16,2},{18,18},{1,1},{3,17},{17,3},{19,19},{4,4},{6,2... | collective-permute-start | bytes 1179656 | tf_op jit(solution)/shard_map/ppermute | solution.py:28
  219.9 8.4 %collective-permute-done.35 = bf16[512,384]{1,0:T(8,128)(2,1)S(1)} collective-permute-done((bf16[512,384]{1,0:T(8,128)(2,1)S(1)}, bf16[512,384]{1,0:T(8,128)(2,1)S(1)}, u32[]{:S(2)}, u32[]{:S(2)}) %collective-permute-start.35) | collective-permute-done | bytes 393248 | tf_op jit(solution)/shard_map/ppermute | solution.py:28
  (138 shorter events, 45.4 us)
Async XLA Ops:
  6.5 62.1 %all-gather.7.cloned.1.call-start = ((), (), s32[]{:S(2)}) async-start(), calls=%async_computation | async-start | bytes 5898240 | tf_op jit(solution)/shard_map/all_gather | solution.py:269
  7.3 115.4 %all-gather.9.cloned.1.call-start = ((), (), s32[]{:S(2)}) async-start(), calls=%async_computation.1 | async-start | bytes 5898240 | tf_op jit(solution)/shard_map/all_gather | solution.py:270
  8.0 161.8 %all-gather.11.cloned.1.call-start = ((), (), s32[]{:S(2)}) async-start(), calls=%async_computation.2 | async-start | bytes 3932160 | tf_op jit(solution)/shard_map/all_gather | solution.py:271
  8.1 12.7 %collective-permute-start = (bf16[512,384]{1,0:T(8,128)(2,1)}, bf16[512,384]{1,0:T(8,128)(2,1)S(1)}, u32[]{:S(2)}, u32[]{:S(2)}) collective-permute-start(bf16[512,384]{1,0:T(8,128)(2,1)} %param.8), channel_id=1, source_target_pairs={{16,0},{0,2},{18,16},{2,18},{17,1},{1,3},{19,17},{3,19},{20,4},{4,... | collective-permute-start | bytes 1179656 | tf_op jit(solution)/shard_map/ppermute | solution.py:28
  8.1 21.0 %collective-permute-start.1 = (bf16[512,384]{1,0:T(8,128)(2,1)}, bf16[512,384]{1,0:T(8,128)(2,1)S(1)}, u32[]{:S(2)}, u32[]{:S(2)}) collective-permute-start(bf16[512,384]{1,0:T(8,128)(2,1)} %param.8), channel_id=1, source_target_pairs={{0,0},{16,2},{2,16},{18,18},{1,1},{17,3},{3,17},{19,19},{4,4},{20,... | collective-permute-start | bytes 1179656 | tf_op jit(solution)/shard_map/ppermute | solution.py:28
  13.6 15.7 %collective-permute-start.2 = (bf16[256,768]{1,0:T(8,128)(2,1)}, bf16[256,768]{1,0:T(8,128)(2,1)S(1)}, u32[]{:S(2)}, u32[]{:S(2)}) collective-permute-start(bf16[256,768]{1,0:T(8,128)(2,1)} %refs_0_.1), channel_id=1, source_target_pairs={{0,96},{32,0},{64,32},{96,64},{1,97},{33,1},{65,33},{97,65},{2,98}... | collective-permute-start | bytes 1179656 | tf_op jit(solution)/shard_map/ppermute | solution.py:23
  16.7 16.0 %collective-permute-start.3 = (bf16[256,768]{1,0:T(8,128)(2,1)}, bf16[256,768]{1,0:T(8,128)(2,1)S(1)}, u32[]{:S(2)}, u32[]{:S(2)}) collective-permute-start(bf16[256,768]{1,0:T(8,128)(2,1)} %refs_0_.1), channel_id=1, source_target_pairs={{0,32},{32,64},{64,96},{96,0},{1,33},{33,65},{65,97},{97,1},{2,34}... | collective-permute-start | bytes 1179656 | tf_op jit(solution)/shard_map/ppermute | solution.py:23
  32.7 17.5 %collective-permute-start.5 = (bf16[2,512,384]{2,1,0:T(8,128)(2,1)S(1)}, bf16[2,512,384]{2,1,0:T(8,128)(2,1)S(1)}, u32[]{:S(2)}, u32[]{:S(2)}) collective-permute-start(bf16[2,512,384]{2,1,0:T(8,128)(2,1)S(1)} %pad_maximum_fusion.refs_0_), channel_id=1, source_target_pairs={{0,4},{4,8},{8,12},{12,0},{1,5},{5,9},{9,13},{13,1},{2,6},{6,10},{... | collective-permute-start | bytes 2359304 | tf_op jit(solution)/shard_map/ppermute | solution.py:23
  34.2 17.6 %collective-permute-start.4 = (bf16[2,512,384]{2,1,0:T(8,128)(2,1)S(1)}, bf16[2,512,384]{2,1,0:T(8,128)(2,1)}, u32[]{:S(2)}, u32[]{:S(2)}) collective-permute-start(bf16[2,512,384]{2,1,0:T(8,128)(2,1)S(1)} %pad_maximum_fusion.refs_0_), channel_id=1, source_target_pairs={{0,12},{4,0},{8,4},{12,8},{1,13},{5,1},{9,5},{13,9},{2,14},{6,2},{... | collective-permute-start | bytes 2359304 | tf_op jit(solution)/shard_map/ppermute | solution.py:23
  35.9 32.7 %collective-permute-start.8 = (bf16[2,512,384]{2,1,0:T(8,128)(2,1)S(1)}, bf16[2,512,384]{2,1,0:T(8,128)(2,1)}, u32[]{:S(2)}, u32[]{:S(2)}) collective-permute-start(bf16[2,512,384]{2,1,0:T(8,128)(2,1)S(1)} %pad_maximum_fusion.refs_0_), channel_id=1, source_target_pairs={{0,1},{1,0},{2,3},{3,2},{4,5},{5,4},{6,7},{7,6},{8,9},{9,8},{10,11... | collective-permute-start | bytes 2359304 | tf_op jit(solution)/shard_map/ppermute | solution.py:23
  56.3 12.3 %collective-permute-start.10 = (bf16[2,512,384]{2,1,0:T(8,128)(2,1)S(1)}, bf16[2,512,384]{2,1,0:T(8,128)(2,1)}, u32[]{:S(2)}, u32[]{:S(2)}) collective-permute-start(bf16[2,512,384]{2,1,0:T(8,128)(2,1)S(1)} %collective-permute-done.5.refs_2_), channel_id=1, source_target_pairs={{0,1},{1,0},{2,3},{3,2},{4,5},{5,4},{6,7},{7,6},{8,9},{9,8},{10,11... | collective-permute-start | bytes 2359304 | tf_op jit(solution)/shard_map/ppermute | solution.py:23
  56.4 12.3 %collective-permute-start.9 = (bf16[2,512,384]{2,1,0:T(8,128)(2,1)}, bf16[2,512,384]{2,1,0:T(8,128)(2,1)}, u32[]{:S(2)}, u32[]{:S(2)}) collective-permute-start(bf16[2,512,384]{2,1,0:T(8,128)(2,1)} %collective-permute-done.4.refs_1_), channel_id=1, source_target_pairs={{0,1},{1,0},{2,3},{3,2},{4,5},{5,4},{6,7},{7,6},{8,9},{9,8},{10,11... | collective-permute-start | bytes 2359304 | tf_op jit(solution)/shard_map/ppermute | solution.py:23
  86.2 53.5 %collective-permute-start.19 = (bf16[2,512,768]{2,1,0:T(8,128)(2,1)}, bf16[2,512,768]{2,1,0:T(8,128)(2,1)}, u32[]{:S(2)}, u32[]{:S(2)}) collective-permute-start(bf16[2,512,768]{2,1,0:T(8,128)(2,1)} %get-tuple-element.28), channel_id=1, source_target_pairs={{0,16},{16,0},{1,17},{17,1},{2,18},{18,2},{3,19},{19,3},{4,20},{20... | collective-permute-start | bytes 4718600 | tf_op jit(solution)/shard_map/ppermute | solution.py:23
  86.7 35.9 %collective-permute-start.16 = (bf16[128,768]{1,0:T(8,128)(2,1)S(1)}, bf16[128,768]{1,0:T(8,128)(2,1)S(1)}, u32[]{:S(2)}, u32[]{:S(2)}) collective-permute-start(bf16[128,768]{1,0:T(8,128)(2,1)S(1)} %slice.168), channel_id=1, source_target_pairs={{0,32},{32,64},{64,96},{96,0},{1,33},{33,65},{65,97},{97,1},{2,34}... | collective-permute-start | bytes 589832 | tf_op jit(solution)/shard_map/ppermute | solution.py:23
  89.3 33.3 %collective-permute-start.17 = (bf16[128,768]{1,0:T(8,128)(2,1)S(1)}, bf16[128,768]{1,0:T(8,128)(2,1)S(1)}, u32[]{:S(2)}, u32[]{:S(2)}) collective-permute-start(bf16[128,768]{1,0:T(8,128)(2,1)S(1)} %slice.169), channel_id=1, source_target_pairs={{0,96},{32,0},{64,32},{96,64},{1,97},{33,1},{65,33},{97,65},{2,98}... | collective-permute-start | bytes 589832 | tf_op jit(solution)/shard_map/ppermute | solution.py:23
  122.7 47.1 %collective-permute-start.21 = (bf16[256,768]{1,0:T(8,128)(2,1)S(1)}, bf16[256,768]{1,0:T(8,128)(2,1)S(1)}, u32[]{:S(2)}, u32[]{:S(2)}) collective-permute-start(bf16[256,768]{1,0:T(8,128)(2,1)S(1)} %slice.171.refs_5_), channel_id=1, source_target_pairs={{0,96},{32,0},{64,32},{96,64},{1,97},{33,1},{65,33},{97,65},{2,98}... | collective-permute-start | bytes 1179656 | tf_op jit(solution)/shard_map/ppermute | solution.py:23
  123.9 45.9 %collective-permute-start.22 = (bf16[256,768]{1,0:T(8,128)(2,1)S(1)}, bf16[256,768]{1,0:T(8,128)(2,1)S(1)}, u32[]{:S(2)}, u32[]{:S(2)}) collective-permute-start(bf16[256,768]{1,0:T(8,128)(2,1)S(1)} %slice.171.refs_5_), channel_id=1, source_target_pairs={{0,32},{32,64},{64,96},{96,0},{1,33},{33,65},{65,97},{97,1},{2,34}... | collective-permute-start | bytes 1179656 | tf_op jit(solution)/shard_map/ppermute | solution.py:23
  124.8 45.0 %collective-permute-start.23 = (bf16[256,768]{1,0:T(8,128)(2,1)S(1)}, bf16[256,768]{1,0:T(8,128)(2,1)S(1)}, u32[]{:S(2)}, u32[]{:S(2)}) collective-permute-start(bf16[256,768]{1,0:T(8,128)(2,1)S(1)} %slice.171.refs_5_), channel_id=1, source_target_pairs={{0,64},{32,96},{64,0},{96,32},{1,65},{33,97},{65,1},{97,33},{2,66}... | collective-permute-start | bytes 1179656 | tf_op jit(solution)/shard_map/ppermute | solution.py:23
  138.9 18.9 %collective-permute-start.18 = (bf16[512,768]{1,0:T(8,128)(2,1)}, bf16[512,768]{1,0:T(8,128)(2,1)S(1)}, u32[]{:S(2)}, u32[]{:S(2)}) collective-permute-start(bf16[512,768]{1,0:T(8,128)(2,1)} %get-tuple-element.27), channel_id=1, source_target_pairs={{0,16},{16,0},{1,17},{17,1},{2,18},{18,2},{3,19},{19,3},{4,20},{20... | collective-permute-start | bytes 2359304 | tf_op jit(solution)/shard_map/ppermute | solution.py:23
  196.0 13.3 %collective-permute-start.26 = (bf16[512,384]{1,0:T(8,128)(2,1)S(1)}, bf16[512,384]{1,0:T(8,128)(2,1)S(1)}, u32[]{:S(2)}, u32[]{:S(2)}) collective-permute-start(bf16[512,384]{1,0:T(8,128)(2,1)S(1)} %pad_maximum_fusion.1), channel_id=1, source_target_pairs={{0,4},{4,8},{8,12},{12,0},{1,5},{5,9},{9,13},{13,1},{2,6},{6,10},{... | collective-permute-start | bytes 1179656 | tf_op jit(solution)/shard_map/ppermute | solution.py:23
  196.5 12.9 %collective-permute-start.28 = (bf16[512,384]{1,0:T(8,128)(2,1)S(1)}, bf16[512,384]{1,0:T(8,128)(2,1)S(1)}, u32[]{:S(2)}, u32[]{:S(2)}) collective-permute-start(bf16[512,384]{1,0:T(8,128)(2,1)S(1)} %pad_maximum_fusion.2), channel_id=1, source_target_pairs={{0,12},{4,0},{8,4},{12,8},{1,13},{5,1},{9,5},{13,9},{2,14},{6,2},{... | collective-permute-start | bytes 1179656 | tf_op jit(solution)/shard_map/ppermute | solution.py:23
  200.2 15.9 %collective-permute-start.32 = (bf16[512,384]{1,0:T(8,128)(2,1)S(1)}, bf16[512,384]{1,0:T(8,128)(2,1)S(1)}, u32[]{:S(2)}, u32[]{:S(2)}) collective-permute-start(bf16[512,384]{1,0:T(8,128)(2,1)S(1)} %pad_maximum_fusion.3), channel_id=1, source_target_pairs={{0,4},{4,8},{8,12},{12,0},{1,5},{5,9},{9,13},{13,1},{2,6},{6,10},{... | collective-permute-start | bytes 1179656 | tf_op jit(solution)/shard_map/ppermute | solution.py:23
  200.7 15.5 %collective-permute-start.34 = (bf16[512,384]{1,0:T(8,128)(2,1)S(1)}, bf16[512,384]{1,0:T(8,128)(2,1)S(1)}, u32[]{:S(2)}, u32[]{:S(2)}) collective-permute-start(bf16[512,384]{1,0:T(8,128)(2,1)S(1)} %pad_maximum_fusion.4), channel_id=1, source_target_pairs={{0,12},{4,0},{8,4},{12,8},{1,13},{5,1},{9,5},{13,9},{2,14},{6,2},{... | collective-permute-start | bytes 1179656 | tf_op jit(solution)/shard_map/ppermute | solution.py:23
  216.4 11.9 %collective-permute-start.35 = (bf16[512,384]{1,0:T(8,128)(2,1)S(1)}, bf16[512,384]{1,0:T(8,128)(2,1)S(1)}, u32[]{:S(2)}, u32[]{:S(2)}) collective-permute-start(bf16[512,384]{1,0:T(8,128)(2,1)S(1)} %fusion.21), channel_id=1, source_target_pairs={{0,0},{2,16},{16,2},{18,18},{1,1},{3,17},{17,3},{19,19},{4,4},{6,2... | collective-permute-start | bytes 1179656 | tf_op jit(solution)/shard_map/ppermute | solution.py:28
  (30 other events, 372.6 us)
Sparse Core Ops, SparseCore 0:
  9.0 57.3 all-gather.6
  68.1 54.5 all-gather.8
  124.3 45.4 all-gather.10
